TPU v7x, 32 devices: a whole 2x2x4 slice. The times are simulated.
32 devices in a mesh: gx: 4 (over y, core), gy: 4 (over z), gz: 2 (over x).
Axes of the slice: x: 2, y: 2, z: 4, core: 2. Of those that a mesh axis runs over, the one named last changes fastest.
Arguments:
- thermal_anomaly: float32 [64, 64, 256], P('gx', 'gy', 'gz'), may hold values from -6 to 6
- specific_vapour: float32 [64, 64, 256], P('gx', 'gy', 'gz'), may hold values from -6 to 6
- server_thermal_load: float32 [64, 64, 256], P('gx', 'gy', 'gz'), may hold values from -5 to 5
- lateral_mixing_coefficient: float32 [64, 64, 256], P('gx', 'gy', 'gz'), may hold values from 40 to 800
- upward_mixing_coefficient: float32 [64, 64, 256], P('gx', 'gy', 'gz'), may hold values from 0.1 to 0.25
- cfl_along_lateral_axis: float32 [64, 64, 256], P('gx', 'gy', 'gz'), may hold values from -30 to 30
- cfl_across_lateral_axis: float32 [64, 64, 256], P('gx', 'gy', 'gz'), may hold values from -30 to 30
- cfl_upward_axis: float32 [64, 64, 256], P('gx', 'gy', 'gz'), may hold values from -0.15 to 0.15
Outputs:
- temperature_new: float32 [64, 64, 256], P('gx', 'gy', 'gz')
- humidity_new: float32 [64, 64, 256], P('gx', 'gy', 'gz')
All inputs are finite; a program needn't handle non-finite values.
Results may differ from a plain program's by a relative error of at most 0.0003.
Values sent between devices are 32-bit elements; how exact they have to be, the bound alone decides.
No kernel may reach another device: no remote copies, remote signals or barrier semaphores. Data moves between devices by JAX's collectives and lax.ppermute only.
A program may use at most 64 MiB of HBM per device.

v0:
```python
import jax
import jax.numpy as jnp
from jax import lax
from jax.sharding import PartitionSpec as P

vapour_scaling = 0.8


def with_halo(block, sides, width):
    for axis, dim in sides:
        count = lax.axis_size(axis)
        forward = [(i, i + 1) for i in range(count - 1)]
        backward = [(target, source) for source, target in forward]
        low = lax.ppermute(
            lax.slice_in_dim(block, block.shape[dim] - width, None, axis=dim), axis, forward
        )
        high = lax.ppermute(lax.slice_in_dim(block, 0, width, axis=dim), axis, backward)
        block = jnp.concatenate([low, block, high], axis=dim)
    return block


def bands(east_coef, west_coef):
    return (-west_coef, 1.0 + east_coef + west_coef, -east_coef)


def eliminate(lower_band, diagonal_band, upper_band, right_side, upper_in, right_in):

    def forward(carried, cell_data):
        upper_before, right_before = carried
        lower_cell, diagonal_cell, upper_cell, right_cell = cell_data
        pivots = diagonal_cell - lower_cell * upper_before
        upper_now = upper_cell / pivots
        right_now = (right_cell - lower_cell * right_before) / pivots
        return ((upper_now, right_now), (upper_now, right_now))

    unused, ratios = lax.scan(
        forward, (upper_in, right_in), (lower_band, diagonal_band, upper_band, right_side)
    )
    return ratios


def substitute(upper_ratios, right_ratios, value_in):

    def backward(value_after, cell_data):
        upper_ratio, right_ratio = cell_data
        value = right_ratio - upper_ratio * value_after
        return (value, value)

    unused, values = lax.scan(backward, value_in, (upper_ratios, right_ratios), reverse=True)
    return values


def whole_solve(east_coef, west_coef, right_side):
    lower_band, diagonal_band, upper_band = bands(east_coef, west_coef)
    zeros = jnp.zeros_like(right_side[0])
    upper_ratios, right_ratios = eliminate(
        lower_band, diagonal_band, upper_band, right_side, zeros, zeros
    )
    return substitute(upper_ratios, right_ratios, zeros)


def body(
    thermal_anomaly,
    specific_vapour,
    server_thermal_load,
    lateral_mixing_coefficient,
    upward_mixing_coefficient,
    cfl_along_lateral_axis,
    cfl_across_lateral_axis,
    cfl_upward_axis,
):
    tracer_bundle = jnp.stack([thermal_anomaly, specific_vapour])
    factors = jnp.array([1.0, vapour_scaling], jnp.float32).reshape(2, 1, 1, 1)
    weights = jnp.array([1.0, 0.0], jnp.float32).reshape(2, 1, 1, 1)
    source = weights * server_thermal_load[None]
    east_x = factors * lateral_mixing_coefficient[None] - 0.5 * cfl_along_lateral_axis[None]
    west_x = factors * lateral_mixing_coefficient[None] + 0.5 * cfl_along_lateral_axis[None]
    east_y = factors * lateral_mixing_coefficient[None] - 0.5 * cfl_across_lateral_axis[None]
    west_y = factors * lateral_mixing_coefficient[None] + 0.5 * cfl_across_lateral_axis[None]
    east_z = factors * upward_mixing_coefficient[None] - 0.5 * cfl_upward_axis[None]
    west_z = factors * upward_mixing_coefficient[None] + 0.5 * cfl_upward_axis[None]
    padded = with_halo(tracer_bundle, (("gy", 2), ("gz", 3)), 1)
    first_side = (
        tracer_bundle
        + (
            east_y * (padded[:, :, 2:, 1:-1] - tracer_bundle)
            + west_y * (padded[:, :, :-2, 1:-1] - tracer_bundle)
        )
        + (
            east_z * (padded[:, :, 1:-1, 2:] - tracer_bundle)
            + west_z * (padded[:, :, 1:-1, :-2] - tracer_bundle)
        )
        + source
    )
    packed = jnp.stack(
        [lateral_mixing_coefficient, cfl_along_lateral_axis, first_side[0], first_side[1]]
    )
    lines = lax.all_to_all(packed, "gx", split_axis=2, concat_axis=1, tiled=True)
    line_east = factors * lines[0][None] - 0.5 * lines[1][None]
    line_west = factors * lines[0][None] + 0.5 * lines[1][None]
    solved = whole_solve(
        jnp.moveaxis(line_east, 1, 0), jnp.moveaxis(line_west, 1, 0), jnp.moveaxis(lines[2:4], 1, 0)
    )
    half_field = lax.all_to_all(
        jnp.moveaxis(solved, 0, 1), "gx", split_axis=1, concat_axis=2, tiled=True
    )
    padded_half = with_halo(half_field, (("gx", 1), ("gz", 3)), 1)
    second_side = (
        half_field
        + (
            east_x * (padded_half[:, 2:, :, 1:-1] - half_field)
            + west_x * (padded_half[:, :-2, :, 1:-1] - half_field)
        )
        + (
            east_z * (padded_half[:, 1:-1, :, 2:] - half_field)
            + west_z * (padded_half[:, 1:-1, :, :-2] - half_field)
        )
        + source
    )
    packed_y = jnp.stack(
        [lateral_mixing_coefficient, cfl_across_lateral_axis, second_side[0], second_side[1]]
    )
    lines_y = lax.all_to_all(packed_y, "gy", split_axis=1, concat_axis=2, tiled=True)
    line_east_y = factors * lines_y[0][None] - 0.5 * lines_y[1][None]
    line_west_y = factors * lines_y[0][None] + 0.5 * lines_y[1][None]
    solved_y = whole_solve(
        jnp.moveaxis(line_east_y, 2, 0),
        jnp.moveaxis(line_west_y, 2, 0),
        jnp.moveaxis(lines_y[2:4], 2, 0),
    )
    new_fields = lax.all_to_all(
        jnp.moveaxis(solved_y, 0, 2), "gy", split_axis=2, concat_axis=1, tiled=True
    )
    return (new_fields[0], new_fields[1])


def solution(mesh):
    in_specs = (
        P("gx", "gy", "gz"),
        P("gx", "gy", "gz"),
        P("gx", "gy", "gz"),
        P("gx", "gy", "gz"),
        P("gx", "gy", "gz"),
        P("gx", "gy", "gz"),
        P("gx", "gy", "gz"),
        P("gx", "gy", "gz"),
    )
    out_specs = (P("gx", "gy", "gz"), P("gx", "gy", "gz"))
    return jax.shard_map(body, mesh=mesh, in_specs=in_specs, out_specs=out_specs, check_vma=False)
```

profile of v0, /device:TPU:0, one launch (start us, length us, event | category | flops | bytes accessed | tf_op | source)
XLA Modules:
  0.0 111.7 jit_solution(8886938260638983529)
XLA Ops:
  0.6 1.1 copy_bitcast_fusion.1
  1.7 0.0 copy-start.2
  1.7 1.4 %collective-permute-start = (f32[2,16,1,128]{3,1,0,2:T(8,128)S(1)}, f32[2,16,1,128]{3,1,0,2:T(8,128)S(1)}, u32[]{:S(2)}, u32[]{:S(2)}) collective-permute-start(f32[2,16,1,128]{3,1,0,2:T(8,128)S(1)} %get-tuple-element.515), channel_id=1, source_target_pairs={{2,0},{4,2},{6,4},{3,1},{5,3},{7,5},{10,8},{12,10},{14,12},{11,9},... | collective-permute-start | bytes 49160 | tf_op jit(solution)/shard_map/ppermute | solution.py:17
  3.1 5.6 %collective-permute-start.1 = (f32[2,16,1,128]{3,1,0,2:T(8,128)S(1)}, f32[2,16,1,128]{3,1,0,2:T(8,128)S(1)}, u32[]{:S(2)}, u32[]{:S(2)}) collective-permute-start(f32[2,16,1,128]{3,1,0,2:T(8,128)S(1)} %get-tuple-element.514), channel_id=1, source_target_pairs={{0,2},{2,4},{4,6},{1,3},{3,5},{5,7},{8,10},{10,12},{12,14},{9,11},... | collective-permute-start | bytes 49160 | tf_op jit(solution)/shard_map/ppermute | solution.py:14
  8.8 1.4 %collective-permute-done.1 = f32[2,16,1,128]{3,1,0,2:T(8,128)S(1)} collective-permute-done((f32[2,16,1,128]{3,1,0,2:T(8,128)S(1)}, f32[2,16,1,128]{3,1,0,2:T(8,128)S(1)}, u32[]{:S(2)}, u32[]{:S(2)}) %collective-permute-start.1) | collective-permute-done | bytes 16416 | tf_op jit(solution)/shard_map/ppermute | solution.py:14
  10.2 0.0 copy-start.1
  10.2 0.1 fusion.51
  10.3 1.3 %collective-permute-start.2 = (f32[2,16,18,1]{3,1,0,2:T(8,128)S(1)}, f32[2,16,18,1]{3,1,0,2:T(8,128)S(1)}, u32[]{:S(2)}, u32[]{:S(2)}) collective-permute-start(f32[2,16,18,1]{3,1,0,2:T(8,128)S(1)} %get-tuple-element.502), channel_id=1, source_target_pairs={{1,0},{3,2},{5,4},{7,6},{9,8},{11,10},{13,12},{15,14},{17,16},{19,... | collective-permute-start | bytes 6920 | tf_op jit(solution)/shard_map/ppermute | solution.py:17
  11.6 0.0 copy-start.3
  11.7 4.7 %collective-permute-start.3 = (f32[2,16,18,1]{3,1,0,2:T(8,128)S(1)}, f32[2,16,18,1]{3,1,0,2:T(8,128)S(1)}, u32[]{:S(2)}, u32[]{:S(2)}) collective-permute-start(f32[2,16,18,1]{3,1,0,2:T(8,128)S(1)} %get-tuple-element.503), channel_id=1, source_target_pairs={{0,1},{2,3},{4,5},{6,7},{8,9},{10,11},{12,13},{14,15},{16,17},{18,... | collective-permute-start | bytes 6920 | tf_op jit(solution)/shard_map/ppermute | solution.py:14
  16.5 0.0 copy-start.4
  16.5 0.8 copy-done.4
  17.4 0.9 copy-done.5
  18.3 0.0 copy-start
  18.4 0.8 copy-done
  19.3 0.8 collective-permute-done.2
  20.1 1.3 %collective-permute-done.3 = f32[2,16,18,1]{3,1,0,2:T(8,128)S(1)} collective-permute-done((f32[2,16,18,1]{3,1,0,2:T(8,128)S(1)}, f32[2,16,18,1]{3,1,0,2:T(8,128)S(1)}, u32[]{:S(2)}, u32[]{:S(2)}) %collective-permute-start.3) | collective-permute-done | bytes 2336 | tf_op jit(solution)/shard_map/ppermute | solution.py:14
  21.5 0.3 multiply_add_fusion.3
  21.8 0.8 fusion.9
  22.6 3.5 %all-to-all-start = ((f32[4,16,16,128]{3,1,0,2:T(8,128)}), f32[4,16,16,128]{3,1,0,2:T(8,128)S(1)}, u32[]{:S(2)}, u32[]{:S(2)}) async-start(f32[4,16,16,128]{3,1,0,2:T(8,128)} %fusion.9), calls=%async_computation | async-start | bytes 1048576 | tf_op jit(solution)/shard_map/all_to_all | solution.py:98
  26.1 8.8 %all-to-all-done = f32[4,16,16,128]{3,1,0,2:T(8,128)S(1)} async-done(((f32[4,16,16,128]{3,1,0,2:T(8,128)}), f32[4,16,16,128]{3,1,0,2:T(8,128)S(1)}, u32[]{:S(2)}, u32[]{:S(2)}) %all-to-all-start) | async-done | bytes 524320 | tf_op jit(solution)/shard_map/all_to_all | solution.py:98
  35.0 0.1 copy.88
  35.1 0.1 copy.90
  35.2 0.2 fusion.16
  35.5 4.4 %while.68 = (s32[]{:T(128)}, f32[2,4,128]{2,1,0:T(4,128)S(1)}, f32[2,4,128]{2,1,0:T(4,128)S(1)}, f32[64,2,4,128]{3,2,1,0:T(4,128)S(1)}, f32[64,2,4,128]{3,2,1,0:...) while((s32[]{:T(128)}, f32[2,4,128]{2,1,0:T(4,128)S(1)}, ...), condition=%wide.region_1.2_spmd.clone, body=%wide.region_0.1_spmd.clone.sunk | while | flops 8195 | bytes 49279 | solution.py:36
  40.0 2.4 %while.69 = (s32[]{:T(128)}, f32[2,4,128]{2,1,0:T(4,128)S(1)}, f32[64,2,4,128]{3,2,1,0:T(4,128)S(1)}, f32[64,2,4,128]{3,2,1,0:T(4,128)S(1)}, f32[64,2,4,128]{3,2...) while((s32[]{:T(128)}, f32[2,4,128]{2,1,0:T(4,128)S(1)}, f32[64,2,4,128]{3,2,1,0:T(4,128)S(1)}, ...), condition=%wide.region_3.4_spmd.clone, body=%wide.region_2.3_spmd.clone.sunk | while | flops 3076 | bytes 20591 | solution.py:49
  42.3 8.4 %all_to_all.63 = f32[2,64,4,128]{3,2,0,1:T(4,128)S(1)} all-to-all(f32[2,64,4,128]{3,2,0,1:T(4,128)S(1)} %bitcast.152), channel_id=1, replica_groups=mesh['gx'=4,'gy'=4,'gz'=2] {'gx'}, dimensions={1} | all-to-all | bytes 524288 | tf_op jit(solution)/shard_map/all_to_all | solution.py:104
  50.8 1.3 %collective-permute-start.4 = (f32[2,1,16,128]{3,1,0,2:T(1,128)S(1)}, f32[2,1,16,128]{3,1,0,2:T(1,128)S(1)}, u32[]{:S(2)}, u32[]{:S(2)}) collective-permute-start(f32[2,1,16,128]{3,1,0,2:T(1,128)S(1)} %get-tuple-element.513), channel_id=1, source_target_pairs={{8,0},{16,8},{24,16},{9,1},{17,9},{25,17},{10,2},{18,10},{26,18},{... | collective-permute-start | bytes 49160 | tf_op jit(solution)/shard_map/ppermute | solution.py:17
  52.1 3.0 %collective-permute-start.5 = (f32[2,1,16,128]{3,1,0,2:T(1,128)S(1)}, f32[2,1,16,128]{3,1,0,2:T(1,128)S(1)}, u32[]{:S(2)}, u32[]{:S(2)}) collective-permute-start(f32[2,1,16,128]{3,1,0,2:T(1,128)S(1)} %get-tuple-element.512), channel_id=1, source_target_pairs={{0,8},{8,16},{16,24},{1,9},{9,17},{17,25},{2,10},{10,18},{18,26},{... | collective-permute-start | bytes 49160 | tf_op jit(solution)/shard_map/ppermute | solution.py:14
  55.2 0.8 collective-permute-done.5
  56.0 0.1 pad_maximum_fusion.2
  56.0 0.2 fusion.50
  56.2 1.3 %collective-permute-start.6 = (f32[2,18,16,1]{3,1,0,2:T(8,128)S(1)}, f32[2,18,16,1]{3,1,0,2:T(8,128)S(1)}, u32[]{:S(2)}, u32[]{:S(2)}) collective-permute-start(f32[2,18,16,1]{3,1,0,2:T(8,128)S(1)} %get-tuple-element.500), channel_id=1, source_target_pairs={{1,0},{3,2},{5,4},{7,6},{9,8},{11,10},{13,12},{15,14},{17,16},{19,... | collective-permute-start | bytes 6920 | tf_op jit(solution)/shard_map/ppermute | solution.py:17
  57.5 4.6 %collective-permute-start.7 = (f32[2,18,16,1]{3,1,0,2:T(8,128)S(1)}, f32[2,18,16,1]{3,1,0,2:T(8,128)S(1)}, u32[]{:S(2)}, u32[]{:S(2)}) collective-permute-start(f32[2,18,16,1]{3,1,0,2:T(8,128)S(1)} %get-tuple-element.501), channel_id=1, source_target_pairs={{0,1},{2,3},{4,5},{6,7},{8,9},{10,11},{12,13},{14,15},{16,17},{18,... | collective-permute-start | bytes 6920 | tf_op jit(solution)/shard_map/ppermute | solution.py:14
  62.2 7.7 %collective-permute-done.6 = f32[2,18,16,1]{3,1,0,2:T(8,128)S(1)} collective-permute-done((f32[2,18,16,1]{3,1,0,2:T(8,128)S(1)}, f32[2,18,16,1]{3,1,0,2:T(8,128)S(1)}, u32[]{:S(2)}, u32[]{:S(2)}) %collective-permute-start.6) | collective-permute-done | bytes 2336 | tf_op jit(solution)/shard_map/ppermute | solution.py:17
  70.0 1.2 %collective-permute-done.7 = f32[2,18,16,1]{3,1,0,2:T(8,128)S(1)} collective-permute-done((f32[2,18,16,1]{3,1,0,2:T(8,128)S(1)}, f32[2,18,16,1]{3,1,0,2:T(8,128)S(1)}, u32[]{:S(2)}, u32[]{:S(2)}) %collective-permute-start.7) | collective-permute-done | bytes 2336 | tf_op jit(solution)/shard_map/ppermute | solution.py:14
  71.2 0.5 multiply_add_fusion.2
  71.7 1.1 copy.95
  72.8 5.4 %all-to-all-start.2 = ((f32[4,16,16,128]{3,2,0,1:T(8,128)}), f32[4,16,16,128]{3,2,0,1:T(8,128)S(1)}, u32[]{:S(2)}, u32[]{:S(2)}) async-start(f32[4,16,16,128]{3,2,0,1:T(8,128)} %copy.95), calls=%async_computation.2 | async-start | bytes 1048576 | tf_op jit(solution)/shard_map/all_to_all | solution.py:123
  78.2 14.4 %all-to-all-done.2 = f32[4,16,16,128]{3,2,0,1:T(8,128)S(1)} async-done(((f32[4,16,16,128]{3,2,0,1:T(8,128)}), f32[4,16,16,128]{3,2,0,1:T(8,128)S(1)}, u32[]{:S(2)}, u32[]{:S(2)}) %all-to-all-start.2) | async-done | bytes 524320 | tf_op jit(solution)/shard_map/all_to_all | solution.py:123
  92.7 0.1 copy.100
  92.8 0.1 copy.98
  93.0 0.2 fusion.20
  93.3 4.4 %while.70 = (s32[]{:T(128)}, f32[2,4,128]{2,1,0:T(4,128)S(1)}, f32[2,4,128]{2,1,0:T(4,128)S(1)}, f32[64,2,4,128]{3,2,1,0:T(4,128)S(1)}, f32[64,2,4,128]{3,2,1,0:...) while((s32[]{:T(128)}, f32[2,4,128]{2,1,0:T(4,128)S(1)}, ...), condition=%wide.region_5.6_spmd.clone, body=%wide.region_4.5_spmd.clone.sunk | while | flops 8195 | bytes 49279 | solution.py:36
  97.7 2.4 %while.71 = (s32[]{:T(128)}, f32[2,4,128]{2,1,0:T(4,128)S(1)}, f32[64,2,4,128]{3,2,1,0:T(4,128)S(1)}, f32[64,2,4,128]{3,2,1,0:T(4,128)S(1)}, f32[64,2,4,128]{3,2...) while((s32[]{:T(128)}, f32[2,4,128]{2,1,0:T(4,128)S(1)}, f32[64,2,4,128]{3,2,1,0:T(4,128)S(1)}, ...), condition=%wide.region_7.8_spmd.clone, body=%wide.region_6.7_spmd.clone.sunk | while | flops 3076 | bytes 20591 | solution.py:49
  100.1 10.8 %all_to_all.64 = f32[2,4,64,128]{3,1,0,2:T(4,128)S(1)} all-to-all(f32[2,4,64,128]{3,1,0,2:T(4,128)S(1)} %bitcast.151), channel_id=1, replica_groups=mesh['gx'=4,'gy'=4,'gz'=2] {'gy'}, dimensions={2} | all-to-all | bytes 524288 | tf_op jit(solution)/shard_map/all_to_all | solution.py:131
  110.9 0.1 copy.113
  110.9 0.7 fusion.52
  (434 shorter events, 8.1 us)
Async XLA Ops:
  1.7 7.1 %copy-start.2 = (f32[16,16,128]{2,1,0:T(8,128)S(1)}, f32[16,16,128]{2,1,0:T(8,128)}, u32[]{:S(2)}) copy-start(f32[16,16,128]{2,1,0:T(8,128)} %param.25) | copy-start | bytes 393220
  1.7 7.1 %collective-permute-start = (f32[2,16,1,128]{3,1,0,2:T(8,128)S(1)}, f32[2,16,1,128]{3,1,0,2:T(8,128)S(1)}, u32[]{:S(2)}, u32[]{:S(2)}) collective-permute-start(f32[2,16,1,128]{3,1,0,2:T(8,128)S(1)} %get-tuple-element.515), channel_id=1, source_target_pairs={{2,0},{4,2},{6,4},{3,1},{5,3},{7,5},{10,8},{12,10},{14,12},{11,9},... | collective-permute-start | bytes 49160 | tf_op jit(solution)/shard_map/ppermute | solution.py:17
  3.1 7.0 %collective-permute-start.1 = (f32[2,16,1,128]{3,1,0,2:T(8,128)S(1)}, f32[2,16,1,128]{3,1,0,2:T(8,128)S(1)}, u32[]{:S(2)}, u32[]{:S(2)}) collective-permute-start(f32[2,16,1,128]{3,1,0,2:T(8,128)S(1)} %get-tuple-element.514), channel_id=1, source_target_pairs={{0,2},{2,4},{4,6},{1,3},{3,5},{5,7},{8,10},{10,12},{12,14},{9,11},... | collective-permute-start | bytes 49160 | tf_op jit(solution)/shard_map/ppermute | solution.py:14
  10.2 6.2 %copy-start.1 = (f32[16,16,128]{2,1,0:T(8,128)S(1)}, f32[16,16,128]{2,1,0:T(8,128)}, u32[]{:S(2)}) copy-start(f32[16,16,128]{2,1,0:T(8,128)} %param.24) | copy-start | bytes 393220
  10.3 9.8 %collective-permute-start.2 = (f32[2,16,18,1]{3,1,0,2:T(8,128)S(1)}, f32[2,16,18,1]{3,1,0,2:T(8,128)S(1)}, u32[]{:S(2)}, u32[]{:S(2)}) collective-permute-start(f32[2,16,18,1]{3,1,0,2:T(8,128)S(1)} %get-tuple-element.502), channel_id=1, source_target_pairs={{1,0},{3,2},{5,4},{7,6},{9,8},{11,10},{13,12},{15,14},{17,16},{19,... | collective-permute-start | bytes 6920 | tf_op jit(solution)/shard_map/ppermute | solution.py:17
  11.6 4.8 %copy-start.3 = (f32[16,16,128]{2,1,0:T(8,128)S(1)}, f32[16,16,128]{2,1,0:T(8,128)}, u32[]{:S(2)}) copy-start(f32[16,16,128]{2,1,0:T(8,128)} %param.21) | copy-start | bytes 393220
  11.7 9.8 %collective-permute-start.3 = (f32[2,16,18,1]{3,1,0,2:T(8,128)S(1)}, f32[2,16,18,1]{3,1,0,2:T(8,128)S(1)}, u32[]{:S(2)}, u32[]{:S(2)}) collective-permute-start(f32[2,16,18,1]{3,1,0,2:T(8,128)S(1)} %get-tuple-element.503), channel_id=1, source_target_pairs={{0,1},{2,3},{4,5},{6,7},{8,9},{10,11},{12,13},{14,15},{16,17},{18,... | collective-permute-start | bytes 6920 | tf_op jit(solution)/shard_map/ppermute | solution.py:14
  16.5 0.9 copy-start.4
  17.4 0.9 copy-start.5
  18.3 0.9 copy-start
  19.2 2.2 %copy-start.6 = (f32[2]{0:T(128)S(1)}, f32[2]{0:T(128)}, u32[]{:S(2)}) copy-start(f32[2]{0:T(128)} %constant.111.clone) | copy-start | bytes 28
  19.2 2.2 %copy-start.7 = (f32[2]{0:T(128)S(1)}, f32[2]{0:T(128)}, u32[]{:S(2)}) copy-start(f32[2]{0:T(128)} %constant.112.clone) | copy-start | bytes 28
  22.6 12.3 %all-to-all-start = ((f32[4,16,16,128]{3,1,0,2:T(8,128)}), f32[4,16,16,128]{3,1,0,2:T(8,128)S(1)}, u32[]{:S(2)}, u32[]{:S(2)}) async-start(f32[4,16,16,128]{3,1,0,2:T(8,128)} %fusion.9), calls=%async_computation | async-start | bytes 1048576 | tf_op jit(solution)/shard_map/all_to_all | solution.py:98
  50.8 4.3 %collective-permute-start.4 = (f32[2,1,16,128]{3,1,0,2:T(1,128)S(1)}, f32[2,1,16,128]{3,1,0,2:T(1,128)S(1)}, u32[]{:S(2)}, u32[]{:S(2)}) collective-permute-start(f32[2,1,16,128]{3,1,0,2:T(1,128)S(1)} %get-tuple-element.513), channel_id=1, source_target_pairs={{8,0},{16,8},{24,16},{9,1},{17,9},{25,17},{10,2},{18,10},{26,18},{... | collective-permute-start | bytes 49160 | tf_op jit(solution)/shard_map/ppermute | solution.py:17
  52.1 3.9 %collective-permute-start.5 = (f32[2,1,16,128]{3,1,0,2:T(1,128)S(1)}, f32[2,1,16,128]{3,1,0,2:T(1,128)S(1)}, u32[]{:S(2)}, u32[]{:S(2)}) collective-permute-start(f32[2,1,16,128]{3,1,0,2:T(1,128)S(1)} %get-tuple-element.512), channel_id=1, source_target_pairs={{0,8},{8,16},{16,24},{1,9},{9,17},{17,25},{2,10},{10,18},{18,26},{... | collective-permute-start | bytes 49160 | tf_op jit(solution)/shard_map/ppermute | solution.py:14
  56.2 13.8 %collective-permute-start.6 = (f32[2,18,16,1]{3,1,0,2:T(8,128)S(1)}, f32[2,18,16,1]{3,1,0,2:T(8,128)S(1)}, u32[]{:S(2)}, u32[]{:S(2)}) collective-permute-start(f32[2,18,16,1]{3,1,0,2:T(8,128)S(1)} %get-tuple-element.500), channel_id=1, source_target_pairs={{1,0},{3,2},{5,4},{7,6},{9,8},{11,10},{13,12},{15,14},{17,16},{19,... | collective-permute-start | bytes 6920 | tf_op jit(solution)/shard_map/ppermute | solution.py:17
  57.5 13.7 %collective-permute-start.7 = (f32[2,18,16,1]{3,1,0,2:T(8,128)S(1)}, f32[2,18,16,1]{3,1,0,2:T(8,128)S(1)}, u32[]{:S(2)}, u32[]{:S(2)}) collective-permute-start(f32[2,18,16,1]{3,1,0,2:T(8,128)S(1)} %get-tuple-element.501), channel_id=1, source_target_pairs={{0,1},{2,3},{4,5},{6,7},{8,9},{10,11},{12,13},{14,15},{16,17},{18,... | collective-permute-start | bytes 6920 | tf_op jit(solution)/shard_map/ppermute | solution.py:14
  72.8 19.8 %all-to-all-start.2 = ((f32[4,16,16,128]{3,2,0,1:T(8,128)}), f32[4,16,16,128]{3,2,0,1:T(8,128)S(1)}, u32[]{:S(2)}, u32[]{:S(2)}) async-start(f32[4,16,16,128]{3,2,0,1:T(8,128)} %copy.95), calls=%async_computation.2 | async-start | bytes 1048576 | tf_op jit(solution)/shard_map/all_to_all | solution.py:123
where the time goes:
time: 112 us
  waiting for transfers between devices  36.5 us (33%)
  starting transfers between devices  32.1 us (29%)
  blocking collectives  19.2 us (17%)
  local copies, waits for them, and re-layouts  8.69 us (8%)
  other arithmetic  7.69 us (7%)
  loops' own time  6.33 us (6%)
  between operations  1.15 us (1%)
    ppermute x4, starting transfers between devices, with_halo(): lax.ppermute(lax.slice_in_dim(block, block.shape[dim] - width, None, axis...  17.9 us
    all_to_all x1, waiting for transfers between devices, body(): lax.all_to_all(packed_y, 'gy', split_axis=1, concat_axis=2, tiled=True)  14.4 us
    all_to_all x1, blocking collectives, body(): lax.all_to_all(jnp.moveaxis(solved_y, 0, 2), 'gy', split_axis=2, concat_a...  10.8 us
    all_to_all x1, waiting for transfers between devices, body(): lax.all_to_all(packed, 'gx', split_axis=2, concat_axis=1, tiled=True)  8.75 us
    ppermute x4, waiting for transfers between devices, with_halo(): lax.ppermute(lax.slice_in_dim(block, 0, width, axis=dim), axis, backward)  8.6 us
    all_to_all x1, blocking collectives, body(): lax.all_to_all(jnp.moveaxis(solved, 0, 1), 'gx', split_axis=1, concat_axi...  8.39 us
    dynamic_update_slice x256, other arithmetic, eliminate(): lax.scan(forward, (upper_in, right_in), (lower_band, diagonal_band, upper...  5.46 us
    all_to_all x1, starting transfers between devices, body(): lax.all_to_all(packed_y, 'gy', split_axis=1, concat_axis=2, tiled=True)  5.45 us
  transfers between devices with their start and end apart: 10, of which 8 were waited for; matrix products, arithmetic and copies ran while one was open for 0% of the time, Pallas kernels for 0%

commit v1 on v0

v1 whole, which is shorter than its diff:
```python
import functools

import jax
import jax.numpy as jnp
from jax import lax
from jax.experimental import pallas as pl
from jax.experimental.pallas import tpu as pltpu
from jax.sharding import PartitionSpec as P

RATIOS = (1.0, 0.8)
F32 = jnp.float32
EXACT = lax.Precision.HIGHEST


def vmem():
    return pl.BlockSpec(memory_space=pltpu.VMEM)


def call(kernel, outs, *args, scratch=(), flops=400000):
    size = sum(4 * a.size for a in args)
    return pl.pallas_call(
        kernel,
        out_shape=tuple(jax.ShapeDtypeStruct(s, F32) for s in outs),
        in_specs=[vmem()] * len(args),
        out_specs=tuple(vmem() for _ in outs),
        scratch_shapes=list(scratch),
        cost_estimate=pl.CostEstimate(flops=flops, bytes_accessed=size, transcendentals=0),
    )(*args)


def factor(n, lat, half_cfl, ratio, inv_out, mid_out, up_out, first_out, last_out):
    inv, mids, ups, firsts = [], [], [], []
    up = first = None
    for k in range(n):
        lateral = ratio * lat(k)
        half = half_cfl(k)
        east, west = lateral - half, lateral + half
        pivot = 1.0 + 2.0 * lateral
        if k:
            pivot = pivot - west * up
        inverse = 1.0 / pivot
        mid = west * inverse
        up = east * inverse
        first = mid if k == 0 else mid * first
        inv_out(k, inverse)
        mid_out(k, mid)
        up_out(k, up)
        ups.append(up)
        firsts.append(first)
    q, r = firsts[-1], ups[-1]
    first_out(n - 1, q)
    last_out(n - 1, r)
    for k in range(n - 2, -1, -1):
        q = firsts[k] + ups[k] * q
        r = ups[k] * r
        first_out(k, q)
        last_out(k, r)


def sweep(n, rhs, inv, mid, up, out):
    values = []
    value = None
    for k in range(n):
        value = inv(k) * rhs(k) if k == 0 else inv(k) * rhs(k) + mid(k) * value
        values.append(value)
    out(n - 1, value)
    for k in range(n - 2, -1, -1):
        value = values[k] + up(k) * value
        out(k, value)


def along(port, before):
    p1, p2, q1, q2, r1, r2 = port
    source, slope = before
    t = 1.0 / (1.0 - q1 * slope)
    step = q2 * slope * t
    return (p2 + q2 * source + step * (p1 + q1 * source), r2 + step * r1)


def mirrored(port):
    p1, p2, q1, q2, r1, r2 = port
    return (p2, p1, r2, r1, q2, q1)


def interface(me, n, port_of, own):
    zero = jnp.zeros_like(own[0])
    left, right = (zero, zero), (zero, zero)
    for j in range(n - 1):
        stepped = along(port_of(j), left)
        left = tuple(jnp.where(j < me, a, b) for a, b in zip(stepped, left))
        i = n - 1 - j
        stepped = along(mirrored(port_of(i)), right)
        right = tuple(jnp.where(i > me, a, b) for a, b in zip(stepped, right))
    p1, p2, q1, q2, r1, r2 = own
    pl_, ql = left
    pr, qr = right
    a1 = p1 + q1 * pl_ + r1 * pr
    a2 = p2 + q2 * pl_ + r2 * pr
    b11, b22 = 1.0 - q1 * ql, 1.0 - r2 * qr
    b12, b21 = r1 * qr, q2 * ql
    t = 1.0 / (b11 * b22 - b12 * b21)
    u1 = (a1 * b22 + b12 * a2) * t
    u2 = (b11 * a2 + b21 * a1) * t
    return pl_ + ql * u1, pr + qr * u2


def faces_kernel(nx, ny, nz, t_ref, h_ref, odd_y, fy1, fy2, fz):
    pass


def strided(ref, f, k, nx, ny):
    return ref[f, pl.ds(k, nx, stride=ny), :]


def coef_kernel(nx, ny, lat, cx, cy, xi, xm, xu, xq, xr, yi, ym, yu, yq, yr):
    def put(ref, f):
        def store(k, v):
            ref[f, k] = v

        return store

    for f, ratio in enumerate(RATIOS):
        factor(
            nx,
            lambda k: lat[pl.ds(k * ny, ny), :],
            lambda k: 0.5 * cx[pl.ds(k * ny, ny), :],
            ratio,
            *(put(ref, f) for ref in (xi, xm, xu, xq, xr)),
        )
        factor(
            ny,
            lambda k: lat[pl.ds(k, nx, stride=ny), :],
            lambda k: 0.5 * cy[pl.ds(k, nx, stride=ny), :],
            ratio,
            *(put(ref, f) for ref in (yi, ym, yu, yq, yr)),
        )


def lane_shifts(v, nz, high, low):
    lane = lax.broadcasted_iota(jnp.int32, v.shape, v.ndim - 1)
    ahead = jnp.where(lane == nz - 1, high, pltpu.roll(v, nz - 1, v.ndim - 1))
    behind = jnp.where(lane == 0, low, pltpu.roll(v, 1, v.ndim - 1))
    return ahead, behind


def first_kernel(nx, ny, nz, t, h, load, lat, up, cy, cz, ylo, yhi, zlo, zhi, xi, xm, xu, d, p):
    for f, (ratio, ref) in enumerate(zip(RATIOS, (t, h))):
        for k in range(nx):
            v = ref[k]
            row = lax.broadcasted_iota(jnp.int32, v.shape, 0)
            ahead = jnp.where(row == ny - 1, yhi[f, pl.ds(k, 1), :], pltpu.roll(v, ny - 1, 0))
            behind = jnp.where(row == 0, ylo[f, pl.ds(k, 1), :], pltpu.roll(v, 1, 0))
            lateral, half = ratio * lat[k], 0.5 * cy[k]
            out = v + ((lateral - half) * (ahead - v) + (lateral + half) * (behind - v))
            ahead, behind = lane_shifts(v, nz, zhi[f, k], zlo[f, k])
            lateral, half = ratio * up[k], 0.5 * cz[k]
            out = out + ((lateral - half) * (ahead - v) + (lateral + half) * (behind - v))
            if f == 0:
                out = out + load[k]
            d[f, k] = out

        def put(k, v):
            p[f, k] = v

        sweep(nx, lambda k: d[f, k], lambda k: xi[f, k], lambda k: xm[f, k], lambda k: xu[f, k], put)


def own_port(ref, f):
    return tuple(ref[v, f] for v in range(6))


def half_kernel(axis, n, by_xor, nx, p, q, r, ports, own, half):
    me = lax.axis_index(axis)
    for f in range(2):

        def port_of(j):
            at = (j ^ me) if by_xor else j
            return tuple(ports[at, v, f] for v in range(6))

        low, high = interface(me, n, port_of, own_port(own, f))
        for k in range(nx):
            half[f, k] = p[f, k] + q[f, k] * low + r[f, k] * high


def second_kernel(nx, ny, nz, half, d, load, up, cz, zlo, zhi, yi, ym, yu, p, s):
    for f, ratio in enumerate(RATIOS):
        for k in range(nx):
            v = half[f, k]
            ahead, behind = lane_shifts(v, nz, zhi[f, k], zlo[f, k])
            lateral, half_cfl = ratio * up[k], 0.5 * cz[k]
            out = 2.0 * v - d[f, k]
            out = out + ((lateral - half_cfl) * (ahead - v) + (lateral + half_cfl) * (behind - v))
            if f == 0:
                out = out + load[k]
            s[f, pl.ds(k * ny, ny), :] = out

        def put(k, v):
            p[f, k] = v

        sweep(
            ny,
            lambda k: s[f, pl.ds(k, nx, stride=ny), :],
            lambda k: yi[f, k],
            lambda k: ym[f, k],
            lambda k: yu[f, k],
            put,
        )


def new_kernel(axis, n, by_xor, nx, ny, p, q, r, ports, own, t_new, h_new):
    me = lax.axis_index(axis)
    for f, ref in enumerate((t_new, h_new)):

        def port_of(j):
            at = (j ^ me) if by_xor else j
            return tuple(ports[at, v, f] for v in range(6))

        low, high = interface(me, n, port_of, own_port(own, f))
        for k in range(ny):
            ref[pl.ds(k, nx, stride=ny), :] = p[f, k] + q[f, k] * low + r[f, k] * high


def neighbours(low_face, high_face, axis):
    n = lax.axis_size(axis)
    even = lax.axis_index(axis) % 2 == 0

    def swap(pairs, value):
        if not pairs:
            return jnp.zeros_like(value)
        return lax.ppermute(value, axis, pairs + [(b, a) for a, b in pairs])

    one = swap([(i, i + 1) for i in range(0, n - 1, 2)], jnp.where(even, high_face, low_face))
    two = swap([(i, i + 1) for i in range(1, n - 1, 2)], jnp.where(even, low_face, high_face))
    return jnp.where(even, two, one), jnp.where(even, one, two)


def everyones(own, axis):
    n = lax.axis_size(axis)
    by_xor = n in (2, 4)
    if not by_xor:
        return by_xor, lax.all_gather(own, axis)
    parts = [own]
    for k in range(1, n):
        parts.append(lax.ppermute(own, axis, [(i, i ^ k) for i in range(n)]))
    return by_xor, jnp.stack(parts)


def body(thermal, vapour, load, lat, up, cx, cy, cz):
    nx, ny, nz = thermal.shape
    flat = (nx * ny, nz)
    lines_x, lines_y = (2, nx, ny, nz), (2, ny, nx, nz)
    fields = jnp.stack([thermal, vapour])
    ylo, yhi = neighbours(fields[:, :, 0, :], fields[:, :, ny - 1, :], "gy")
    zlo, zhi = neighbours(fields[:, :, :, 0], fields[:, :, :, nz - 1], "gz")
    xi, xm, xu, xq, xr, yi, ym, yu, yq, yr = call(
        functools.partial(coef_kernel, nx, ny),
        (lines_x,) * 5 + (lines_y,) * 5,
        lat.reshape(flat),
        cx.reshape(flat),
        cy.reshape(flat),
    )
    d, p = call(
        functools.partial(first_kernel, nx, ny, nz),
        (lines_x, lines_x),
        thermal, vapour, load, lat, up, cy, cz, ylo, yhi, zlo[..., None], zhi[..., None], xi, xm, xu,
    )
    own = jnp.stack([p[:, 0], p[:, -1], xq[:, 0], xq[:, -1], xr[:, 0], xr[:, -1]])
    by_xor, ports = everyones(own, "gx")
    (half,) = call(
        functools.partial(half_kernel, "gx", lax.axis_size("gx"), by_xor, nx),
        (lines_x,),
        p, xq, xr, ports, own,
    )
    zlo, zhi = neighbours(half[:, :, :, 0], half[:, :, :, nz - 1], "gz")
    (p,) = call(
        functools.partial(second_kernel, nx, ny, nz),
        (lines_y,),
        half, d, load, up, cz, zlo[..., None], zhi[..., None], yi, ym, yu,
        scratch=[pltpu.VMEM((2,) + flat, F32)],
    )
    own = jnp.stack([p[:, 0], p[:, -1], yq[:, 0], yq[:, -1], yr[:, 0], yr[:, -1]])
    by_xor, ports = everyones(own, "gy")
    t_new, h_new = call(
        functools.partial(new_kernel, "gy", lax.axis_size("gy"), by_xor, nx, ny),
        (flat, flat),
        p, yq, yr, ports, own,
    )
    return t_new.reshape(thermal.shape), h_new.reshape(thermal.shape)


def solution(mesh):
    spec = P("gx", "gy", "gz")
    return jax.shard_map(
        body, mesh=mesh, in_specs=(spec,) * 8, out_specs=(spec, spec), check_vma=False
    )
```

time: 112 us -> 61 us (0.54)
  waiting for transfers between devices: 36.5 us -> 14.6 us
  blocking collectives: 19.2 us -> 0 us
  starting transfers between devices: 32.1 us -> 15 us
  Pallas kernels: 0 us -> 12.4 us
  loops' own time: 6.33 us -> 0 us
  local copies, waits for them, and re-layouts: 8.69 us -> 12.5 us
  other arithmetic: 7.69 us -> 4.86 us
    all_to_all x2 -> x0, waiting for transfers between devices: 23.1 us -> none  [the longest x1 14.4 us: body(): lax.all_to_all(packed_y, 'gy', split_axis=1, concat_axis=2, tiled=True)]
    all_to_all x2 -> x0, blocking collectives: 19.2 us -> none  [the longest x1 10.8 us: body(): lax.all_to_all(jnp.moveaxis(solved_y, 0, 2), 'gy', split_axis=2, concat_a...]
    pallas_call x0 -> x5, Pallas kernels: none -> 12.4 us  [call(): pl.pallas_call(kernel, out_shape=tuple((jax.ShapeDtypeStruct(s, F32) for...]
    all_to_all x2 -> x0, starting transfers between devices: 8.92 us -> none  [the longest x1 5.45 us: body(): lax.all_to_all(packed_y, 'gy', split_axis=1, concat_axis=2, tiled=True)]
    ppermute x8 -> x10, starting transfers between devices: 23.2 us -> 15 us  [the longest x4 8.76 us: swap(): return lax.ppermute(value, axis, pairs + [(b, a) for a, b in pairs])]
    another operation x4 -> x0, loops' own time: 6.33 us -> none  [the longest x2 3.91 us: eliminate(): lax.scan(forward, (upper_in, right_in), (lower_band, diagonal_band, upper...]
    dynamic_update_slice x256 -> x0, other arithmetic: 5.46 us -> none  [eliminate(): lax.scan(forward, (upper_in, right_in), (lower_band, diagonal_band, upper...]
    unnamed x21 -> x18, local copies, waits for them, and re-layouts: 2.8 us -> 7.21 us
  transfers between devices with their start and end apart: 10 -> 10, of which waited for: 8 -> 5; matrix products, arithmetic and copies ran while one was open for 0% -> 3% of each run, Pallas kernels for 0% -> 5%
where the time goes in v1:
time: 61 us; the launch traced here: 60.1 us
  starting transfers between devices  15 us (25%)
  waiting for transfers between devices  14.6 us (24%)
  local copies, waits for them, and re-layouts  12.5 us (20%)
  Pallas kernels  12.4 us (20%)
  other arithmetic  4.86 us (8%)
  between operations  0.72 us (1%)
    pallas_call x5, Pallas kernels, call(): pl.pallas_call(kernel, out_shape=tuple((jax.ShapeDtypeStruct(s, F32) for...  12.4 us
    ppermute x6, waiting for transfers between devices, everyones(): parts.append(lax.ppermute(own, axis, [(i, i ^ k) for i in range(n)]))  11.3 us
    ppermute x4, starting transfers between devices, swap(): return lax.ppermute(value, axis, pairs + [(b, a) for a, b in pairs])  8.76 us
    unnamed x18, local copies, waits for them, and re-layouts  7.21 us
    ppermute x6, starting transfers between devices, everyones(): parts.append(lax.ppermute(own, axis, [(i, i ^ k) for i in range(n)]))  6.25 us
    ppermute x4, waiting for transfers between devices, swap(): return lax.ppermute(value, axis, pairs + [(b, a) for a, b in pairs])  3.21 us
    select_n x3, other arithmetic, neighbours(): jnp.where(even, high_face, low_face)  2.68 us
    broadcast_in_dim x2, local copies, waits for them, and re-layouts, body(): zlo[..., None]  1.94 us
  transfers between devices with their start and end apart: 10, of which 5 were waited for; matrix products, arithmetic and copies ran while one was open for 3% of the time, Pallas kernels for 5%

profile of v1, /device:TPU:0, one launch (start us, length us, event | category | flops | bytes accessed | tf_op | source)
XLA Modules:
  0.0 60.1 jit_solution(5864006621437176552)
XLA Ops:
  0.6 0.0 copy-start
  0.7 0.0 copy-start.1
  0.7 1.4 %fusion.2 = f32[2,16,16]{2,1,0:T(8,128)S(1)} fusion(f32[1,16,16,128]{3,2,1,0:T(8,128)} %bitcast.82, f32[1,16,16,128]{3,2,1,0:T(8,128)} %bitcast.80, pred[]{:T(512)S(6)} %eq.12), kind=kLoop, calls=%fused_computation.6 | loop fusion | flops 1536 | bytes 264193 | tf_op jit(solution)/shard_map/jit(_where)/select_n | solution.py:232
  2.1 3.0 %collective-permute-start.2 = (f32[2,16,16]{2,1,0:T(8,128)S(1)}, f32[2,16,16]{2,1,0:T(8,128)S(1)}, u32[]{:S(2)}, u32[]{:S(2)}) collective-permute-start(f32[2,16,16]{2,1,0:T(8,128)S(1)} %fusion.2), channel_id=1, source_target_pairs={{0,1},{1,0},{2,3},{3,2},{4,5},{5,4},{6,7},{7,6},{8,9},{9,8},{10,11... | collective-permute-start | bytes 6152 | tf_op jit(solution)/shard_map/ppermute | solution.py:230
  5.1 0.7 %collective-permute-start = (f32[2,16,128]{2,1,0:T(8,128)S(1)}, f32[2,16,128]{2,1,0:T(8,128)S(1)}, u32[]{:S(2)}, u32[]{:S(2)}) collective-permute-start(f32[2,16,128]{2,1,0:T(8,128)S(1)} %bitcast.98), channel_id=1, source_target_pairs={{2,4},{4,2},{3,5},{5,3},{10,12},{12,10},{11,13},{13,11},{18,20},{2... | collective-permute-start | bytes 49160 | tf_op jit(solution)/shard_map/ppermute | solution.py:230
  5.8 4.5 %collective-permute-start.1 = (f32[2,16,128]{2,1,0:T(8,128)S(1)}, f32[2,16,128]{2,1,0:T(8,128)S(1)}, u32[]{:S(2)}, u32[]{:S(2)}) collective-permute-start(f32[2,16,128]{2,1,0:T(8,128)S(1)} %bitcast.97), channel_id=1, source_target_pairs={{0,2},{4,6},{2,0},{6,4},{1,3},{5,7},{3,1},{7,5},{8,10},{12,14},{10... | collective-permute-start | bytes 49160 | tf_op jit(solution)/shard_map/ppermute | solution.py:230
  10.3 2.8 %shard_map.95 = (f32[2,16,16,128]{3,2,1,0:T(8,128)}, f32[2,16,16,128]{3,2,1,0:T(8,128)}, f32[2,16,16,128]{3,2,1,0:T(8,128)}, f32[2,16,16,128]{3,2,1,0:T(8,128)},...) custom-call(f32[256,128]{1,0:T(8,128)} %bitcast.84, ...), custom_call_target="tpu_custom_call" | custom-call | flops 400000 | bytes 393216 | tf_op jit(solution)/shard_map/pallas_call | solution.py:21
  13.1 0.0 collective-permute-done.2
  13.1 1.0 %copy.126.zhi = f32[2,16,16,1]{3,2,1,0:T(8,128)} copy(f32[2,16,16,1]{2,1,0,3:T(8,128)S(1)} %get-tuple-element.37) | data formatting | bytes 4096 | tf_op jit(solution)/shard_map/broadcast_in_dim | solution.py:265
  14.1 1.0 %copy.125.zlo = f32[2,16,16,1]{3,2,1,0:T(8,128)} copy(f32[2,16,16,1]{2,1,0,3:T(8,128)S(1)} %get-tuple-element.38) | data formatting | bytes 4096 | tf_op jit(solution)/shard_map/broadcast_in_dim | solution.py:265
  15.0 0.0 collective-permute-done
  15.0 0.0 collective-permute-done.1
  15.0 0.6 %broadcast_select_fusion.2 = (f32[2,16,128]{2,1,0:T(8,128)}, f32[2,16,128]{2,1,0:T(8,128)}) fusion(f32[2,16,128]{2,1,0:T(8,128)S(1)} %collective-permute-done.1, f32[2,16,128]{2,1,0:T(8,128)S(1)} %collective-permute-done, pred[]{:T(512)S(6)} %eq.11), kind=kLoop, calls=%fused_computation.39 | loop fusion | flops 8192 | bytes 65537 | tf_op jit(solution)/shard_map/jit(_where)/select_n | solution.py:234
  15.7 2.8 %shard_map.96 = (f32[2,16,16,128]{3,2,1,0:T(8,128)}, f32[2,16,16,128]{3,2,1,0:T(8,128)}) custom-call(f32[16,16,128]{2,1,0:T(8,128)} %t.1, f32[16,16,128]{2,1,0:T(8,128)} %h.1, f32[16,16,128]{2,1,0:T(8,128)} %load.3, f32[16,16,128]{2,1,0:T(8,128)} %lat.1, f32[16,16,128]{2,1,0:T(8,128)} %up.3, f32[16,16,128]{2,1,0:T(8,128)} %cy.1, f32[16,16,128]{2,1,0:T(8,128)} %cz.3, ...), custom_call_target="tpu_custom_call" | custom-call | flops 400000 | bytes 1740800 | tf_op jit(solution)/shard_map/pallas_call | solution.py:21
  18.4 0.7 %constant_dynamic-update-slice_fusion.5 = f32[6,2,16,128]{3,2,1,0:T(8,128)S(1)} fusion(f32[2,16,16,128]{3,2,1,0:T(8,128)} %get-tuple-element.19.p), kind=kLoop, calls=%fused_computation.14 | loop fusion | bytes 32768
  19.2 0.7 %constant_dynamic-update-slice_fusion.4 = f32[6,2,16,128]{3,2,1,0:T(8,128)S(1)} fusion(f32[6,2,16,128]{3,2,1,0:T(8,128)S(1)} %constant_dynamic-update-slice_fusion.5, f32[2,16,16,128]{3,2,1,0:T(8,128)} %get-tuple-element.19.p), kind=kLoop, calls=%fused_computation.13 | loop fusion | bytes 32768
  19.9 0.7 %constant_dynamic-update-slice_fusion.3 = f32[6,2,16,128]{3,2,1,0:T(8,128)S(1)} fusion(f32[6,2,16,128]{3,2,1,0:T(8,128)S(1)} %constant_dynamic-update-slice_fusion.4, f32[2,16,16,128]{3,2,1,0:T(8,128)} %get-tuple-element.20.q), kind=kLoop, calls=%fused_computation.12 | loop fusion | bytes 32768
  20.6 0.7 %constant_dynamic-update-slice_fusion.2 = f32[6,2,16,128]{3,2,1,0:T(8,128)S(1)} fusion(f32[6,2,16,128]{3,2,1,0:T(8,128)S(1)} %constant_dynamic-update-slice_fusion.3, f32[2,16,16,128]{3,2,1,0:T(8,128)} %get-tuple-element.20.q), kind=kLoop, calls=%fused_computation.11 | loop fusion | bytes 32768
  21.3 0.7 %constant_dynamic-update-slice_fusion.1 = f32[6,2,16,128]{3,2,1,0:T(8,128)S(1)} fusion(f32[6,2,16,128]{3,2,1,0:T(8,128)S(1)} %constant_dynamic-update-slice_fusion.2, f32[2,16,16,128]{3,2,1,0:T(8,128)} %get-tuple-element.21.r), kind=kLoop, calls=%fused_computation.10 | loop fusion | bytes 32768
  22.0 0.7 %constant_dynamic-update-slice_fusion.own = f32[6,2,16,128]{3,2,1,0:T(8,128)S(1)} fusion(f32[6,2,16,128]{3,2,1,0:T(8,128)S(1)} %constant_dynamic-update-slice_fusion.1, f32[2,16,16,128]{3,2,1,0:T(8,128)} %get-tuple-element.21.r), kind=kLoop, calls=%fused_computation.9 | loop fusion | bytes 32768 | tf_op jit(solution)/shard_map/stack | solution.py:267
  22.8 0.1 collective-permute-start.5
  22.9 1.4 %collective-permute-start.4 = (f32[6,2,16,128]{3,2,1,0:T(8,128)S(1)}, f32[6,2,16,128]{3,2,1,0:T(8,128)S(1)}, u32[]{:S(2)}, u32[]{:S(2)}) collective-permute-start(f32[6,2,16,128]{3,2,1,0:T(8,128)S(1)} %constant_dynamic-update-slice_fusion.own), channel_id=1, source_target_pairs={{0,16},{8,24},{16,0},{24,8},{1,17},{9,25},{17,1},{25,9},{2,18},{10... | collective-permute-start | bytes 294920 | tf_op jit(solution)/shard_map/ppermute | solution.py:244
  24.3 0.3 collective-permute-start.3
  24.6 3.2 %collective-permute-done.5 = f32[6,2,16,128]{3,2,1,0:T(8,128)S(1)} collective-permute-done((f32[6,2,16,128]{3,2,1,0:T(8,128)S(1)}, f32[6,2,16,128]{3,2,1,0:T(8,128)S(1)}, u32[]{:S(2)}, u32[]{:S(2)}) %collective-permute-start.5) | collective-permute-done | bytes 98336 | tf_op jit(solution)/shard_map/ppermute | solution.py:244
  27.8 2.2 %collective-permute-done.4 = f32[6,2,16,128]{3,2,1,0:T(8,128)S(1)} collective-permute-done((f32[6,2,16,128]{3,2,1,0:T(8,128)S(1)}, f32[6,2,16,128]{3,2,1,0:T(8,128)S(1)}, u32[]{:S(2)}, u32[]{:S(2)}) %collective-permute-start.4) | collective-permute-done | bytes 98336 | tf_op jit(solution)/shard_map/ppermute | solution.py:244
  30.0 0.0 collective-permute-done.3
  30.0 0.8 %pad_maximum_fusion.ports = f32[4,6,2,16,128]{4,3,2,1,0:T(8,128)} fusion(f32[1,6,2,16,128]{4,3,2,1,0:T(8,128)S(1)} %bitcast.89, f32[1,6,2,16,128]{4,3,2,1,0:T(8,128)S(1)} %bitcast.91, f32[1,6,2,16,128]{4,3,2,1,0:T(8,128)S(1)} %bitcast.93, f32[1,6,2,16,128]{4,3,2,1,0:T(8,128)S(1)} %bitcast.86), kind=kLoop, calls=%fused_computation | loop fusion | flops 294912 | bytes 786432 | tf_op jit(solution)/shard_map/stack | solution.py:245
  30.7 2.1 %shard_map.97.half = f32[2,16,16,128]{3,2,1,0:T(8,128)} custom-call(f32[2,16,16,128]{3,2,1,0:T(8,128)} %get-tuple-element.19.p, f32[2,16,16,128]{3,2,1,0:T(8,128)} %get-tuple-element.20.q, f32[2,16,16,128]{3,2,1,0:T(8,128)} %get-tuple-element.21.r, f32[4,6,2,16,128]{4,3,2,1,0:T(8,128)} %pad_maximum_fusion.ports, f32[6,2,16,128]{3,2,1,0:T(8,128)} %copy-done.2), custom_call_target="tpu_custom_call" | custom-call | flops 400000 | bytes 1277952 | tf_op jit(solution)/shard_map/pallas_call | solution.py:21
  32.8 1.3 %fusion = f32[2,16,16]{2,1,0:T(8,128)S(1)} fusion(f32[2,16,16,128]{3,2,1,0:T(8,128)} %shard_map.97.half, pred[]{:T(512)S(6)} %eq.12), kind=kLoop, calls=%fused_computation.3 | loop fusion | flops 512 | bytes 6145 | tf_op jit(solution)/shard_map/jit(_where)/select_n | solution.py:232
  34.1 0.6 collective-permute-start.6
  34.7 3.2 %collective-permute-done.6 = f32[2,16,16]{2,1,0:T(8,128)S(1)} collective-permute-done((f32[2,16,16]{2,1,0:T(8,128)S(1)}, f32[2,16,16]{2,1,0:T(8,128)S(1)}, u32[]{:S(2)}, u32[]{:S(2)}) %collective-permute-start.6) | collective-permute-done | bytes 2080 | tf_op jit(solution)/shard_map/ppermute | solution.py:230
  37.9 1.0 %copy.134.zhi = f32[2,16,16,1]{3,2,1,0:T(8,128)} copy(f32[2,16,16,1]{2,1,0,3:T(8,128)S(1)} %get-tuple-element.35) | data formatting | bytes 4096 | tf_op jit(solution)/shard_map/broadcast_in_dim | solution.py:278
  38.9 1.0 %copy.133.zlo = f32[2,16,16,1]{3,2,1,0:T(8,128)} copy(f32[2,16,16,1]{2,1,0,3:T(8,128)S(1)} %get-tuple-element.36) | data formatting | bytes 4096 | tf_op jit(solution)/shard_map/broadcast_in_dim | solution.py:278
  39.8 2.7 %shard_map.98.p = f32[2,16,16,128]{3,2,1,0:T(8,128)} custom-call(f32[2,16,16,128]{3,2,1,0:T(8,128)} %shard_map.97.half, f32[2,16,16,128]{3,2,1,0:T(8,128)} %get-tuple-element.22.d, f32[16,16,128]{2,1,0:T(8,128)} %load.3, f32[16,16,128]{2,1,0:T(8,128)} %up.3, f32[16,16,128]{2,1,0:T(8,128)} %cz.3, f32[2,16,16,1]{3,2,1,0:T(8,128)} %copy.133.zlo, ...), custom_call_target="tpu_custom_call" | custom-call | flops 400000 | bytes 1708032 | tf_op jit(solution)/shard_map/pallas_call | solution.py:21
  42.5 0.7 %constant_dynamic-update-slice_fusion.11 = f32[6,2,16,128]{3,2,1,0:T(8,128)S(1)} fusion(f32[2,16,16,128]{3,2,1,0:T(8,128)} %shard_map.98.p), kind=kLoop, calls=%fused_computation.20 | loop fusion | bytes 32768
  43.2 0.7 %constant_dynamic-update-slice_fusion.10 = f32[6,2,16,128]{3,2,1,0:T(8,128)S(1)} fusion(f32[6,2,16,128]{3,2,1,0:T(8,128)S(1)} %constant_dynamic-update-slice_fusion.11, f32[2,16,16,128]{3,2,1,0:T(8,128)} %shard_map.98.p), kind=kLoop, calls=%fused_computation.19 | loop fusion | bytes 32768
  44.0 0.7 %constant_dynamic-update-slice_fusion.9 = f32[6,2,16,128]{3,2,1,0:T(8,128)S(1)} fusion(f32[6,2,16,128]{3,2,1,0:T(8,128)S(1)} %constant_dynamic-update-slice_fusion.10, f32[2,16,16,128]{3,2,1,0:T(8,128)} %get-tuple-element.26.q), kind=kLoop, calls=%fused_computation.18 | loop fusion | bytes 32768
  44.7 0.7 %constant_dynamic-update-slice_fusion.8 = f32[6,2,16,128]{3,2,1,0:T(8,128)S(1)} fusion(f32[6,2,16,128]{3,2,1,0:T(8,128)S(1)} %constant_dynamic-update-slice_fusion.9, f32[2,16,16,128]{3,2,1,0:T(8,128)} %get-tuple-element.26.q), kind=kLoop, calls=%fused_computation.17 | loop fusion | bytes 32768
  45.4 0.7 %constant_dynamic-update-slice_fusion.7 = f32[6,2,16,128]{3,2,1,0:T(8,128)S(1)} fusion(f32[6,2,16,128]{3,2,1,0:T(8,128)S(1)} %constant_dynamic-update-slice_fusion.8, f32[2,16,16,128]{3,2,1,0:T(8,128)} %get-tuple-element.27.r), kind=kLoop, calls=%fused_computation.16 | loop fusion | bytes 32768
  46.1 0.7 %constant_dynamic-update-slice_fusion.6.own = f32[6,2,16,128]{3,2,1,0:T(8,128)S(1)} fusion(f32[6,2,16,128]{3,2,1,0:T(8,128)S(1)} %constant_dynamic-update-slice_fusion.7, f32[2,16,16,128]{3,2,1,0:T(8,128)} %get-tuple-element.27.r), kind=kLoop, calls=%fused_computation.15 | loop fusion | bytes 32768 | tf_op jit(solution)/shard_map/stack | solution.py:281
  46.8 1.3 %collective-permute-start.9 = (f32[6,2,16,128]{3,2,1,0:T(8,128)S(1)}, f32[6,2,16,128]{3,2,1,0:T(8,128)S(1)}, u32[]{:S(2)}, u32[]{:S(2)}) collective-permute-start(f32[6,2,16,128]{3,2,1,0:T(8,128)S(1)} %constant_dynamic-update-slice_fusion.6.own), channel_id=1, source_target_pairs={{0,6},{2,4},{4,2},{6,0},{1,7},{3,5},{5,3},{7,1},{8,14},{10,12},{12... | collective-permute-start | bytes 294920 | tf_op jit(solution)/shard_map/ppermute | solution.py:244
  48.2 0.1 collective-permute-start.8
  48.3 2.9 %collective-permute-start.7 = (f32[6,2,16,128]{3,2,1,0:T(8,128)S(1)}, f32[6,2,16,128]{3,2,1,0:T(8,128)S(1)}, u32[]{:S(2)}, u32[]{:S(2)}) collective-permute-start(f32[6,2,16,128]{3,2,1,0:T(8,128)S(1)} %constant_dynamic-update-slice_fusion.6.own), channel_id=1, source_target_pairs={{0,2},{2,0},{4,6},{6,4},{1,3},{3,1},{5,7},{7,5},{8,10},{10,8},{12,... | collective-permute-start | bytes 294920 | tf_op jit(solution)/shard_map/ppermute | solution.py:244
  51.2 3.1 %collective-permute-done.9 = f32[6,2,16,128]{3,2,1,0:T(8,128)S(1)} collective-permute-done((f32[6,2,16,128]{3,2,1,0:T(8,128)S(1)}, f32[6,2,16,128]{3,2,1,0:T(8,128)S(1)}, u32[]{:S(2)}, u32[]{:S(2)}) %collective-permute-start.9) | collective-permute-done | bytes 98336 | tf_op jit(solution)/shard_map/ppermute | solution.py:244
  54.3 2.9 %collective-permute-done.8 = f32[6,2,16,128]{3,2,1,0:T(8,128)S(1)} collective-permute-done((f32[6,2,16,128]{3,2,1,0:T(8,128)S(1)}, f32[6,2,16,128]{3,2,1,0:T(8,128)S(1)}, u32[]{:S(2)}, u32[]{:S(2)}) %collective-permute-start.8) | collective-permute-done | bytes 98336 | tf_op jit(solution)/shard_map/ppermute | solution.py:244
  57.2 0.0 collective-permute-done.7
  57.2 0.8 %pad_maximum_fusion.1.ports = f32[4,6,2,16,128]{4,3,2,1,0:T(8,128)} fusion(f32[1,6,2,16,128]{4,3,2,1,0:T(8,128)S(1)} %bitcast.90, f32[1,6,2,16,128]{4,3,2,1,0:T(8,128)S(1)} %bitcast.92, f32[1,6,2,16,128]{4,3,2,1,0:T(8,128)S(1)} %bitcast.94, f32[1,6,2,16,128]{4,3,2,1,0:T(8,128)S(1)} %bitcast.87), kind=kLoop, calls=%fused_computation.1 | loop fusion | flops 294912 | bytes 786432 | tf_op jit(solution)/shard_map/stack | solution.py:245
  58.0 2.1 %shard_map.99 = (f32[256,128]{1,0:T(8,128)}, f32[256,128]{1,0:T(8,128)}) custom-call(f32[2,16,16,128]{3,2,1,0:T(8,128)} %shard_map.98.p, f32[2,16,16,128]{3,2,1,0:T(8,128)} %get-tuple-element.26.q, f32[2,16,16,128]{3,2,1,0:T(8,128)} %get-tuple-element.27.r, f32[4,6,2,16,128]{4,3,2,1,0:T(8,128)} %pad_maximum_fusion.1.ports, f32[6,2,16,128]{3,2,1,0:T(8,128)} %copy-done.3), custom_call_target="tpu_custom_call" | custom-call | flops 400000 | bytes 1277952 | tf_op jit(solution)/shard_map/pallas_call | solution.py:21
  (10 shorter events, 0.1 us)
Async XLA Ops:
  0.6 4.4 %copy-start = (f32[16,16,128]{2,1,0:T(8,128)S(1)}, f32[16,16,128]{2,1,0:T(8,128)}, u32[]{:S(2)}) copy-start(f32[16,16,128]{2,1,0:T(8,128)} %t.1) | copy-start | bytes 393220
  0.7 4.4 %copy-start.1 = (f32[16,16,128]{2,1,0:T(8,128)S(1)}, f32[16,16,128]{2,1,0:T(8,128)}, u32[]{:S(2)}) copy-start(f32[16,16,128]{2,1,0:T(8,128)} %h.1) | copy-start | bytes 393220
  2.1 11.0 %collective-permute-start.2 = (f32[2,16,16]{2,1,0:T(8,128)S(1)}, f32[2,16,16]{2,1,0:T(8,128)S(1)}, u32[]{:S(2)}, u32[]{:S(2)}) collective-permute-start(f32[2,16,16]{2,1,0:T(8,128)S(1)} %fusion.2), channel_id=1, source_target_pairs={{0,1},{1,0},{2,3},{3,2},{4,5},{5,4},{6,7},{7,6},{8,9},{9,8},{10,11... | collective-permute-start | bytes 6152 | tf_op jit(solution)/shard_map/ppermute | solution.py:230
  5.1 9.9 %collective-permute-start = (f32[2,16,128]{2,1,0:T(8,128)S(1)}, f32[2,16,128]{2,1,0:T(8,128)S(1)}, u32[]{:S(2)}, u32[]{:S(2)}) collective-permute-start(f32[2,16,128]{2,1,0:T(8,128)S(1)} %bitcast.98), channel_id=1, source_target_pairs={{2,4},{4,2},{3,5},{5,3},{10,12},{12,10},{11,13},{13,11},{18,20},{2... | collective-permute-start | bytes 49160 | tf_op jit(solution)/shard_map/ppermute | solution.py:230
  5.8 9.2 %collective-permute-start.1 = (f32[2,16,128]{2,1,0:T(8,128)S(1)}, f32[2,16,128]{2,1,0:T(8,128)S(1)}, u32[]{:S(2)}, u32[]{:S(2)}) collective-permute-start(f32[2,16,128]{2,1,0:T(8,128)S(1)} %bitcast.97), channel_id=1, source_target_pairs={{0,2},{4,6},{2,0},{6,4},{1,3},{5,7},{3,1},{7,5},{8,10},{12,14},{10... | collective-permute-start | bytes 49160 | tf_op jit(solution)/shard_map/ppermute | solution.py:230
  22.8 8.0 %copy-start.2 = (f32[6,2,16,128]{3,2,1,0:T(8,128)}, f32[6,2,16,128]{3,2,1,0:T(8,128)S(1)}, u32[]{:S(2)}) copy-start(f32[6,2,16,128]{3,2,1,0:T(8,128)S(1)} %constant_dynamic-update-slice_fusion.own) | copy-start | bytes 294916
  22.8 5.0 %collective-permute-start.5 = (f32[6,2,16,128]{3,2,1,0:T(8,128)S(1)}, f32[6,2,16,128]{3,2,1,0:T(8,128)S(1)}, u32[]{:S(2)}, u32[]{:S(2)}) collective-permute-start(f32[6,2,16,128]{3,2,1,0:T(8,128)S(1)} %constant_dynamic-update-slice_fusion.own), channel_id=1, source_target_pairs={{0,24},{8,16},{16,8},{24,0},{1,25},{9,17},{17,9},{25,1},{2,26},{10... | collective-permute-start | bytes 294920 | tf_op jit(solution)/shard_map/ppermute | solution.py:244
  22.9 7.1 %collective-permute-start.4 = (f32[6,2,16,128]{3,2,1,0:T(8,128)S(1)}, f32[6,2,16,128]{3,2,1,0:T(8,128)S(1)}, u32[]{:S(2)}, u32[]{:S(2)}) collective-permute-start(f32[6,2,16,128]{3,2,1,0:T(8,128)S(1)} %constant_dynamic-update-slice_fusion.own), channel_id=1, source_target_pairs={{0,16},{8,24},{16,0},{24,8},{1,17},{9,25},{17,1},{25,9},{2,18},{10... | collective-permute-start | bytes 294920 | tf_op jit(solution)/shard_map/ppermute | solution.py:244
  24.3 5.7 %collective-permute-start.3 = (f32[6,2,16,128]{3,2,1,0:T(8,128)S(1)}, f32[6,2,16,128]{3,2,1,0:T(8,128)S(1)}, u32[]{:S(2)}, u32[]{:S(2)}) collective-permute-start(f32[6,2,16,128]{3,2,1,0:T(8,128)S(1)} %constant_dynamic-update-slice_fusion.own), channel_id=1, source_target_pairs={{0,8},{8,0},{16,24},{24,16},{1,9},{9,1},{17,25},{25,17},{2,10},{10... | collective-permute-start | bytes 294920 | tf_op jit(solution)/shard_map/ppermute | solution.py:244
  34.1 3.8 %collective-permute-start.6 = (f32[2,16,16]{2,1,0:T(8,128)S(1)}, f32[2,16,16]{2,1,0:T(8,128)S(1)}, u32[]{:S(2)}, u32[]{:S(2)}) collective-permute-start(f32[2,16,16]{2,1,0:T(8,128)S(1)} %fusion), channel_id=1, source_target_pairs={{0,1},{1,0},{2,3},{3,2},{4,5},{5,4},{6,7},{7,6},{8,9},{9,8},{10,11... | collective-permute-start | bytes 6152 | tf_op jit(solution)/shard_map/ppermute | solution.py:230
  46.8 11.2 %copy-start.3 = (f32[6,2,16,128]{3,2,1,0:T(8,128)}, f32[6,2,16,128]{3,2,1,0:T(8,128)S(1)}, u32[]{:S(2)}) copy-start(f32[6,2,16,128]{3,2,1,0:T(8,128)S(1)} %constant_dynamic-update-slice_fusion.6.own) | copy-start | bytes 294916
  46.8 7.5 %collective-permute-start.9 = (f32[6,2,16,128]{3,2,1,0:T(8,128)S(1)}, f32[6,2,16,128]{3,2,1,0:T(8,128)S(1)}, u32[]{:S(2)}, u32[]{:S(2)}) collective-permute-start(f32[6,2,16,128]{3,2,1,0:T(8,128)S(1)} %constant_dynamic-update-slice_fusion.6.own), channel_id=1, source_target_pairs={{0,6},{2,4},{4,2},{6,0},{1,7},{3,5},{5,3},{7,1},{8,14},{10,12},{12... | collective-permute-start | bytes 294920 | tf_op jit(solution)/shard_map/ppermute | solution.py:244
  48.2 9.0 %collective-permute-start.8 = (f32[6,2,16,128]{3,2,1,0:T(8,128)S(1)}, f32[6,2,16,128]{3,2,1,0:T(8,128)S(1)}, u32[]{:S(2)}, u32[]{:S(2)}) collective-permute-start(f32[6,2,16,128]{3,2,1,0:T(8,128)S(1)} %constant_dynamic-update-slice_fusion.6.own), channel_id=1, source_target_pairs={{0,4},{2,6},{4,0},{6,2},{1,5},{3,7},{5,1},{7,3},{8,12},{10,14},{12... | collective-permute-start | bytes 294920 | tf_op jit(solution)/shard_map/ppermute | solution.py:244
  48.3 8.9 %collective-permute-start.7 = (f32[6,2,16,128]{3,2,1,0:T(8,128)S(1)}, f32[6,2,16,128]{3,2,1,0:T(8,128)S(1)}, u32[]{:S(2)}, u32[]{:S(2)}) collective-permute-start(f32[6,2,16,128]{3,2,1,0:T(8,128)S(1)} %constant_dynamic-update-slice_fusion.6.own), channel_id=1, source_target_pairs={{0,2},{2,0},{4,6},{6,4},{1,3},{3,1},{5,7},{7,5},{8,10},{10,8},{12,... | collective-permute-start | bytes 294920 | tf_op jit(solution)/shard_map/ppermute | solution.py:244

commit v2 on v1

v2 whole, which is shorter than its diff:
```python
import functools

import jax
import jax.numpy as jnp
from jax import lax
from jax.experimental import pallas as pl
from jax.experimental.pallas import tpu as pltpu
from jax.sharding import PartitionSpec as P

RATIOS = (1.0, 0.8)
F32 = jnp.float32


def vmem():
    return pl.BlockSpec(memory_space=pltpu.VMEM)


def call(kernel, outs, *args, scratch=(), flops=400000, space=pltpu.VMEM):
    size = sum(4 * a.size for a in args)
    return pl.pallas_call(
        kernel,
        out_shape=tuple(jax.ShapeDtypeStruct(s, F32) for s in outs),
        in_specs=[pl.BlockSpec(memory_space=space)] * len(args),
        out_specs=tuple(vmem() for _ in outs),
        scratch_shapes=list(scratch),
        compiler_params=pltpu.CompilerParams(vmem_limit_bytes=8 << 20),
        cost_estimate=pl.CostEstimate(flops=flops, bytes_accessed=size, transcendentals=0),
    )(*args)


def factor(n, lat, half_cfl, ratio, inv_out, mid_out, up_out, first_out, last_out):
    ups, firsts = [], []
    up = first = None
    for k in range(n):
        lateral = ratio * lat(k)
        half = half_cfl(k)
        east, west = lateral - half, lateral + half
        pivot = 1.0 + 2.0 * lateral
        if k:
            pivot = pivot - west * up
        inverse = 1.0 / pivot
        mid = west * inverse
        up = east * inverse
        first = mid if k == 0 else mid * first
        inv_out(k, inverse)
        mid_out(k, mid)
        up_out(k, up)
        ups.append(up)
        firsts.append(first)
    q, r = firsts[-1], ups[-1]
    first_out(n - 1, q)
    last_out(n - 1, r)
    q2, r2 = q, r
    for k in range(n - 2, -1, -1):
        q = firsts[k] + ups[k] * q
        r = ups[k] * r
        first_out(k, q)
        last_out(k, r)
    return q, q2, r, r2


def sweep(n, rhs, inv, mid, up, out):
    values = []
    value = None
    for k in range(n):
        value = inv(k) * rhs(k) if k == 0 else inv(k) * rhs(k) + mid(k) * value
        values.append(value)
    out(n - 1, value)
    last = value
    for k in range(n - 2, -1, -1):
        value = values[k] + up(k) * value
        out(k, value)
    return value, last


def along(port, before):
    p1, p2, q1, q2, r1, r2 = port
    source, slope = before
    t = 1.0 / (1.0 - q1 * slope)
    step = q2 * slope * t
    return p2 + q2 * source + step * (p1 + q1 * source), r2 + step * r1


def mirrored(port):
    p1, p2, q1, q2, r1, r2 = port
    return p2, p1, r2, r1, q2, q1


def pick(flag, a, b):
    return tuple(jnp.where(flag, x, y) for x, y in zip(a, b))


def beside(port, left, right):
    p1, p2, q1, q2, r1, r2 = port
    pl_, ql = left
    pr, qr = right
    a1 = p1 + q1 * pl_ + r1 * pr
    a2 = p2 + q2 * pl_ + r2 * pr
    b11, b22 = 1.0 - q1 * ql, 1.0 - r2 * qr
    b12, b21 = r1 * qr, q2 * ql
    t = 1.0 / (b11 * b22 - b12 * b21)
    u1 = (a1 * b22 + b12 * a2) * t
    u2 = (b11 * a2 + b21 * a1) * t
    return pl_ + ql * u1, pr + qr * u2


def place(axis):
    me = lax.axis_index(axis)
    second = me // 2
    return second == 1, second == me % 2, me % 2


def oriented(axis, ends, coefs, f):
    port = tuple(ends) + tuple(coefs[v, f] for v in range(4))
    return pick(place(axis)[0], mirrored(port), port)


def pair_source(axis, f, ends, own, near):
    outer = place(axis)[1]
    zero = jnp.zeros_like(ends[0])
    mine = oriented(axis, ends, own, f)
    other = oriented(axis, (zero, zero), near, f)
    q1, q2, r1, r2 = pick(outer, other[2:], mine[2:])
    slope = jnp.where(outer, mine[5], other[5])
    step = q2 / (1.0 - q1 * slope)
    part = jnp.where(outer, step * mine[1], mine[1] + step * slope * mine[0])
    return part, r2 + step * slope * r1


def pair_whole(axis, f, ends, near_ends, own, near):
    outer = place(axis)[1]
    mine = oriented(axis, ends, own, f)
    other = oriented(axis, near_ends, near, f)
    first, then = pick(outer, mine, other), pick(outer, other, mine)
    return along(then, (first[1], first[5]))


def pair_values(axis, f, ends, near_ends, own, near, far):
    second, outer, _ = place(axis)
    zero = jnp.zeros_like(ends[0])
    mine = oriented(axis, ends, own, f)
    other = oriented(axis, near_ends, near, f)
    ahead = pick(outer, along(mirrored(other), far), far)
    behind = pick(outer, (zero, zero), (other[1], other[5]))
    back, front = beside(mine, behind, ahead)
    return pick(second, (front, back), (back, front))


def scan_values(axis, f, blocks, ends, own, ports):
    me, n = lax.axis_index(axis), lax.axis_size(axis)
    mine = tuple(ends) + tuple(own[v, f] for v in range(4))
    zero = jnp.zeros_like(mine[0])

    def port_of(j):
        return tuple(ports[j, 2 * f + v] for v in range(2)) + tuple(
            ports[j, 2 * blocks + blocks * v + f] for v in range(4)
        )

    def step(j, sides):
        left, right = sides
        left = pick(j < me, along(port_of(j), left), left)
        i = n - 1 - j
        right = pick(i > me, along(mirrored(port_of(i)), right), right)
        return left, right

    left, right = lax.fori_loop(0, n, step, ((zero, zero), (zero, zero)))
    return beside(mine, left, right)


def everyones(axis, ends, own):
    blocks = own.shape[1]
    return lax.all_gather(
        jnp.concatenate([ends, own.reshape((4 * blocks,) + own.shape[2:])]), axis
    )


def swap(value, axis, k):
    return lax.ppermute(value, axis, [(i, i ^ k) for i in range(lax.axis_size(axis))])


PLANES = ("load", "lat", "up", "cx", "cy", "cz")


def open_kernel(nx, nz, *refs):
    ins, outs, tiles, sems = refs[:8], refs[8:16], refs[16], refs[17]
    copies = [pltpu.make_async_copy(a, b, sems.at[i]) for i, (a, b) in enumerate(zip(ins, outs))]
    for copy in copies:
        copy.start()
    upper = lax.axis_index("gz")
    edge, inner = 1 - upper, 2 - 3 * upper
    planes = [(0, edge), (1, edge), (0, inner), (1, inner)] + [(i, edge) for i in range(2, 8)]
    per_tile = nz // nx
    arrived = set()
    lane = lax.broadcasted_iota(jnp.int32, outs[0].shape[1:], 1)
    for first in range(0, len(planes), per_tile):
        tile = jnp.zeros(outs[0].shape[1:], F32)
        for a, (i, offset) in enumerate(planes[first : first + per_tile]):
            if i not in arrived:
                copies[i].wait()
                arrived.add(i)
            for k in range(nx):
                to = nx * a + k
                shift = lax.rem(offset + (to + nz), nz)
                tile = jnp.where(lane == to, pltpu.roll(outs[i][k], shift, 1), tile)
        tiles[first // per_tile] = tile


def put(ref, f):
    def store(k, v):
        ref[f, k] = v

    return store


def coef_kernel(nx, ny, t, h, lat, cx, cy, xi, xm, xu, xq, xr, yi, ym, yu, yq, yr, xown, yown, one, two):
    even = lax.axis_index("gy") % 2 == 0
    for f, (ratio, ref) in enumerate(zip(RATIOS, (t, h))):
        low = ref[pl.ds(0, nx, stride=ny), :]
        high = ref[pl.ds(ny - 1, nx, stride=ny), :]
        one[f] = jnp.where(even, high, low)
        two[f] = jnp.where(even, low, high)
    for f, ratio in enumerate(RATIOS):
        own = factor(
            nx,
            lambda k: lat[pl.ds(k * ny, ny), :],
            lambda k: 0.5 * cx[pl.ds(k * ny, ny), :],
            ratio,
            *(put(ref, f) for ref in (xi, xm, xu, xq, xr)),
        )
        for v in range(4):
            xown[v, f] = own[v]
        own = factor(
            ny,
            lambda k: lat[pl.ds(k, nx, stride=ny), :],
            lambda k: 0.5 * cy[pl.ds(k, nx, stride=ny), :],
            ratio,
            *(put(ref, f) for ref in (yi, ym, yu, yq, yr)),
        )
        for v in range(4):
            yown[v, f] = own[v]
            one[2 + 2 * v + f] = own[v]


class Ghost:
    def __init__(self, shape, nx):
        self.shape, self.nx = shape, nx
        self.first = lax.broadcasted_iota(jnp.int32, shape, 1) < shape[1] // 2
        self.ratio = jnp.where(self.first, RATIOS[0], RATIOS[1])

    def lane(self, tiles, plane, k):
        at = self.nx * plane + k
        column = tiles[at // self.shape[1], :, at % self.shape[1] : at % self.shape[1] + 1]
        return jnp.broadcast_to(column, self.shape)

    def fields(self, tiles, plane, k):
        return jnp.where(self.first, self.lane(tiles, plane, k), self.lane(tiles, plane + 1, k))

    def named(self, tiles, name, k):
        return self.lane(tiles, 4 + PLANES.index(name), k)

    def row(self, row, k):
        shape = (1, self.shape[1])
        first = lax.broadcasted_iota(jnp.int32, shape, 1) < shape[1] // 2
        a = jnp.broadcast_to(row[:, k : k + 1], shape)
        b = jnp.broadcast_to(row[:, self.nx + k : self.nx + k + 1], shape)
        return jnp.where(first, a, b)


def ghost_kernel(nx, tiles, xown, gi, gm, gu, gq, gr, own):
    ghost = Ghost(tiles.shape[1:], nx)

    def keep(ref):
        def store(k, v):
            ref[k] = v

        return store

    ports = factor(
        nx,
        lambda k: ghost.named(tiles, "lat", k),
        lambda k: 0.5 * ghost.named(tiles, "cx", k),
        ghost.ratio,
        *(keep(ref) for ref in (gi, gm, gu, gq, gr)),
    )
    for v in range(4):
        own[v, 0] = xown[v, 0]
        own[v, 1] = xown[v, 1]
        own[v, 2] = ports[v]


def lateral_step(v, ahead_row, behind_row, lateral, half):
    ny = v.shape[0]
    row = lax.broadcasted_iota(jnp.int32, v.shape, 0)
    ahead = jnp.where(row == ny - 1, ahead_row, pltpu.roll(v, ny - 1, 0))
    behind = jnp.where(row == 0, behind_row, pltpu.roll(v, 1, 0))
    return (lateral - half) * (ahead - v) + (lateral + half) * (behind - v)


def vertical_step(nz, v, column, lateral, half):
    upper = lax.axis_index("gz")
    lane = lax.broadcasted_iota(jnp.int32, v.shape, 1)
    column = jnp.broadcast_to(column, v.shape)
    ahead = jnp.where(lane == nz - 1, jnp.where(upper == 0, column, 0.0), pltpu.roll(v, nz - 1, 1))
    behind = jnp.where(lane == 0, jnp.where(upper == 0, 0.0, column), pltpu.roll(v, 1, 1))
    return (lateral - half) * (ahead - v) + (lateral + half) * (behind - v)


def first_kernel(
    nx, ny, nz, t, h, load, lat, up, cy, cz, one, two, mine, tiles, xi, xm, xu, gi, gm, gu, d, p, gp, ends
):
    even = lax.axis_index("gy") % 2 == 0
    upper = lax.axis_index("gz")
    last = one.shape[0] - 1
    for f, (ratio, ref) in enumerate(zip(RATIOS, (t, h))):
        low_rows = jnp.where(even, two[f], one[f])
        high_rows = jnp.where(even, one[f], two[f])
        for k in range(nx):
            v = ref[k]
            out = v + lateral_step(
                v, high_rows[k : k + 1], low_rows[k : k + 1], ratio * lat[k], 0.5 * cy[k]
            )
            at = nx * f + k
            out = out + vertical_step(nz, v, tiles[0, :, at : at + 1], ratio * up[k], 0.5 * cz[k])
            if f == 0:
                out = out + load[k]
            d[f, k] = out
        ends[2 * f], ends[2 * f + 1] = sweep(
            nx, lambda k: d[f, k], lambda k: xi[f, k], lambda k: xm[f, k], lambda k: xu[f, k], put(p, f)
        )
    ghost = Ghost(tiles.shape[1:], nx)
    low_row = jnp.where(even, two[2], one[last])[ny - 1 : ny]
    high_row = jnp.where(even, one[last], two[2])[0:1]
    sides = []
    for k in range(nx):
        v = ghost.fields(tiles, 0, k)
        out = v + lateral_step(
            v,
            ghost.row(high_row, k),
            ghost.row(low_row, k),
            ghost.ratio * ghost.named(tiles, "lat", k),
            0.5 * ghost.named(tiles, "cy", k),
        )
        inner, here = ghost.fields(tiles, 2, k), ghost.fields(mine, 0, k)
        ahead, behind = jnp.where(upper == 0, inner, here), jnp.where(upper == 0, here, inner)
        lateral, half = ghost.ratio * ghost.named(tiles, "up", k), 0.5 * ghost.named(tiles, "cz", k)
        out = out + ((lateral - half) * (ahead - v) + (lateral + half) * (behind - v))
        sides.append(out + jnp.where(ghost.first, ghost.named(tiles, "load", k), 0.0))

    def keep(k, v):
        gp[k] = v

    ends[4], ends[5] = sweep(
        nx, lambda k: sides[k], lambda k: gi[k], lambda k: gm[k], lambda k: gu[k], keep
    )


def pair_kernel(axis, blocks, ends, near_ends, own, near, out):
    for f in range(blocks):
        source, slope = pair_whole(
            axis, f, (ends[2 * f], ends[2 * f + 1]), (near_ends[2 * f], near_ends[2 * f + 1]), own, near
        )
        if f == 2:
            lane = lax.broadcasted_iota(jnp.int32, source.shape, 1)
            out[4] = jnp.where((lane & 32) == 0, source, slope)
        else:
            out[2 * f] = source
            out[2 * f + 1] = slope


def far_word(far, f):
    if f < 2:
        return far[2 * f], far[2 * f + 1]
    both = far[4]
    lane = lax.broadcasted_iota(jnp.int32, both.shape, 1)
    source = jnp.where((lane & 32) == 0, both, pltpu.roll(both, 32, 1))
    slope = jnp.where((lane & 32) == 0, pltpu.roll(both, both.shape[1] - 32, 1), both)
    return source, slope


def second_kernel(
    paired, nx, ny, nz, p, q, r, gp, gq, gr, ends, near_ends, own, near, far,
    d, load, up, cz, yi, ym, yu, yown, ynear, py, *rest,
):
    outs, s = rest[:-1], rest[-1]

    def values(f):
        mine = (ends[2 * f], ends[2 * f + 1])
        if not paired[0]:
            return scan_values("gx", f, 3, mine, own, far)
        other = (near_ends[2 * f], near_ends[2 * f + 1])
        return pair_values("gx", f, mine, other, own, near, far_word(far, f))

    ghost_low, ghost_high = values(2)
    yends, slopes = [], []
    for f, ratio in enumerate(RATIOS):
        low, high = values(f)
        for k in range(nx):
            v = p[f, k] + q[f, k] * low + r[f, k] * high
            beyond = gp[k] + gq[k] * ghost_low + gr[k] * ghost_high
            at = f * nz // 2
            out = 2.0 * v - d[f, k]
            out = out + vertical_step(nz, v, beyond[:, at : at + 1], ratio * up[k], 0.5 * cz[k])
            if f == 0:
                out = out + load[k]
            s[f, pl.ds(k * ny, ny), :] = out
        mine = sweep(
            ny,
            lambda k: s[f, pl.ds(k, nx, stride=ny), :],
            lambda k: yi[f, k],
            lambda k: ym[f, k],
            lambda k: yu[f, k],
            put(py, f),
        )
        outs[0][2 * f], outs[0][2 * f + 1] = mine
        if paired[1]:
            outs[1][f], slope = pair_source("gy", f, mine, yown, ynear)
            slopes.append(slope)
    if paired[1]:
        outs[1][2] = jnp.where(place("gy")[2] == 0, slopes[0], slopes[1])


def new_kernel(paired, nx, ny, p, q, r, ends, near_ends, own, near, *rest):
    received, news = rest[:-2], rest[-2:]
    for f, ref in enumerate(news):
        mine = (ends[2 * f], ends[2 * f + 1])
        if paired:
            other = (near_ends[2 * f], near_ends[2 * f + 1])
            two, three = received
            slope = jnp.where(place("gy")[2] == f, two[2], three[2])
            low, high = pair_values("gy", f, mine, other, own, near, (two[f] + three[f], slope))
        else:
            low, high = scan_values("gy", f, 2, mine, own, received[0])
        for k in range(ny):
            ref[pl.ds(k, nx, stride=ny), :] = p[f, k] + q[f, k] * low + r[f, k] * high


def neighbours(one, two, axis):
    n = lax.axis_size(axis)

    def swapped(first, value):
        pairs = [(i, i + 1) for i in range(first, n - 1, 2)]
        if not pairs:
            return jnp.zeros_like(value)
        return lax.ppermute(value, axis, pairs + [(b, a) for a, b in pairs])

    return swapped(0, one), swapped(1, two)


def body(thermal, vapour, load, lat, up, cx, cy, cz):
    nx, ny, nz = thermal.shape
    assert lax.axis_size("gz") == 2 and nx * 8 == nz
    flat = (nx * ny, nz)
    lines_x, lines_y = (2, nx, ny, nz), (2, ny, nx, nz)
    block_x, block_y = (ny, nz), (nx, nz)
    paired = (lax.axis_size("gx") == 4, lax.axis_size("gy") == 4)
    thermal, vapour, load, lat, up, cx, cy, cz, mine = call(
        functools.partial(open_kernel, nx, nz),
        (thermal.shape,) * 8 + ((2,) + block_x,),
        *(
            pltpu.with_memory_space_constraint(a, pltpu.HBM)
            for a in (thermal, vapour, load, lat, up, cx, cy, cz)
        ),
        scratch=[pltpu.SemaphoreType.DMA((8,))],
        space=pltpu.HBM,
    )
    tiles = swap(mine, "gz", 1)
    xi, xm, xu, xq, xr, yi, ym, yu, yq, yr, xown, yown, one, two = call(
        functools.partial(coef_kernel, nx, ny),
        (lines_x,) * 5
        + (lines_y,) * 5
        + ((4, 2) + block_x, (4, 2) + block_y, (10,) + block_y, (2,) + block_y),
        *(a.reshape(flat) for a in (thermal, vapour, lat, cx, cy)),
    )
    one = one if paired[1] else one[:2]
    one, two = neighbours(
        jnp.concatenate([one, tiles[:1]]), jnp.concatenate([two, tiles[:1]]), "gy"
    )
    ynear = one[2:10].reshape(yown.shape) if paired[1] else yown
    gi, gm, gu, gq, gr, own = call(
        functools.partial(ghost_kernel, nx),
        ((nx,) + block_x,) * 5 + ((4, 3) + block_x,),
        tiles, xown,
    )
    near = swap(own, "gx", 1) if paired[0] else own
    d, p, gp, ends = call(
        functools.partial(first_kernel, nx, ny, nz),
        (lines_x, lines_x, (nx,) + block_x, (6,) + block_x),
        thermal, vapour, load, lat, up, cy, cz, one, two, mine, tiles, xi, xm, xu, gi, gm, gu,
    )
    if paired[0]:
        near_ends = swap(ends, "gx", 1)
        (word,) = call(
            functools.partial(pair_kernel, "gx", 3), ((5,) + block_x,), ends, near_ends, own, near
        )
        far = swap(word, "gx", 2)
    else:
        near_ends, far = ends, everyones("gx", ends, own)
    py, yends, *outs = call(
        functools.partial(second_kernel, paired, nx, ny, nz),
        (lines_y, (4,) + block_y) + (((3,) + block_y,) if paired[1] else ()),
        p, xq, xr, gp, gq, gr, ends, near_ends, own, near, far,
        d, load, up, cz, yi, ym, yu, yown, ynear,
        scratch=[pltpu.VMEM((2,) + flat, F32)],
    )
    if paired[1]:
        near_ends = swap(yends, "gy", 1)
        received = [swap(outs[0], "gy", 2), swap(outs[0], "gy", 3)]
    else:
        near_ends, received = yends, [everyones("gy", yends, yown)]
    t_new, h_new = call(
        functools.partial(new_kernel, paired[1], nx, ny),
        (flat, flat),
        py, yq, yr, yends, near_ends, yown, ynear, *received,
    )
    return t_new.reshape(thermal.shape), h_new.reshape(thermal.shape)


def solution(mesh):
    spec = P("gx", "gy", "gz")
    return jax.shard_map(
        body, mesh=mesh, in_specs=(spec,) * 8, out_specs=(spec, spec), check_vma=False
    )
```

time: 61 us -> 31.8 us (0.52); the launches traced: 60.1 us -> 31.6 us
  local copies, waits for them, and re-layouts: 12.5 us -> 0.01 us
  Pallas kernels: 12.4 us -> 4.91 us
  other arithmetic: 4.86 us -> 0.01 us
  waiting for transfers between devices: 14.6 us -> 10.3 us
  starting transfers between devices: 15 us -> 15.7 us
    pallas_call x5 -> x7, Pallas kernels: 12.4 us -> 4.91 us  [call(): pl.pallas_call(kernel, out_shape=tuple((jax.ShapeDtypeStruct(s, F32) for...]
    unnamed x18 -> x0, local copies, waits for them, and re-layouts: 7.21 us -> none
    ppermute x10 -> x9, waiting for transfers between devices: 14.6 us -> 10.3 us  [the longest x7 8.77 us: swap(): lax.ppermute(value, axis, [(i, i ^ k) for i in range(lax.axis_size(axis))])]
    broadcast_in_dim x4 -> x0, local copies, waits for them, and re-layouts: 3.87 us -> none  [the longest x2 1.94 us: body(): zlo[..., None]]
    select_n x5 -> x0, other arithmetic: 3.3 us -> none  [the longest x3 2.68 us: neighbours(): jnp.where(even, high_face, low_face)]
    another operation x2 -> x0, other arithmetic: 1.54 us -> none  [everyones(): return (by_xor, jnp.stack(parts))]
    another operation x2 -> x0, local copies, waits for them, and re-layouts: 1.44 us -> none  [the longest x1 0.72 us: body(): jnp.stack([p[:, 0], p[:, -1], yq[:, 0], yq[:, -1], yr[:, 0], yr[:, -1]])]
    ppermute x10 -> x9, starting transfers between devices: 15 us -> 15.7 us  [the longest x7 12.9 us: swap(): lax.ppermute(value, axis, [(i, i ^ k) for i in range(lax.axis_size(axis))])]
  transfers between devices with their start and end apart: 10 -> 9, of which waited for: 5 -> 6; matrix products, arithmetic and copies ran while one was open for 3% -> 0% of each run, Pallas kernels for 5% -> 5%
where the time goes in v2:
time: 31.8 us; the launch traced here: 31.6 us
  starting transfers between devices  15.7 us (49%)
  waiting for transfers between devices  10.3 us (32%)
  Pallas kernels  4.91 us (15%)
  between operations  0.71 us (2%)
    ppermute x7, starting transfers between devices, swap(): lax.ppermute(value, axis, [(i, i ^ k) for i in range(lax.axis_size(axis))])  12.9 us
    ppermute x7, waiting for transfers between devices, swap(): lax.ppermute(value, axis, [(i, i ^ k) for i in range(lax.axis_size(axis))])  8.77 us
    pallas_call x7, Pallas kernels, call(): pl.pallas_call(kernel, out_shape=tuple((jax.ShapeDtypeStruct(s, F32) for...  4.91 us
    ppermute x2, starting transfers between devices, swapped(): return lax.ppermute(value, axis, pairs + [(b, a) for a, b in pairs])  2.83 us
    ppermute x2, waiting for transfers between devices, swapped(): return lax.ppermute(value, axis, pairs + [(b, a) for a, b in pairs])  1.49 us
  transfers between devices with their start and end apart: 9, of which 6 were waited for; matrix products, arithmetic and copies ran while one was open for 0% of the time, Pallas kernels for 5%

profile of v2, /device:TPU:0, one launch (start us, length us, event | category | flops | bytes accessed | tf_op | source)
XLA Modules:
  0.0 31.6 jit_solution(10743342666823564905)
XLA Ops:
  0.6 1.9 %shard_map.95 = (f32[16,16,128]{2,1,0:T(8,128)S(1)}, f32[16,16,128]{2,1,0:T(8,128)S(1)}, f32[16,16,128]{2,1,0:T(8,128)S(1)}, f32[16,16,128]{2,1,0:T(8,128)S(1)},...) custom-call(f32[16,16,128]{2,1,0:T(8,128)} %refs_0_.1, ...), custom_call_target="tpu_custom_call" | custom-call | flops 400000 | bytes 1048576 | tf_op jit(solution)/shard_map/pallas_call | solution.py:20
  2.5 3.0 %collective-permute-start = (f32[2,16,128]{2,1,0:T(8,128)S(1)}, f32[2,16,128]{2,1,0:T(8,128)S(1)}, u32[]{:S(2)}, u32[]{:S(2)}) collective-permute-start(f32[2,16,128]{2,1,0:T(8,128)S(1)} %get-tuple-element.49.mine), channel_id=1, source_target_pairs={{0,1},{1,0},{2,3},{3,2},{4,5},{5,4},{6,7},{7,6},{8,9},{9,8},{10,11... | collective-permute-start | bytes 49160 | tf_op jit(solution)/shard_map/ppermute | solution.py:178
  5.5 0.4 %shard_map.96 = (f32[2,16,16,128]{3,2,1,0:T(8,128)S(1)}, f32[2,16,16,128]{3,2,1,0:T(8,128)S(1)}, f32[2,16,16,128]{3,2,1,0:T(8,128)S(1)}, f32[2,16,16,128]{3,2,1,...) custom-call(f32[256,128]{1,0:T(8,128)S(1)} %bitcast.10, ...), custom_call_target="tpu_custom_call" | custom-call | flops 400000 | bytes 655360 | tf_op jit(solution)/shard_map/pallas_call | solution.py:20
  6.0 1.3 %collective-permute-done.tiles = f32[2,16,128]{2,1,0:T(8,128)S(1)} collective-permute-done((f32[2,16,128]{2,1,0:T(8,128)S(1)}, f32[2,16,128]{2,1,0:T(8,128)S(1)}, u32[]{:S(2)}, u32[]{:S(2)}) %collective-permute-start) | collective-permute-done | bytes 16416 | tf_op jit(solution)/shard_map/ppermute | solution.py:178
  7.3 2.2 %collective-permute-start.1 = (f32[11,16,128]{2,1,0:T(8,128)S(1)}, f32[11,16,128]{2,1,0:T(8,128)S(1)}, u32[]{:S(2)}, u32[]{:S(2)}) collective-permute-start(f32[11,16,128]{2,1,0:T(8,128)S(1)} %pad_maximum_fusion), channel_id=1, source_target_pairs={{0,2},{4,6},{2,0},{6,4},{1,3},{5,7},{3,1},{7,5},{8,10},{12,14},{10... | collective-permute-start | bytes 270344 | tf_op jit(solution)/shard_map/ppermute | solution.py:444
  9.4 0.2 shard_map.97
  9.7 0.1 collective-permute-start.4
  9.8 0.7 %collective-permute-start.2 = (f32[3,16,128]{2,1,0:T(8,128)S(1)}, f32[3,16,128]{2,1,0:T(8,128)S(1)}, u32[]{:S(2)}, u32[]{:S(2)}) collective-permute-start(f32[3,16,128]{2,1,0:T(8,128)S(1)} %pad_maximum_fusion.1), channel_id=1, source_target_pairs={{2,4},{4,2},{3,5},{5,3},{10,12},{12,10},{11,13},{13,11},{18,20},{2... | collective-permute-start | bytes 73736 | tf_op jit(solution)/shard_map/ppermute | solution.py:444
  10.5 0.0 collective-permute-done.2.two
  10.5 1.5 %collective-permute-done.1.one = f32[11,16,128]{2,1,0:T(8,128)S(1)} collective-permute-done((f32[11,16,128]{2,1,0:T(8,128)S(1)}, f32[11,16,128]{2,1,0:T(8,128)S(1)}, u32[]{:S(2)}, u32[]{:S(2)}) %collective-permute-start.1) | collective-permute-done | bytes 90144 | tf_op jit(solution)/shard_map/ppermute | solution.py:444
  12.0 1.1 %shard_map.98 = (f32[2,16,16,128]{3,2,1,0:T(8,128)S(1)}, f32[2,16,16,128]{3,2,1,0:T(8,128)S(1)}, f32[16,16,128]{2,1,0:T(8,128)S(1)}, f32[6,16,128]{2,1,0:T(8,128)S(1)}) custom-call(f32[16,16,128]{2,1,0:T(8,128)S(1)} %get-tuple-element.40.t, f32[16,16,128]{2,1,0:T(8,128)S(1)} %get-tuple-element.41.h, f32[16,16,128]{2,1,0:T(8,128)S(1)} %get-tuple-element.42.load, ...), custom_call_target="tpu_custom_call" | custom-call | flops 400000 | bytes 2244608 | tf_op jit(solution)/shard_map/pallas_call | solution.py:20
  13.0 0.1 collective-permute-start.3
  13.1 0.0 collective-permute-done.4.near
  13.1 1.2 %collective-permute-done.3.near_ends = f32[6,16,128]{2,1,0:T(8,128)S(1)} collective-permute-done((f32[6,16,128]{2,1,0:T(8,128)S(1)}, f32[6,16,128]{2,1,0:T(8,128)S(1)}, u32[]{:S(2)}, u32[]{:S(2)}) %collective-permute-start.3) | collective-permute-done | bytes 49184 | tf_op jit(solution)/shard_map/ppermute | solution.py:178
  14.4 2.0 %collective-permute-start.5 = (f32[5,16,128]{2,1,0:T(8,128)S(1)}, f32[5,16,128]{2,1,0:T(8,128)S(1)}, u32[]{:S(2)}, u32[]{:S(2)}) collective-permute-start(f32[5,16,128]{2,1,0:T(8,128)S(1)} %shard_map.99), channel_id=1, source_target_pairs={{0,16},{8,24},{16,0},{24,8},{1,17},{9,25},{17,1},{25,9},{2,18},{10... | collective-permute-start | bytes 122888 | tf_op jit(solution)/shard_map/ppermute | solution.py:178
  16.4 2.0 %collective-permute-done.5.far = f32[5,16,128]{2,1,0:T(8,128)S(1)} collective-permute-done((f32[5,16,128]{2,1,0:T(8,128)S(1)}, f32[5,16,128]{2,1,0:T(8,128)S(1)}, u32[]{:S(2)}, u32[]{:S(2)}) %collective-permute-start.5) | collective-permute-done | bytes 40992 | tf_op jit(solution)/shard_map/ppermute | solution.py:178
  18.4 0.5 %shard_map.100 = (f32[2,16,16,128]{3,2,1,0:T(8,128)S(1)}, f32[4,16,128]{2,1,0:T(8,128)S(1)}, f32[3,16,128]{2,1,0:T(8,128)S(1)}) custom-call(f32[2,16,16,128]{3,2,1,0:T(8,128)S(1)} %get-tuple-element.58.p, f32[2,16,16,128]{3,2,1,0:T(8,128)S(1)} %get-tuple-element.59.q, f32[2,16,16,128]{3,2,1,0:T(8,128)S(1)} %get-tuple-element.60.r, ...), custom_call_target="tpu_custom_call" | custom-call | flops 400000 | bytes 3088384 | tf_op jit(solution)/shard_map/pallas_call | solution.py:20
  18.9 4.8 %collective-permute-start.6 = (f32[4,16,128]{2,1,0:T(8,128)S(1)}, f32[4,16,128]{2,1,0:T(8,128)S(1)}, u32[]{:S(2)}, u32[]{:S(2)}) collective-permute-start(f32[4,16,128]{2,1,0:T(8,128)S(1)} %get-tuple-element.74.ends), channel_id=1, source_target_pairs={{0,2},{2,0},{4,6},{6,4},{1,3},{3,1},{5,7},{7,5},{8,10},{10,8},{12,... | collective-permute-start | bytes 98312 | tf_op jit(solution)/shard_map/ppermute | solution.py:178
  23.7 1.5 %collective-permute-start.7 = (f32[3,16,128]{2,1,0:T(8,128)S(1)}, f32[3,16,128]{2,1,0:T(8,128)S(1)}, u32[]{:S(2)}, u32[]{:S(2)}) collective-permute-start(f32[3,16,128]{2,1,0:T(8,128)S(1)} %get-tuple-element.75), channel_id=1, source_target_pairs={{0,4},{2,6},{4,0},{6,2},{1,5},{3,7},{5,1},{7,3},{8,12},{10,14},{12... | collective-permute-start | bytes 73736 | tf_op jit(solution)/shard_map/ppermute | solution.py:178
  25.2 1.4 %collective-permute-start.8 = (f32[3,16,128]{2,1,0:T(8,128)S(1)}, f32[3,16,128]{2,1,0:T(8,128)S(1)}, u32[]{:S(2)}, u32[]{:S(2)}) collective-permute-start(f32[3,16,128]{2,1,0:T(8,128)S(1)} %get-tuple-element.75), channel_id=1, source_target_pairs={{0,6},{2,4},{4,2},{6,0},{1,7},{3,5},{5,3},{7,1},{8,14},{10,12},{12... | collective-permute-start | bytes 73736 | tf_op jit(solution)/shard_map/ppermute | solution.py:178
  26.6 2.0 %collective-permute-done.7.rest_0_ = f32[3,16,128]{2,1,0:T(8,128)S(1)} collective-permute-done((f32[3,16,128]{2,1,0:T(8,128)S(1)}, f32[3,16,128]{2,1,0:T(8,128)S(1)}, u32[]{:S(2)}, u32[]{:S(2)}) %collective-permute-start.7) | collective-permute-done | bytes 24608 | tf_op jit(solution)/shard_map/ppermute | solution.py:178
  28.5 2.3 %collective-permute-done.8.rest_1_ = f32[3,16,128]{2,1,0:T(8,128)S(1)} collective-permute-done((f32[3,16,128]{2,1,0:T(8,128)S(1)}, f32[3,16,128]{2,1,0:T(8,128)S(1)}, u32[]{:S(2)}, u32[]{:S(2)}) %collective-permute-start.8) | collective-permute-done | bytes 24608 | tf_op jit(solution)/shard_map/ppermute | solution.py:178
  30.8 0.0 collective-permute-done.6.near_ends
  30.8 0.8 %shard_map.101 = (f32[256,128]{1,0:T(8,128)}, f32[256,128]{1,0:T(8,128)}) custom-call(f32[2,16,16,128]{3,2,1,0:T(8,128)S(1)} %get-tuple-element.71.p, f32[2,16,16,128]{3,2,1,0:T(8,128)S(1)} %get-tuple-element.72.q, f32[2,16,16,128]{3,2,1,0:T(8,128)S(1)} %get-tuple-element.73.r, f32[4,16,128]{2,1,0:T(8,128)S(1)} %get-tuple-element.74.ends, ...), custom_call_target="tpu_custom_call" | custom-call | flops 400000 | bytes 1032192 | tf_op jit(solution)/shard_map/pallas_call | solution.py:20
  (5 shorter events, 0.1 us)
Async XLA Ops:
  2.5 4.8 %collective-permute-start = (f32[2,16,128]{2,1,0:T(8,128)S(1)}, f32[2,16,128]{2,1,0:T(8,128)S(1)}, u32[]{:S(2)}, u32[]{:S(2)}) collective-permute-start(f32[2,16,128]{2,1,0:T(8,128)S(1)} %get-tuple-element.49.mine), channel_id=1, source_target_pairs={{0,1},{1,0},{2,3},{3,2},{4,5},{5,4},{6,7},{7,6},{8,9},{9,8},{10,11... | collective-permute-start | bytes 49160 | tf_op jit(solution)/shard_map/ppermute | solution.py:178
  7.3 4.7 %collective-permute-start.1 = (f32[11,16,128]{2,1,0:T(8,128)S(1)}, f32[11,16,128]{2,1,0:T(8,128)S(1)}, u32[]{:S(2)}, u32[]{:S(2)}) collective-permute-start(f32[11,16,128]{2,1,0:T(8,128)S(1)} %pad_maximum_fusion), channel_id=1, source_target_pairs={{0,2},{4,6},{2,0},{6,4},{1,3},{5,7},{3,1},{7,5},{8,10},{12,14},{10... | collective-permute-start | bytes 270344 | tf_op jit(solution)/shard_map/ppermute | solution.py:444
  9.7 3.4 %collective-permute-start.4 = (f32[4,3,16,128]{3,2,1,0:T(8,128)S(1)}, f32[4,3,16,128]{3,2,1,0:T(8,128)S(1)}, u32[]{:S(2)}, u32[]{:S(2)}) collective-permute-start(f32[4,3,16,128]{3,2,1,0:T(8,128)S(1)} %get-tuple-element.65.own), channel_id=1, source_target_pairs={{0,8},{8,0},{16,24},{24,16},{1,9},{9,1},{17,25},{25,17},{2,10},{10... | collective-permute-start | bytes 294920 | tf_op jit(solution)/shard_map/ppermute | solution.py:178
  9.8 0.7 %collective-permute-start.2 = (f32[3,16,128]{2,1,0:T(8,128)S(1)}, f32[3,16,128]{2,1,0:T(8,128)S(1)}, u32[]{:S(2)}, u32[]{:S(2)}) collective-permute-start(f32[3,16,128]{2,1,0:T(8,128)S(1)} %pad_maximum_fusion.1), channel_id=1, source_target_pairs={{2,4},{4,2},{3,5},{5,3},{10,12},{12,10},{11,13},{13,11},{18,20},{2... | collective-permute-start | bytes 73736 | tf_op jit(solution)/shard_map/ppermute | solution.py:444
  13.0 1.3 %collective-permute-start.3 = (f32[6,16,128]{2,1,0:T(8,128)S(1)}, f32[6,16,128]{2,1,0:T(8,128)S(1)}, u32[]{:S(2)}, u32[]{:S(2)}) collective-permute-start(f32[6,16,128]{2,1,0:T(8,128)S(1)} %get-tuple-element.64.ends), channel_id=1, source_target_pairs={{0,8},{8,0},{16,24},{24,16},{1,9},{9,1},{17,25},{25,17},{2,10},{10... | collective-permute-start | bytes 147464 | tf_op jit(solution)/shard_map/ppermute | solution.py:178
  14.4 4.1 %collective-permute-start.5 = (f32[5,16,128]{2,1,0:T(8,128)S(1)}, f32[5,16,128]{2,1,0:T(8,128)S(1)}, u32[]{:S(2)}, u32[]{:S(2)}) collective-permute-start(f32[5,16,128]{2,1,0:T(8,128)S(1)} %shard_map.99), channel_id=1, source_target_pairs={{0,16},{8,24},{16,0},{24,8},{1,17},{9,25},{17,1},{25,9},{2,18},{10... | collective-permute-start | bytes 122888 | tf_op jit(solution)/shard_map/ppermute | solution.py:178
  18.9 11.9 %collective-permute-start.6 = (f32[4,16,128]{2,1,0:T(8,128)S(1)}, f32[4,16,128]{2,1,0:T(8,128)S(1)}, u32[]{:S(2)}, u32[]{:S(2)}) collective-permute-start(f32[4,16,128]{2,1,0:T(8,128)S(1)} %get-tuple-element.74.ends), channel_id=1, source_target_pairs={{0,2},{2,0},{4,6},{6,4},{1,3},{3,1},{5,7},{7,5},{8,10},{10,8},{12,... | collective-permute-start | bytes 98312 | tf_op jit(solution)/shard_map/ppermute | solution.py:178
  23.7 4.8 %collective-permute-start.7 = (f32[3,16,128]{2,1,0:T(8,128)S(1)}, f32[3,16,128]{2,1,0:T(8,128)S(1)}, u32[]{:S(2)}, u32[]{:S(2)}) collective-permute-start(f32[3,16,128]{2,1,0:T(8,128)S(1)} %get-tuple-element.75), channel_id=1, source_target_pairs={{0,4},{2,6},{4,0},{6,2},{1,5},{3,7},{5,1},{7,3},{8,12},{10,14},{12... | collective-permute-start | bytes 73736 | tf_op jit(solution)/shard_map/ppermute | solution.py:178
  25.2 5.6 %collective-permute-start.8 = (f32[3,16,128]{2,1,0:T(8,128)S(1)}, f32[3,16,128]{2,1,0:T(8,128)S(1)}, u32[]{:S(2)}, u32[]{:S(2)}) collective-permute-start(f32[3,16,128]{2,1,0:T(8,128)S(1)} %get-tuple-element.75), channel_id=1, source_target_pairs={{0,6},{2,4},{4,2},{6,0},{1,7},{3,5},{5,3},{7,1},{8,14},{10,12},{12... | collective-permute-start | bytes 73736 | tf_op jit(solution)/shard_map/ppermute | solution.py:178

commit v3 on v2

--- a/solution.py
+++ b/solution.py
@@ -7,6 +7,7 @@
 from jax.experimental.pallas import tpu as pltpu
 from jax.sharding import PartitionSpec as P
 
+
 RATIOS = (1.0, 0.8)
 F32 = jnp.float32
 
@@ -17,6 +18,10 @@
 
 def call(kernel, outs, *args, scratch=(), flops=400000, space=pltpu.VMEM):
     size = sum(4 * a.size for a in args)
+    return run(kernel, outs, args, scratch, flops, size, space)
+
+
+def run(kernel, outs, args, scratch, flops, size, space):
     return pl.pallas_call(
         kernel,
         out_shape=tuple(jax.ShapeDtypeStruct(s, F32) for s in outs),
@@ -193,15 +198,17 @@
     arrived = set()
     lane = lax.broadcasted_iota(jnp.int32, outs[0].shape[1:], 1)
     for first in range(0, len(planes), per_tile):
-        tile = jnp.zeros(outs[0].shape[1:], F32)
+        tile = None
         for a, (i, offset) in enumerate(planes[first : first + per_tile]):
             if i not in arrived:
                 copies[i].wait()
                 arrived.add(i)
+            plane = None
             for k in range(nx):
                 to = nx * a + k
-                shift = lax.rem(offset + (to + nz), nz)
-                tile = jnp.where(lane == to, pltpu.roll(outs[i][k], shift, 1), tile)
+                moved = pltpu.roll(outs[i][k], lax.rem(offset + (to + nz), nz), 1)
+                plane = moved if k == 0 else jnp.where(lane == to, moved, plane)
+            tile = plane if a == 0 else jnp.where(lane < nx * a, tile, plane)
         tiles[first // per_tile] = tile
 
 
@@ -238,7 +245,6 @@
         )
         for v in range(4):
             yown[v, f] = own[v]
-            one[2 + 2 * v + f] = own[v]
 
 
 class Ghost:
@@ -258,42 +264,18 @@
     def named(self, tiles, name, k):
         return self.lane(tiles, 4 + PLANES.index(name), k)
 
-    def row(self, row, k):
-        shape = (1, self.shape[1])
-        first = lax.broadcasted_iota(jnp.int32, shape, 1) < shape[1] // 2
-        a = jnp.broadcast_to(row[:, k : k + 1], shape)
-        b = jnp.broadcast_to(row[:, self.nx + k : self.nx + k + 1], shape)
-        return jnp.where(first, a, b)
-
-
-def ghost_kernel(nx, tiles, xown, gi, gm, gu, gq, gr, own):
-    ghost = Ghost(tiles.shape[1:], nx)
-
-    def keep(ref):
-        def store(k, v):
-            ref[k] = v
-
-        return store
-
-    ports = factor(
-        nx,
-        lambda k: ghost.named(tiles, "lat", k),
-        lambda k: 0.5 * ghost.named(tiles, "cx", k),
-        ghost.ratio,
-        *(keep(ref) for ref in (gi, gm, gu, gq, gr)),
-    )
-    for v in range(4):
-        own[v, 0] = xown[v, 0]
-        own[v, 1] = xown[v, 1]
-        own[v, 2] = ports[v]
-
-
-def lateral_step(v, ahead_row, behind_row, lateral, half):
+
+def lateral_step(v, lateral, half):
     ny = v.shape[0]
+    me, n = lax.axis_index("gy"), lax.axis_size("gy")
     row = lax.broadcasted_iota(jnp.int32, v.shape, 0)
-    ahead = jnp.where(row == ny - 1, ahead_row, pltpu.roll(v, ny - 1, 0))
-    behind = jnp.where(row == 0, behind_row, pltpu.roll(v, 1, 0))
-    return (lateral - half) * (ahead - v) + (lateral + half) * (behind - v)
+    ahead = jnp.where(row == ny - 1, 0.0, pltpu.roll(v, ny - 1, 0))
+    behind = jnp.where(row == 0, 0.0, pltpu.roll(v, 1, 0))
+    east, west = lateral - half, lateral + half
+    inside_high = (row == ny - 1) & (me < n - 1)
+    inside_low = (row == 0) & (me > 0)
+    side = jnp.where(inside_high, east, jnp.where(inside_low, west, 0.0))
+    return east * (ahead - v) + west * (behind - v), side
 
 
 def vertical_step(nz, v, column, lateral, half):
@@ -305,52 +287,82 @@
     return (lateral - half) * (ahead - v) + (lateral + half) * (behind - v)
 
 
-def first_kernel(
-    nx, ny, nz, t, h, load, lat, up, cy, cz, one, two, mine, tiles, xi, xm, xu, gi, gm, gu, d, p, gp, ends
+def early_kernel(
+    nx, nz, t, h, load, lat, up, cy, cz, mine, tiles, xown,
+    gi, gm, gu, gq, gr, own, d, side, gd, gside,
 ):
-    even = lax.axis_index("gy") % 2 == 0
     upper = lax.axis_index("gz")
-    last = one.shape[0] - 1
+    ghost = Ghost(tiles.shape[1:], nx)
+
+    def keep(ref):
+        def store(k, v):
+            ref[k] = v
+
+        return store
+
+    lateral = [ghost.ratio * ghost.named(tiles, "lat", k) for k in range(nx)]
+    ports = factor(
+        nx,
+        lambda k: lateral[k],
+        lambda k: 0.5 * ghost.named(tiles, "cx", k),
+        1.0,
+        *(keep(ref) for ref in (gi, gm, gu, gq, gr)),
+    )
+    for v in range(4):
+        own[v, 0] = xown[v, 0]
+        own[v, 1] = xown[v, 1]
+        own[v, 2] = ports[v]
+    for k in range(nx):
+        v = ghost.fields(tiles, 0, k)
+        step, gside[k] = lateral_step(v, lateral[k], 0.5 * ghost.named(tiles, "cy", k))
+        inner, here = ghost.fields(tiles, 2, k), ghost.fields(mine, 0, k)
+        ahead, behind = jnp.where(upper == 0, inner, here), jnp.where(upper == 0, here, inner)
+        rise, half = ghost.ratio * ghost.named(tiles, "up", k), 0.5 * ghost.named(tiles, "cz", k)
+        step = step + ((rise - half) * (ahead - v) + (rise + half) * (behind - v))
+        gd[k] = v + step + jnp.where(ghost.first, ghost.named(tiles, "load", k), 0.0)
     for f, (ratio, ref) in enumerate(zip(RATIOS, (t, h))):
-        low_rows = jnp.where(even, two[f], one[f])
-        high_rows = jnp.where(even, one[f], two[f])
         for k in range(nx):
             v = ref[k]
-            out = v + lateral_step(
-                v, high_rows[k : k + 1], low_rows[k : k + 1], ratio * lat[k], 0.5 * cy[k]
+            step, side[f, k] = lateral_step(v, ratio * lat[k], 0.5 * cy[k])
+            at = nx * f + k
+            out = v + step + vertical_step(
+                nz, v, tiles[0, :, at : at + 1], ratio * up[k], 0.5 * cz[k]
             )
-            at = nx * f + k
-            out = out + vertical_step(nz, v, tiles[0, :, at : at + 1], ratio * up[k], 0.5 * cz[k])
-            if f == 0:
-                out = out + load[k]
-            d[f, k] = out
+            d[f, k] = out + load[k] if f == 0 else out
+
+
+def first_kernel(
+    nx, ny, faces, d0, side, gd, gside, xi, xm, xu, gi, gm, gu, d, p, gp, ends
+):
+    odd = lax.axis_index("gy") % 2
+    half = ny // 2
+    for f in range(2):
+        for k in range(nx):
+            low = faces[1 - odd, f, pl.ds(k, half, stride=0), :]
+            high = faces[odd, f, pl.ds(k, half, stride=0), :]
+            d[f, k, :half] = d0[f, k, :half] + side[f, k, :half] * low
+            d[f, k, half:] = d0[f, k, half:] + side[f, k, half:] * high
         ends[2 * f], ends[2 * f + 1] = sweep(
             nx, lambda k: d[f, k], lambda k: xi[f, k], lambda k: xm[f, k], lambda k: xu[f, k], put(p, f)
         )
-    ghost = Ghost(tiles.shape[1:], nx)
-    low_row = jnp.where(even, two[2], one[last])[ny - 1 : ny]
-    high_row = jnp.where(even, one[last], two[2])[0:1]
-    sides = []
-    for k in range(nx):
-        v = ghost.fields(tiles, 0, k)
-        out = v + lateral_step(
-            v,
-            ghost.row(high_row, k),
-            ghost.row(low_row, k),
-            ghost.ratio * ghost.named(tiles, "lat", k),
-            0.5 * ghost.named(tiles, "cy", k),
-        )
-        inner, here = ghost.fields(tiles, 2, k), ghost.fields(mine, 0, k)
-        ahead, behind = jnp.where(upper == 0, inner, here), jnp.where(upper == 0, here, inner)
-        lateral, half = ghost.ratio * ghost.named(tiles, "up", k), 0.5 * ghost.named(tiles, "cz", k)
-        out = out + ((lateral - half) * (ahead - v) + (lateral + half) * (behind - v))
-        sides.append(out + jnp.where(ghost.first, ghost.named(tiles, "load", k), 0.0))
+    low_row = faces[1 - odd, 2, pl.ds(ny - 1, half, stride=0), :]
+    high_row = faces[odd, 2, pl.ds(0, half, stride=0), :]
+    first = lax.broadcasted_iota(jnp.int32, low_row.shape, 1) < low_row.shape[1] // 2
+
+    def spread(row, k):
+        a = jnp.broadcast_to(row[:, k : k + 1], row.shape)
+        b = jnp.broadcast_to(row[:, nx + k : nx + k + 1], row.shape)
+        return jnp.where(first, a, b)
+
+    def rhs(k):
+        beside_rows = jnp.concatenate([spread(low_row, k), spread(high_row, k)])
+        return gd[k] + gside[k] * beside_rows
 
     def keep(k, v):
         gp[k] = v
 
     ends[4], ends[5] = sweep(
-        nx, lambda k: sides[k], lambda k: gi[k], lambda k: gm[k], lambda k: gu[k], keep
+        nx, rhs, lambda k: gi[k], lambda k: gm[k], lambda k: gu[k], keep
     )
 
 
@@ -391,7 +403,7 @@
         return pair_values("gx", f, mine, other, own, near, far_word(far, f))
 
     ghost_low, ghost_high = values(2)
-    yends, slopes = [], []
+    slopes = []
     for f, ratio in enumerate(RATIOS):
         low, high = values(f)
         for k in range(nx):
@@ -434,14 +446,19 @@
             ref[pl.ds(k, nx, stride=ny), :] = p[f, k] + q[f, k] * low + r[f, k] * high
 
 
-def neighbours(one, two, axis):
-    n = lax.axis_size(axis)
+def neighbours(one, two):
+    across, n = lax.axis_size("gx"), lax.axis_size("gy")
 
     def swapped(first, value):
-        pairs = [(i, i + 1) for i in range(first, n - 1, 2)]
-        if not pairs:
-            return jnp.zeros_like(value)
-        return lax.ppermute(value, axis, pairs + [(b, a) for a, b in pairs])
+        partner = {i: i ^ 1 if first == 0 else ((i + 1) ^ 1) - 1 for i in range(n)}
+        pairs = []
+        for x in range(across):
+            for i in range(n):
+                j = partner[i]
+                target = (x, j) if 0 <= j < n else (x ^ 1, i)
+                if target[0] < across:
+                    pairs.append((x * n + i, target[0] * n + target[1]))
+        return lax.ppermute(value, ("gx", "gy"), pairs)
 
     return swapped(0, one), swapped(1, two)
 
@@ -468,30 +485,27 @@
         functools.partial(coef_kernel, nx, ny),
         (lines_x,) * 5
         + (lines_y,) * 5
-        + ((4, 2) + block_x, (4, 2) + block_y, (10,) + block_y, (2,) + block_y),
+        + ((4, 2) + block_x, (4, 2) + block_y, (2,) + block_y, (2,) + block_y),
         *(a.reshape(flat) for a in (thermal, vapour, lat, cx, cy)),
     )
-    one = one if paired[1] else one[:2]
     one, two = neighbours(
-        jnp.concatenate([one, tiles[:1]]), jnp.concatenate([two, tiles[:1]]), "gy"
-    )
-    ynear = one[2:10].reshape(yown.shape) if paired[1] else yown
-    gi, gm, gu, gq, gr, own = call(
-        functools.partial(ghost_kernel, nx),
-        ((nx,) + block_x,) * 5 + ((4, 3) + block_x,),
-        tiles, xown,
+        jnp.concatenate([one, tiles[:1]]), jnp.concatenate([two, tiles[:1]])
+    )
+    gi, gm, gu, gq, gr, own, d, side, gd, gside = call(
+        functools.partial(early_kernel, nx, nz),
+        ((nx,) + block_x,) * 5 + ((4, 3) + block_x, lines_x, lines_x) + ((nx,) + block_x,) * 2,
+        thermal, vapour, load, lat, up, cy, cz, mine, tiles, xown,
     )
     near = swap(own, "gx", 1) if paired[0] else own
+    ynear = swap(yown, "gy", 1) if paired[1] else yown
     d, p, gp, ends = call(
-        functools.partial(first_kernel, nx, ny, nz),
+        functools.partial(first_kernel, nx, ny),
         (lines_x, lines_x, (nx,) + block_x, (6,) + block_x),
-        thermal, vapour, load, lat, up, cy, cz, one, two, mine, tiles, xi, xm, xu, gi, gm, gu,
+        jnp.stack([one, two]), d, side, gd, gside, xi, xm, xu, gi, gm, gu,
     )
     if paired[0]:
         near_ends = swap(ends, "gx", 1)
-        (word,) = call(
-            functools.partial(pair_kernel, "gx", 3), ((5,) + block_x,), ends, near_ends, own, near
-        )
+        (word,) = call(functools.partial(pair_kernel, "gx", 3), ((5,) + block_x,), ends, near_ends, own, near)
         far = swap(word, "gx", 2)
     else:
         near_ends, far = ends, everyones("gx", ends, own)
@@ -503,8 +517,8 @@
         scratch=[pltpu.VMEM((2,) + flat, F32)],
     )
     if paired[1]:
+        received = [swap(outs[0], "gy", k) for k in (2, 3)]
         near_ends = swap(yends, "gy", 1)
-        received = [swap(outs[0], "gy", 2), swap(outs[0], "gy", 3)]
     else:
         near_ends, received = yends, [everyones("gy", yends, yown)]
     t_new, h_new = call(
@@ -517,6 +531,4 @@
 
 def solution(mesh):
     spec = P("gx", "gy", "gz")
-    return jax.shard_map(
-        body, mesh=mesh, in_specs=(spec,) * 8, out_specs=(spec, spec), check_vma=False
-    )
+    return jax.shard_map(body, mesh=mesh, in_specs=(spec,) * 8, out_specs=(spec, spec), check_vma=False)

time: 31.8 us -> 29.5 us (0.928)
  waiting for transfers between devices: 10.3 us -> 8.74 us
  starting transfers between devices: 15.7 us -> 15 us
    ppermute x2, waiting for transfers between devices: 1.49 us -> 0.25 us  [swapped(): return lax.ppermute(value, ('gx', 'gy'), pairs)]
    ppermute x2, starting transfers between devices: 2.83 us -> 2.11 us  [swapped(): return lax.ppermute(value, ('gx', 'gy'), pairs)]
    ppermute x7 -> x8, waiting for transfers between devices: 8.77 us -> 8.5 us  [swap(): lax.ppermute(value, axis, [(i, i ^ k) for i in range(lax.axis_size(axis))])]
    ppermute x7 -> x8, starting transfers between devices: 12.9 us -> 12.9 us  [swap(): lax.ppermute(value, axis, [(i, i ^ k) for i in range(lax.axis_size(axis))])]
  transfers between devices with their start and end apart: 9 -> 10, of which waited for: 6 -> 6; matrix products, arithmetic and copies ran while one was open for 0% -> 0% of each run, Pallas kernels for 5% -> 6%
where the time goes in v3:
time: 29.5 us; the launch traced here: 29.3 us
  starting transfers between devices  15 us (51%)
  waiting for transfers between devices  8.74 us (30%)
  Pallas kernels  4.88 us (17%)
  between operations  0.68 us (2%)
    ppermute x8, starting transfers between devices, swap(): lax.ppermute(value, axis, [(i, i ^ k) for i in range(lax.axis_size(axis))])  12.9 us
    ppermute x8, waiting for transfers between devices, swap(): lax.ppermute(value, axis, [(i, i ^ k) for i in range(lax.axis_size(axis))])  8.5 us
    pallas_call x7, Pallas kernels, run(): pl.pallas_call(kernel, out_shape=tuple((jax.ShapeDtypeStruct(s, F32) for...  4.88 us
    ppermute x2, starting transfers between devices, swapped(): return lax.ppermute(value, ('gx', 'gy'), pairs)  2.11 us
  transfers between devices with their start and end apart: 10, of which 6 were waited for; matrix products, arithmetic and copies ran while one was open for 0% of the time, Pallas kernels for 6%

profile of v3, /device:TPU:0, one launch (start us, length us, event | category | flops | bytes accessed | tf_op | source)
XLA Modules:
  0.0 29.3 jit_solution(10108069740460255700)
XLA Ops:
  0.6 1.9 %shard_map.95 = (f32[16,16,128]{2,1,0:T(8,128)S(1)}, f32[16,16,128]{2,1,0:T(8,128)S(1)}, f32[16,16,128]{2,1,0:T(8,128)S(1)}, f32[16,16,128]{2,1,0:T(8,128)S(1)},...) custom-call(f32[16,16,128]{2,1,0:T(8,128)} %refs_0_.1, ...), custom_call_target="tpu_custom_call" | custom-call | flops 400000 | bytes 1048576 | tf_op jit(solution)/shard_map/pallas_call | solution.py:25
  2.5 3.0 %collective-permute-start = (f32[2,16,128]{2,1,0:T(8,128)S(1)}, f32[2,16,128]{2,1,0:T(8,128)S(1)}, u32[]{:S(2)}, u32[]{:S(2)}) collective-permute-start(f32[2,16,128]{2,1,0:T(8,128)S(1)} %get-tuple-element.50.mine), channel_id=1, source_target_pairs={{0,1},{1,0},{2,3},{3,2},{4,5},{5,4},{6,7},{7,6},{8,9},{9,8},{10,11... | collective-permute-start | bytes 49160 | tf_op jit(solution)/shard_map/ppermute | solution.py:183
  5.5 0.4 %shard_map.96 = (f32[2,16,16,128]{3,2,1,0:T(8,128)S(1)}, f32[2,16,16,128]{3,2,1,0:T(8,128)S(1)}, f32[2,16,16,128]{3,2,1,0:T(8,128)S(1)}, f32[2,16,16,128]{3,2,1,...) custom-call(f32[256,128]{1,0:T(8,128)S(1)} %bitcast.9, ...), custom_call_target="tpu_custom_call" | custom-call | flops 400000 | bytes 655360 | tf_op jit(solution)/shard_map/pallas_call | solution.py:25
  6.0 1.3 %collective-permute-done.tiles = f32[2,16,128]{2,1,0:T(8,128)S(1)} collective-permute-done((f32[2,16,128]{2,1,0:T(8,128)S(1)}, f32[2,16,128]{2,1,0:T(8,128)S(1)}, u32[]{:S(2)}, u32[]{:S(2)}) %collective-permute-start) | collective-permute-done | bytes 16416 | tf_op jit(solution)/shard_map/ppermute | solution.py:183
  7.3 2.1 %collective-permute-start.1 = (f32[3,16,128]{2,1,0:T(8,128)S(1)}, f32[3,16,128]{2,1,0:T(8,128)S(1)}, u32[]{:S(2)}, u32[]{:S(2)}) collective-permute-start(f32[3,16,128]{2,1,0:T(8,128)S(1)} %get-tuple-element.86), channel_id=1, source_target_pairs={{0,2},{2,0},{4,6},{6,4},{8,10},{10,8},{12,14},{14,12},{16,18},{18,... | collective-permute-start | bytes 73736 | tf_op jit(solution)/shard_map/ppermute | solution.py:461
  9.4 0.0 collective-permute-start.2
  9.4 1.0 %shard_map.97 = (f32[16,16,128]{2,1,0:T(8,128)S(1)}, f32[16,16,128]{2,1,0:T(8,128)S(1)}, f32[16,16,128]{2,1,0:T(8,128)S(1)}, f32[16,16,128]{2,1,0:T(8,128)S(1)},...) custom-call(f32[16,16,128]{2,1,0:T(8,128)S(1)} %get-tuple-element.44, ...), custom_call_target="tpu_custom_call" | custom-call | flops 400000 | bytes 1015808 | tf_op jit(solution)/shard_map/pallas_call | solution.py:25
  10.4 0.6 %collective-permute-start.4 = (f32[4,3,16,128]{3,2,1,0:T(8,128)S(1)}, f32[4,3,16,128]{3,2,1,0:T(8,128)S(1)}, u32[]{:S(2)}, u32[]{:S(2)}) collective-permute-start(f32[4,3,16,128]{3,2,1,0:T(8,128)S(1)} %get-tuple-element.73.own), channel_id=1, source_target_pairs={{0,8},{8,0},{16,24},{24,16},{1,9},{9,1},{17,25},{25,17},{2,10},{10... | collective-permute-start | bytes 294920 | tf_op jit(solution)/shard_map/ppermute | solution.py:183
  10.9 0.2 collective-permute-done.1
  11.2 0.0 collective-permute-done.2
  11.2 0.3 shard_map.98
  11.5 0.1 collective-permute-start.3
  11.5 3.2 %collective-permute-start.6 = (f32[4,2,16,128]{3,2,1,0:T(8,128)S(1)}, f32[4,2,16,128]{3,2,1,0:T(8,128)S(1)}, u32[]{:S(2)}, u32[]{:S(2)}) collective-permute-start(f32[4,2,16,128]{3,2,1,0:T(8,128)S(1)} %get-tuple-element.78.yown.own), channel_id=1, source_target_pairs={{0,2},{2,0},{4,6},{6,4},{1,3},{3,1},{5,7},{7,5},{8,10},{10,8},{12,... | collective-permute-start | bytes 196616 | tf_op jit(solution)/shard_map/ppermute | solution.py:183
  14.8 0.0 collective-permute-done.3.near_ends
  14.8 0.0 collective-permute-done.4.near
  14.8 1.6 %collective-permute-start.5 = (f32[5,16,128]{2,1,0:T(8,128)S(1)}, f32[5,16,128]{2,1,0:T(8,128)S(1)}, u32[]{:S(2)}, u32[]{:S(2)}) collective-permute-start(f32[5,16,128]{2,1,0:T(8,128)S(1)} %shard_map.99), channel_id=1, source_target_pairs={{0,16},{8,24},{16,0},{24,8},{1,17},{9,25},{17,1},{25,9},{2,18},{10... | collective-permute-start | bytes 122888 | tf_op jit(solution)/shard_map/ppermute | solution.py:183
  16.4 1.0 %collective-permute-done.6.ynear.near = f32[4,2,16,128]{3,2,1,0:T(8,128)S(1)} collective-permute-done((f32[4,2,16,128]{3,2,1,0:T(8,128)S(1)}, f32[4,2,16,128]{3,2,1,0:T(8,128)S(1)}, u32[]{:S(2)}, u32[]{:S(2)}) %collective-permute-start.6) | collective-permute-done | bytes 65568 | tf_op jit(solution)/shard_map/ppermute | solution.py:183
  17.4 1.4 %collective-permute-done.5.far = f32[5,16,128]{2,1,0:T(8,128)S(1)} collective-permute-done((f32[5,16,128]{2,1,0:T(8,128)S(1)}, f32[5,16,128]{2,1,0:T(8,128)S(1)}, u32[]{:S(2)}, u32[]{:S(2)}) %collective-permute-start.5) | collective-permute-done | bytes 40992 | tf_op jit(solution)/shard_map/ppermute | solution.py:183
  18.9 0.5 %shard_map.100 = (f32[2,16,16,128]{3,2,1,0:T(8,128)S(1)}, f32[4,16,128]{2,1,0:T(8,128)S(1)}, f32[3,16,128]{2,1,0:T(8,128)S(1)}) custom-call(f32[2,16,16,128]{3,2,1,0:T(8,128)S(1)} %get-tuple-element.66.p, f32[2,16,16,128]{3,2,1,0:T(8,128)S(1)} %get-tuple-element.67.q, f32[2,16,16,128]{3,2,1,0:T(8,128)S(1)} %get-tuple-element.68.r, ...), custom_call_target="tpu_custom_call" | custom-call | flops 400000 | bytes 3088384 | tf_op jit(solution)/shard_map/pallas_call | solution.py:25
  19.4 1.2 %collective-permute-start.7 = (f32[4,16,128]{2,1,0:T(8,128)S(1)}, f32[4,16,128]{2,1,0:T(8,128)S(1)}, u32[]{:S(2)}, u32[]{:S(2)}) collective-permute-start(f32[4,16,128]{2,1,0:T(8,128)S(1)} %get-tuple-element.82.ends), channel_id=1, source_target_pairs={{0,2},{2,0},{4,6},{6,4},{1,3},{3,1},{5,7},{7,5},{8,10},{10,8},{12,... | collective-permute-start | bytes 98312 | tf_op jit(solution)/shard_map/ppermute | solution.py:183
  20.6 2.3 %collective-permute-start.8 = (f32[3,16,128]{2,1,0:T(8,128)S(1)}, f32[3,16,128]{2,1,0:T(8,128)S(1)}, u32[]{:S(2)}, u32[]{:S(2)}) collective-permute-start(f32[3,16,128]{2,1,0:T(8,128)S(1)} %get-tuple-element.83), channel_id=1, source_target_pairs={{0,4},{2,6},{4,0},{6,2},{1,5},{3,7},{5,1},{7,3},{8,12},{10,14},{12... | collective-permute-start | bytes 73736 | tf_op jit(solution)/shard_map/ppermute | solution.py:183
  22.9 0.9 %collective-permute-start.9 = (f32[3,16,128]{2,1,0:T(8,128)S(1)}, f32[3,16,128]{2,1,0:T(8,128)S(1)}, u32[]{:S(2)}, u32[]{:S(2)}) collective-permute-start(f32[3,16,128]{2,1,0:T(8,128)S(1)} %get-tuple-element.83), channel_id=1, source_target_pairs={{0,6},{2,4},{4,2},{6,0},{1,7},{3,5},{5,3},{7,1},{8,14},{10,12},{12... | collective-permute-start | bytes 73736 | tf_op jit(solution)/shard_map/ppermute | solution.py:183
  23.8 1.5 %collective-permute-done.8.rest_0_ = f32[3,16,128]{2,1,0:T(8,128)S(1)} collective-permute-done((f32[3,16,128]{2,1,0:T(8,128)S(1)}, f32[3,16,128]{2,1,0:T(8,128)S(1)}, u32[]{:S(2)}, u32[]{:S(2)}) %collective-permute-start.8) | collective-permute-done | bytes 24608 | tf_op jit(solution)/shard_map/ppermute | solution.py:183
  25.3 3.2 %collective-permute-done.9.rest_1_ = f32[3,16,128]{2,1,0:T(8,128)S(1)} collective-permute-done((f32[3,16,128]{2,1,0:T(8,128)S(1)}, f32[3,16,128]{2,1,0:T(8,128)S(1)}, u32[]{:S(2)}, u32[]{:S(2)}) %collective-permute-start.9) | collective-permute-done | bytes 24608 | tf_op jit(solution)/shard_map/ppermute | solution.py:183
  28.5 0.0 collective-permute-done.7.near_ends
  28.5 0.8 %shard_map.101 = (f32[256,128]{1,0:T(8,128)}, f32[256,128]{1,0:T(8,128)}) custom-call(f32[2,16,16,128]{3,2,1,0:T(8,128)S(1)} %get-tuple-element.79.p, f32[2,16,16,128]{3,2,1,0:T(8,128)S(1)} %get-tuple-element.80.q, f32[2,16,16,128]{3,2,1,0:T(8,128)S(1)} %get-tuple-element.81.r, f32[4,16,128]{2,1,0:T(8,128)S(1)} %get-tuple-element.82.ends, ...), custom_call_target="tpu_custom_call" | custom-call | flops 400000 | bytes 1032192 | tf_op jit(solution)/shard_map/pallas_call | solution.py:25
  (4 shorter events, 0.1 us)
Async XLA Ops:
  2.5 4.8 %collective-permute-start = (f32[2,16,128]{2,1,0:T(8,128)S(1)}, f32[2,16,128]{2,1,0:T(8,128)S(1)}, u32[]{:S(2)}, u32[]{:S(2)}) collective-permute-start(f32[2,16,128]{2,1,0:T(8,128)S(1)} %get-tuple-element.50.mine), channel_id=1, source_target_pairs={{0,1},{1,0},{2,3},{3,2},{4,5},{5,4},{6,7},{7,6},{8,9},{9,8},{10,11... | collective-permute-start | bytes 49160 | tf_op jit(solution)/shard_map/ppermute | solution.py:183
  7.3 3.9 %collective-permute-start.1 = (f32[3,16,128]{2,1,0:T(8,128)S(1)}, f32[3,16,128]{2,1,0:T(8,128)S(1)}, u32[]{:S(2)}, u32[]{:S(2)}) collective-permute-start(f32[3,16,128]{2,1,0:T(8,128)S(1)} %get-tuple-element.86), channel_id=1, source_target_pairs={{0,2},{2,0},{4,6},{6,4},{8,10},{10,8},{12,14},{14,12},{16,18},{18,... | collective-permute-start | bytes 73736 | tf_op jit(solution)/shard_map/ppermute | solution.py:461
  9.4 1.8 %collective-permute-start.2 = (f32[3,16,128]{2,1,0:T(8,128)S(1)}, f32[3,16,128]{2,1,0:T(8,128)S(1)}, u32[]{:S(2)}, u32[]{:S(2)}) collective-permute-start(f32[3,16,128]{2,1,0:T(8,128)S(1)} %get-tuple-element.87), channel_id=1, source_target_pairs={{0,8},{2,4},{4,2},{6,14},{8,0},{10,12},{12,10},{14,6},{16,24},{18,... | collective-permute-start | bytes 73736 | tf_op jit(solution)/shard_map/ppermute | solution.py:461
  10.4 4.4 %collective-permute-start.4 = (f32[4,3,16,128]{3,2,1,0:T(8,128)S(1)}, f32[4,3,16,128]{3,2,1,0:T(8,128)S(1)}, u32[]{:S(2)}, u32[]{:S(2)}) collective-permute-start(f32[4,3,16,128]{3,2,1,0:T(8,128)S(1)} %get-tuple-element.73.own), channel_id=1, source_target_pairs={{0,8},{8,0},{16,24},{24,16},{1,9},{9,1},{17,25},{25,17},{2,10},{10... | collective-permute-start | bytes 294920 | tf_op jit(solution)/shard_map/ppermute | solution.py:183
  11.5 3.3 %collective-permute-start.3 = (f32[6,16,128]{2,1,0:T(8,128)S(1)}, f32[6,16,128]{2,1,0:T(8,128)S(1)}, u32[]{:S(2)}, u32[]{:S(2)}) collective-permute-start(f32[6,16,128]{2,1,0:T(8,128)S(1)} %get-tuple-element.72.ends), channel_id=1, source_target_pairs={{0,8},{8,0},{16,24},{24,16},{1,9},{9,1},{17,25},{25,17},{2,10},{10... | collective-permute-start | bytes 147464 | tf_op jit(solution)/shard_map/ppermute | solution.py:183
  11.5 5.9 %collective-permute-start.6 = (f32[4,2,16,128]{3,2,1,0:T(8,128)S(1)}, f32[4,2,16,128]{3,2,1,0:T(8,128)S(1)}, u32[]{:S(2)}, u32[]{:S(2)}) collective-permute-start(f32[4,2,16,128]{3,2,1,0:T(8,128)S(1)} %get-tuple-element.78.yown.own), channel_id=1, source_target_pairs={{0,2},{2,0},{4,6},{6,4},{1,3},{3,1},{5,7},{7,5},{8,10},{10,8},{12,... | collective-permute-start | bytes 196616 | tf_op jit(solution)/shard_map/ppermute | solution.py:183
  14.8 4.1 %collective-permute-start.5 = (f32[5,16,128]{2,1,0:T(8,128)S(1)}, f32[5,16,128]{2,1,0:T(8,128)S(1)}, u32[]{:S(2)}, u32[]{:S(2)}) collective-permute-start(f32[5,16,128]{2,1,0:T(8,128)S(1)} %shard_map.99), channel_id=1, source_target_pairs={{0,16},{8,24},{16,0},{24,8},{1,17},{9,25},{17,1},{25,9},{2,18},{10... | collective-permute-start | bytes 122888 | tf_op jit(solution)/shard_map/ppermute | solution.py:183
  19.4 9.2 %collective-permute-start.7 = (f32[4,16,128]{2,1,0:T(8,128)S(1)}, f32[4,16,128]{2,1,0:T(8,128)S(1)}, u32[]{:S(2)}, u32[]{:S(2)}) collective-permute-start(f32[4,16,128]{2,1,0:T(8,128)S(1)} %get-tuple-element.82.ends), channel_id=1, source_target_pairs={{0,2},{2,0},{4,6},{6,4},{1,3},{3,1},{5,7},{7,5},{8,10},{10,8},{12,... | collective-permute-start | bytes 98312 | tf_op jit(solution)/shard_map/ppermute | solution.py:183
  20.6 4.8 %collective-permute-start.8 = (f32[3,16,128]{2,1,0:T(8,128)S(1)}, f32[3,16,128]{2,1,0:T(8,128)S(1)}, u32[]{:S(2)}, u32[]{:S(2)}) collective-permute-start(f32[3,16,128]{2,1,0:T(8,128)S(1)} %get-tuple-element.83), channel_id=1, source_target_pairs={{0,4},{2,6},{4,0},{6,2},{1,5},{3,7},{5,1},{7,3},{8,12},{10,14},{12... | collective-permute-start | bytes 73736 | tf_op jit(solution)/shard_map/ppermute | solution.py:183
  22.9 5.6 %collective-permute-start.9 = (f32[3,16,128]{2,1,0:T(8,128)S(1)}, f32[3,16,128]{2,1,0:T(8,128)S(1)}, u32[]{:S(2)}, u32[]{:S(2)}) collective-permute-start(f32[3,16,128]{2,1,0:T(8,128)S(1)} %get-tuple-element.83), channel_id=1, source_target_pairs={{0,6},{2,4},{4,2},{6,0},{1,7},{3,5},{5,3},{7,1},{8,14},{10,12},{12... | collective-permute-start | bytes 73736 | tf_op jit(solution)/shard_map/ppermute | solution.py:183

commit v4 on v3

--- a/solution.py
+++ b/solution.py
@@ -115,16 +115,20 @@
     return second == 1, second == me % 2, me % 2
 
 
-def oriented(axis, ends, coefs, f):
-    port = tuple(ends) + tuple(coefs[v, f] for v in range(4))
+def coefs_of(ref, f):
+    return tuple(ref[v, f] for v in range(4))
+
+
+def oriented(axis, ends, coefs):
+    port = tuple(ends) + tuple(coefs)
     return pick(place(axis)[0], mirrored(port), port)
 
 
-def pair_source(axis, f, ends, own, near):
+def pair_source(axis, ends, own, near):
     outer = place(axis)[1]
-    zero = jnp.zeros_like(ends[0])
-    mine = oriented(axis, ends, own, f)
-    other = oriented(axis, (zero, zero), near, f)
+    zero = jnp.zeros_like(own[0])
+    mine = oriented(axis, ends or (zero, zero), own)
+    other = oriented(axis, (zero, zero), near)
     q1, q2, r1, r2 = pick(outer, other[2:], mine[2:])
     slope = jnp.where(outer, mine[5], other[5])
     step = q2 / (1.0 - q1 * slope)
@@ -132,34 +136,20 @@
     return part, r2 + step * slope * r1
 
 
-def pair_whole(axis, f, ends, near_ends, own, near):
-    outer = place(axis)[1]
-    mine = oriented(axis, ends, own, f)
-    other = oriented(axis, near_ends, near, f)
-    first, then = pick(outer, mine, other), pick(outer, other, mine)
-    return along(then, (first[1], first[5]))
-
-
-def pair_values(axis, f, ends, near_ends, own, near, far):
+def pair_values(axis, ends, near_ends, own, near, far):
     second, outer, _ = place(axis)
     zero = jnp.zeros_like(ends[0])
-    mine = oriented(axis, ends, own, f)
-    other = oriented(axis, near_ends, near, f)
+    mine = oriented(axis, ends, own)
+    other = oriented(axis, near_ends, near)
     ahead = pick(outer, along(mirrored(other), far), far)
     behind = pick(outer, (zero, zero), (other[1], other[5]))
     back, front = beside(mine, behind, ahead)
     return pick(second, (front, back), (back, front))
 
 
-def scan_values(axis, f, blocks, ends, own, ports):
+def scan_values(axis, mine, port_of):
     me, n = lax.axis_index(axis), lax.axis_size(axis)
-    mine = tuple(ends) + tuple(own[v, f] for v in range(4))
     zero = jnp.zeros_like(mine[0])
-
-    def port_of(j):
-        return tuple(ports[j, 2 * f + v] for v in range(2)) + tuple(
-            ports[j, 2 * blocks + blocks * v + f] for v in range(4)
-        )
 
     def step(j, sides):
         left, right = sides
@@ -172,10 +162,9 @@
     return beside(mine, left, right)
 
 
-def everyones(axis, ends, own):
-    blocks = own.shape[1]
+def everyones(axis, ends, own, *more):
     return lax.all_gather(
-        jnp.concatenate([ends, own.reshape((4 * blocks,) + own.shape[2:])]), axis
+        jnp.concatenate([ends, own.reshape((8,) + own.shape[2:]), *more]), axis
     )
 
 
@@ -194,21 +183,32 @@
     upper = lax.axis_index("gz")
     edge, inner = 1 - upper, 2 - 3 * upper
     planes = [(0, edge), (1, edge), (0, inner), (1, inner)] + [(i, edge) for i in range(2, 8)]
+    lane = lax.broadcasted_iota(jnp.int32, outs[0].shape[1:], 1)
+
+    def plane(a, i, offset):
+        moved = [
+            pltpu.roll(outs[i][k], lax.rem(offset + (nx * a + k + nz), nz), 1) for k in range(nx)
+        ]
+        bit = 1
+        while len(moved) > 1:
+            moved = [jnp.where((lane & bit) == 0, x, y) for x, y in zip(moved[::2], moved[1::2])]
+            bit *= 2
+        return moved[0]
+
     per_tile = nz // nx
-    arrived = set()
-    lane = lax.broadcasted_iota(jnp.int32, outs[0].shape[1:], 1)
+    packed = []
+    for group in (range(2), range(2, 8)):
+        for i in group:
+            copies[i].wait()
+        for n, (i, offset) in enumerate(planes):
+            if i in group:
+                packed.append((n, plane(n % per_tile, i, offset)))
     for first in range(0, len(planes), per_tile):
         tile = None
-        for a, (i, offset) in enumerate(planes[first : first + per_tile]):
-            if i not in arrived:
-                copies[i].wait()
-                arrived.add(i)
-            plane = None
-            for k in range(nx):
-                to = nx * a + k
-                moved = pltpu.roll(outs[i][k], lax.rem(offset + (to + nz), nz), 1)
-                plane = moved if k == 0 else jnp.where(lane == to, moved, plane)
-            tile = plane if a == 0 else jnp.where(lane < nx * a, tile, plane)
+        for n, part in packed:
+            if first <= n < first + per_tile:
+                at = nx * (n - first)
+                tile = part if tile is None else jnp.where(lane < at, tile, part)
         tiles[first // per_tile] = tile
 
 
@@ -247,6 +247,11 @@
             yown[v, f] = own[v]
 
 
+def slope_kernel(axis, own, near, out):
+    for f in range(2):
+        out[f] = pair_source(axis, None, coefs_of(own, f), coefs_of(near, f))[1]
+
+
 class Ghost:
     def __init__(self, shape, nx):
         self.shape, self.nx = shape, nx
@@ -287,34 +292,35 @@
     return (lateral - half) * (ahead - v) + (lateral + half) * (behind - v)
 
 
+def ghost_kernel(nx, tiles, gi, gm, gu, gq, gr, own):
+    ghost = Ghost(tiles.shape[1:], nx)
+
+    def keep(ref):
+        def store(k, v):
+            ref[k] = v
+
+        return store
+
+    ports = factor(
+        nx,
+        lambda k: ghost.named(tiles, "lat", k),
+        lambda k: 0.5 * ghost.named(tiles, "cx", k),
+        ghost.ratio,
+        *(keep(ref) for ref in (gi, gm, gu, gq, gr)),
+    )
+    for v in range(4):
+        own[v] = ports[v]
+
+
 def early_kernel(
-    nx, nz, t, h, load, lat, up, cy, cz, mine, tiles, xown,
-    gi, gm, gu, gq, gr, own, d, side, gd, gside,
+    nx, nz, t, h, load, lat, up, cy, cz, mine, tiles, d, side, gd, gside
 ):
     upper = lax.axis_index("gz")
     ghost = Ghost(tiles.shape[1:], nx)
-
-    def keep(ref):
-        def store(k, v):
-            ref[k] = v
-
-        return store
-
-    lateral = [ghost.ratio * ghost.named(tiles, "lat", k) for k in range(nx)]
-    ports = factor(
-        nx,
-        lambda k: lateral[k],
-        lambda k: 0.5 * ghost.named(tiles, "cx", k),
-        1.0,
-        *(keep(ref) for ref in (gi, gm, gu, gq, gr)),
-    )
-    for v in range(4):
-        own[v, 0] = xown[v, 0]
-        own[v, 1] = xown[v, 1]
-        own[v, 2] = ports[v]
     for k in range(nx):
         v = ghost.fields(tiles, 0, k)
-        step, gside[k] = lateral_step(v, lateral[k], 0.5 * ghost.named(tiles, "cy", k))
+        lateral = ghost.ratio * ghost.named(tiles, "lat", k)
+        step, gside[k] = lateral_step(v, lateral, 0.5 * ghost.named(tiles, "cy", k))
         inner, here = ghost.fields(tiles, 2, k), ghost.fields(mine, 0, k)
         ahead, behind = jnp.where(upper == 0, inner, here), jnp.where(upper == 0, here, inner)
         rise, half = ghost.ratio * ghost.named(tiles, "up", k), 0.5 * ghost.named(tiles, "cz", k)
@@ -332,7 +338,8 @@
 
 
 def first_kernel(
-    nx, ny, faces, d0, side, gd, gside, xi, xm, xu, gi, gm, gu, d, p, gp, ends
+    paired, nx, ny, faces, d0, side, gd, gside, xi, xm, xu, gi, gm, gu, own, near, gown, gnear,
+    d, p, gp, ends, *word
 ):
     odd = lax.axis_index("gy") % 2
     half = ny // 2
@@ -342,9 +349,12 @@
             high = faces[odd, f, pl.ds(k, half, stride=0), :]
             d[f, k, :half] = d0[f, k, :half] + side[f, k, :half] * low
             d[f, k, half:] = d0[f, k, half:] + side[f, k, half:] * high
-        ends[2 * f], ends[2 * f + 1] = sweep(
+        mine = sweep(
             nx, lambda k: d[f, k], lambda k: xi[f, k], lambda k: xm[f, k], lambda k: xu[f, k], put(p, f)
         )
+        ends[2 * f], ends[2 * f + 1] = mine
+        if paired:
+            word[0][f] = pair_source("gx", mine, coefs_of(own, f), coefs_of(near, f))[0]
     low_row = faces[1 - odd, 2, pl.ds(ny - 1, half, stride=0), :]
     high_row = faces[odd, 2, pl.ds(0, half, stride=0), :]
     first = lax.broadcasted_iota(jnp.int32, low_row.shape, 1) < low_row.shape[1] // 2
@@ -361,49 +371,58 @@
     def keep(k, v):
         gp[k] = v
 
-    ends[4], ends[5] = sweep(
-        nx, rhs, lambda k: gi[k], lambda k: gm[k], lambda k: gu[k], keep
-    )
-
-
-def pair_kernel(axis, blocks, ends, near_ends, own, near, out):
-    for f in range(blocks):
-        source, slope = pair_whole(
-            axis, f, (ends[2 * f], ends[2 * f + 1]), (near_ends[2 * f], near_ends[2 * f + 1]), own, near
-        )
-        if f == 2:
-            lane = lax.broadcasted_iota(jnp.int32, source.shape, 1)
-            out[4] = jnp.where((lane & 32) == 0, source, slope)
-        else:
-            out[2 * f] = source
-            out[2 * f + 1] = slope
-
-
-def far_word(far, f):
-    if f < 2:
-        return far[2 * f], far[2 * f + 1]
-    both = far[4]
+    mine = sweep(nx, rhs, lambda k: gi[k], lambda k: gm[k], lambda k: gu[k], keep)
+    ends[4] = packed(*mine)
+    if paired:
+        word[0][2] = packed(*pair_source("gx", mine, x_coefs(own, gown, 2), x_coefs(near, gnear, 2)))
+
+
+def packed(a, b):
+    lane = lax.broadcasted_iota(jnp.int32, a.shape, 1)
+    return jnp.where((lane & 32) == 0, a, b)
+
+
+def unpacked(both):
     lane = lax.broadcasted_iota(jnp.int32, both.shape, 1)
-    source = jnp.where((lane & 32) == 0, both, pltpu.roll(both, 32, 1))
-    slope = jnp.where((lane & 32) == 0, pltpu.roll(both, both.shape[1] - 32, 1), both)
-    return source, slope
+    a = jnp.where((lane & 32) == 0, both, pltpu.roll(both, 32, 1))
+    b = jnp.where((lane & 32) == 0, pltpu.roll(both, both.shape[1] - 32, 1), both)
+    return a, b
+
+
+def x_ends(ends, f):
+    return (ends[2 * f], ends[2 * f + 1]) if f < 2 else unpacked(ends[4])
+
+
+def x_coefs(own, ghost, f):
+    return coefs_of(own, f) if f < 2 else tuple(ghost[v] for v in range(4))
 
 
 def second_kernel(
-    paired, nx, ny, nz, p, q, r, gp, gq, gr, ends, near_ends, own, near, far,
-    d, load, up, cz, yi, ym, yu, yown, ynear, py, *rest,
+    paired, nx, ny, nz, p, q, r, gp, gq, gr, ends, near_ends, own, near, gown, gnear, slopes,
+    d, load, up, cz, yi, ym, yu, yown, ynear, *rest,
 ):
-    outs, s = rest[:-1], rest[-1]
+    far, (py, *outs, s) = rest[: 1 + paired[0]], rest[1 + paired[0] :]
 
     def values(f):
-        mine = (ends[2 * f], ends[2 * f + 1])
-        if not paired[0]:
-            return scan_values("gx", f, 3, mine, own, far)
-        other = (near_ends[2 * f], near_ends[2 * f + 1])
-        return pair_values("gx", f, mine, other, own, near, far_word(far, f))
+        mine, coefs = x_ends(ends, f), x_coefs(own, gown, f)
+        if paired[0]:
+            two, three = far
+            if f < 2:
+                word = two[f] + three[f], slopes[f]
+            else:
+                word, more = unpacked(two[2]), unpacked(three[2])
+                word = word[0] + more[0], word[1]
+            other, other_coefs = x_ends(near_ends, f), x_coefs(near, gnear, f)
+            return pair_values("gx", mine, other, coefs, other_coefs, word)
+
+        def port_of(j):
+            theirs = x_ends(far[0].at[j], f)
+            at = [5 + 2 * v + f if f < 2 else 13 + v for v in range(4)]
+            return tuple(theirs) + tuple(far[0][j, i] for i in at)
+
+        return scan_values("gx", tuple(mine) + coefs, port_of)
 
     ghost_low, ghost_high = values(2)
-    slopes = []
     for f, ratio in enumerate(RATIOS):
         low, high = values(f)
         for k in range(nx):
@@ -425,23 +444,29 @@
         )
         outs[0][2 * f], outs[0][2 * f + 1] = mine
         if paired[1]:
-            outs[1][f], slope = pair_source("gy", f, mine, yown, ynear)
-            slopes.append(slope)
-    if paired[1]:
-        outs[1][2] = jnp.where(place("gy")[2] == 0, slopes[0], slopes[1])
-
-
-def new_kernel(paired, nx, ny, p, q, r, ends, near_ends, own, near, *rest):
+            outs[1][f] = pair_source("gy", mine, coefs_of(yown, f), coefs_of(ynear, f))[0]
+
+
+def new_kernel(paired, nx, ny, p, q, r, ends, near_ends, own, near, slopes, *rest):
     received, news = rest[:-2], rest[-2:]
     for f, ref in enumerate(news):
         mine = (ends[2 * f], ends[2 * f + 1])
+        coefs = coefs_of(own, f)
         if paired:
             other = (near_ends[2 * f], near_ends[2 * f + 1])
             two, three = received
-            slope = jnp.where(place("gy")[2] == f, two[2], three[2])
-            low, high = pair_values("gy", f, mine, other, own, near, (two[f] + three[f], slope))
+            low, high = pair_values(
+                "gy", mine, other, coefs, coefs_of(near, f), (two[f] + three[f], slopes[f])
+            )
         else:
-            low, high = scan_values("gy", f, 2, mine, own, received[0])
+            (ports,) = received
+
+            def port_of(j):
+                return (ports[j, 2 * f], ports[j, 2 * f + 1]) + tuple(
+                    ports[j, 4 + 2 * v + f] for v in range(4)
+                )
+
+            low, high = scan_values("gy", mine + coefs, port_of)
         for k in range(ny):
             ref[pl.ds(k, nx, stride=ny), :] = p[f, k] + q[f, k] * low + r[f, k] * high
 
@@ -488,32 +513,42 @@
         + ((4, 2) + block_x, (4, 2) + block_y, (2,) + block_y, (2,) + block_y),
         *(a.reshape(flat) for a in (thermal, vapour, lat, cx, cy)),
     )
+    xnear, ynear, xslopes, yslopes = xown, yown, xown[0], yown[0]
+    if paired[0]:
+        xnear = swap(xown, "gx", 1)
+        (xslopes,) = call(functools.partial(slope_kernel, "gx"), ((2,) + block_x,), xown, xnear)
+        xslopes = swap(xslopes, "gx", 2)
+    if paired[1]:
+        ynear = swap(yown, "gy", 1)
+        (yslopes,) = call(functools.partial(slope_kernel, "gy"), ((2,) + block_y,), yown, ynear)
+        yslopes = swap(yslopes, "gy", 3)
     one, two = neighbours(
         jnp.concatenate([one, tiles[:1]]), jnp.concatenate([two, tiles[:1]])
     )
-    gi, gm, gu, gq, gr, own, d, side, gd, gside = call(
+    gi, gm, gu, gq, gr, gown = call(
+        functools.partial(ghost_kernel, nx), ((nx,) + block_x,) * 5 + ((4,) + block_x,), tiles
+    )
+    d, side, gd, gside = call(
         functools.partial(early_kernel, nx, nz),
-        ((nx,) + block_x,) * 5 + ((4, 3) + block_x, lines_x, lines_x) + ((nx,) + block_x,) * 2,
-        thermal, vapour, load, lat, up, cy, cz, mine, tiles, xown,
-    )
-    near = swap(own, "gx", 1) if paired[0] else own
-    ynear = swap(yown, "gy", 1) if paired[1] else yown
-    d, p, gp, ends = call(
-        functools.partial(first_kernel, nx, ny),
-        (lines_x, lines_x, (nx,) + block_x, (6,) + block_x),
-        jnp.stack([one, two]), d, side, gd, gside, xi, xm, xu, gi, gm, gu,
+        (lines_x, lines_x) + ((nx,) + block_x,) * 2,
+        thermal, vapour, load, lat, up, cy, cz, mine, tiles,
+    )
+    gnear = swap(gown, "gx", 1) if paired[0] else gown
+    d, p, gp, ends, *word = call(
+        functools.partial(first_kernel, paired[0], nx, ny),
+        (lines_x, lines_x, (nx,) + block_x, (5,) + block_x) + ((3,) + block_x,) * paired[0],
+        jnp.stack([one, two]), d, side, gd, gside, xi, xm, xu, gi, gm, gu, xown, xnear, gown, gnear,
     )
     if paired[0]:
         near_ends = swap(ends, "gx", 1)
-        (word,) = call(functools.partial(pair_kernel, "gx", 3), ((5,) + block_x,), ends, near_ends, own, near)
-        far = swap(word, "gx", 2)
+        far = [swap(word[0], "gx", k) for k in (2, 3)]
     else:
-        near_ends, far = ends, everyones("gx", ends, own)
+        near_ends, far = ends, [everyones("gx", ends, xown, gown)]
     py, yends, *outs = call(
         functools.partial(second_kernel, paired, nx, ny, nz),
-        (lines_y, (4,) + block_y) + (((3,) + block_y,) if paired[1] else ()),
-        p, xq, xr, gp, gq, gr, ends, near_ends, own, near, far,
-        d, load, up, cz, yi, ym, yu, yown, ynear,
+        (lines_y, (4,) + block_y) + (((2,) + block_y,) if paired[1] else ()),
+        p, xq, xr, gp, gq, gr, ends, near_ends, xown, xnear, gown, gnear, xslopes,
+        d, load, up, cz, yi, ym, yu, yown, ynear, *far,
         scratch=[pltpu.VMEM((2,) + flat, F32)],
     )
     if paired[1]:
@@ -524,11 +559,13 @@
     t_new, h_new = call(
         functools.partial(new_kernel, paired[1], nx, ny),
         (flat, flat),
-        py, yq, yr, yends, near_ends, yown, ynear, *received,
+        py, yq, yr, yends, near_ends, yown, ynear, yslopes, *received,
     )
     return t_new.reshape(thermal.shape), h_new.reshape(thermal.shape)
 
 
 def solution(mesh):
     spec = P("gx", "gy", "gz")
-    return jax.shard_map(body, mesh=mesh, in_specs=(spec,) * 8, out_specs=(spec, spec), check_vma=False)
+    return jax.shard_map(
+        body, mesh=mesh, in_specs=(spec,) * 8, out_specs=(spec, spec), check_vma=False
+    )

time: 29.5 us -> 30.8 us (1.044)
  starting transfers between devices: 15 us -> 16.6 us
    ppermute x8 -> x12, starting transfers between devices: 12.9 us -> 14.5 us  [swap(): lax.ppermute(value, axis, [(i, i ^ k) for i in range(lax.axis_size(axis))])]
    pallas_call x7 -> x9, Pallas kernels: 4.88 us -> 4.79 us  [run(): pl.pallas_call(kernel, out_shape=tuple((jax.ShapeDtypeStruct(s, F32) for...]
    ppermute x8 -> x12, waiting for transfers between devices: 8.5 us -> 8.52 us  [swap(): lax.ppermute(value, axis, [(i, i ^ k) for i in range(lax.axis_size(axis))])]
  transfers between devices with their start and end apart: 10 -> 14, of which waited for: 6 -> 5; matrix products, arithmetic and copies ran while one was open for 0% -> 0% of each run, Pallas kernels for 6% -> 6%
where the time goes in v4:
time: 30.8 us; the launch traced here: 30.7 us
  starting transfers between devices  16.6 us (54%)
  waiting for transfers between devices  8.52 us (28%)
  Pallas kernels  4.79 us (16%)
  between operations  0.7 us (2%)
    ppermute x12, starting transfers between devices, swap(): lax.ppermute(value, axis, [(i, i ^ k) for i in range(lax.axis_size(axis))])  14.5 us
    ppermute x12, waiting for transfers between devices, swap(): lax.ppermute(value, axis, [(i, i ^ k) for i in range(lax.axis_size(axis))])  8.52 us
    pallas_call x9, Pallas kernels, run(): pl.pallas_call(kernel, out_shape=tuple((jax.ShapeDtypeStruct(s, F32) for...  4.79 us
    ppermute x2, starting transfers between devices, swapped(): return lax.ppermute(value, ('gx', 'gy'), pairs)  2.11 us
  transfers between devices with their start and end apart: 14, of which 5 were waited for; matrix products, arithmetic and copies ran while one was open for 0% of the time, Pallas kernels for 6%

profile of v4, /device:TPU:0, one launch (start us, length us, event | category | flops | bytes accessed | tf_op | source)
XLA Modules:
  0.0 30.7 jit_solution(15590942704830708736)
XLA Ops:
  0.6 1.6 %shard_map.95 = (f32[16,16,128]{2,1,0:T(8,128)S(1)}, f32[16,16,128]{2,1,0:T(8,128)S(1)}, f32[16,16,128]{2,1,0:T(8,128)S(1)}, f32[16,16,128]{2,1,0:T(8,128)S(1)},...) custom-call(f32[16,16,128]{2,1,0:T(8,128)} %refs_0_.1, ...), custom_call_target="tpu_custom_call" | custom-call | flops 400000 | bytes 1048576 | tf_op jit(solution)/shard_map/pallas_call | solution.py:25
  2.3 3.0 %collective-permute-start = (f32[2,16,128]{2,1,0:T(8,128)S(1)}, f32[2,16,128]{2,1,0:T(8,128)S(1)}, u32[]{:S(2)}, u32[]{:S(2)}) collective-permute-start(f32[2,16,128]{2,1,0:T(8,128)S(1)} %get-tuple-element.51.mine), channel_id=1, source_target_pairs={{0,1},{1,0},{2,3},{3,2},{4,5},{5,4},{6,7},{7,6},{8,9},{9,8},{10,11... | collective-permute-start | bytes 49160 | tf_op jit(solution)/shard_map/ppermute | solution.py:172
  5.3 0.4 %shard_map.96 = (f32[2,16,16,128]{3,2,1,0:T(8,128)S(1)}, f32[2,16,16,128]{3,2,1,0:T(8,128)S(1)}, f32[2,16,16,128]{3,2,1,0:T(8,128)S(1)}, f32[2,16,16,128]{3,2,1,...) custom-call(f32[256,128]{1,0:T(8,128)S(1)} %bitcast.9, ...), custom_call_target="tpu_custom_call" | custom-call | flops 400000 | bytes 655360 | tf_op jit(solution)/shard_map/pallas_call | solution.py:25
  5.7 1.3 %collective-permute-done.tiles = f32[2,16,128]{2,1,0:T(8,128)S(1)} collective-permute-done((f32[2,16,128]{2,1,0:T(8,128)S(1)}, f32[2,16,128]{2,1,0:T(8,128)S(1)}, u32[]{:S(2)}, u32[]{:S(2)}) %collective-permute-start) | collective-permute-done | bytes 16416 | tf_op jit(solution)/shard_map/ppermute | solution.py:172
  7.0 2.1 %collective-permute-start.1 = (f32[3,16,128]{2,1,0:T(8,128)S(1)}, f32[3,16,128]{2,1,0:T(8,128)S(1)}, u32[]{:S(2)}, u32[]{:S(2)}) collective-permute-start(f32[3,16,128]{2,1,0:T(8,128)S(1)} %get-tuple-element.88), channel_id=1, source_target_pairs={{0,2},{2,0},{4,6},{6,4},{8,10},{10,8},{12,14},{14,12},{16,18},{18,... | collective-permute-start | bytes 73736 | tf_op jit(solution)/shard_map/ppermute | solution.py:486
  9.1 0.0 collective-permute-start.2
  9.1 0.5 %collective-permute-start.3 = (f32[4,2,16,128]{3,2,1,0:T(8,128)S(1)}, f32[4,2,16,128]{3,2,1,0:T(8,128)S(1)}, u32[]{:S(2)}, u32[]{:S(2)}) collective-permute-start(f32[4,2,16,128]{3,2,1,0:T(8,128)S(1)} %get-tuple-element.66.own), channel_id=1, source_target_pairs={{0,8},{8,0},{16,24},{24,16},{1,9},{9,1},{17,25},{25,17},{2,10},{10... | collective-permute-start | bytes 196616 | tf_op jit(solution)/shard_map/ppermute | solution.py:172
  9.6 2.6 %collective-permute-start.7 = (f32[4,2,16,128]{3,2,1,0:T(8,128)S(1)}, f32[4,2,16,128]{3,2,1,0:T(8,128)S(1)}, u32[]{:S(2)}, u32[]{:S(2)}) collective-permute-start(f32[4,2,16,128]{3,2,1,0:T(8,128)S(1)} %get-tuple-element.79.yown.own), channel_id=1, source_target_pairs={{0,2},{2,0},{4,6},{6,4},{1,3},{3,1},{5,7},{7,5},{8,10},{10,8},{12,... | collective-permute-start | bytes 196616 | tf_op jit(solution)/shard_map/ppermute | solution.py:172
  12.3 0.2 shard_map.98
  12.5 0.3 collective-permute-start.4
  12.8 0.9 %shard_map.97 = (f32[2,16,16,128]{3,2,1,0:T(8,128)S(1)}, f32[2,16,16,128]{3,2,1,0:T(8,128)S(1)}, f32[16,16,128]{2,1,0:T(8,128)S(1)}, f32[16,16,128]{2,1,0:T(8,128)S(1)}) custom-call(f32[16,16,128]{2,1,0:T(8,128)S(1)} %get-tuple-element.45.t, f32[16,16,128]{2,1,0:T(8,128)S(1)} %get-tuple-element.46.h, f32[16,16,128]{2,1,0:T(8,128)S(1)} %get-tuple-element.53.load, ...), custom_call_target="tpu_custom_call" | custom-call | flops 400000 | bytes 950272 | tf_op jit(solution)/shard_map/pallas_call | solution.py:25
  13.8 0.0 collective-permute-done.1
  13.8 0.0 collective-permute-done.2
  13.8 0.0 collective-permute-done.4.gnear
  13.8 0.0 collective-permute-done.3.near
  13.8 0.3 shard_map.99
  14.1 0.3 %collective-permute-start.5 = (f32[5,16,128]{2,1,0:T(8,128)S(1)}, f32[5,16,128]{2,1,0:T(8,128)S(1)}, u32[]{:S(2)}, u32[]{:S(2)}) collective-permute-start(f32[5,16,128]{2,1,0:T(8,128)S(1)} %get-tuple-element.74.ends), channel_id=1, source_target_pairs={{0,8},{8,0},{16,24},{24,16},{1,9},{9,1},{17,25},{25,17},{2,10},{10... | collective-permute-start | bytes 122888 | tf_op jit(solution)/shard_map/ppermute | solution.py:172
  14.4 1.4 %collective-permute-start.9 = (f32[3,16,128]{2,1,0:T(8,128)S(1)}, f32[3,16,128]{2,1,0:T(8,128)S(1)}, u32[]{:S(2)}, u32[]{:S(2)}) collective-permute-start(f32[3,16,128]{2,1,0:T(8,128)S(1)} %get-tuple-element.80), channel_id=1, source_target_pairs={{0,24},{8,16},{16,8},{24,0},{1,25},{9,17},{17,9},{25,1},{2,26},{10... | collective-permute-start | bytes 73736 | tf_op jit(solution)/shard_map/ppermute | solution.py:172
  15.8 0.5 %collective-permute-start.8 = (f32[3,16,128]{2,1,0:T(8,128)S(1)}, f32[3,16,128]{2,1,0:T(8,128)S(1)}, u32[]{:S(2)}, u32[]{:S(2)}) collective-permute-start(f32[3,16,128]{2,1,0:T(8,128)S(1)} %get-tuple-element.80), channel_id=1, source_target_pairs={{0,16},{8,24},{16,0},{24,8},{1,17},{9,25},{17,1},{25,9},{2,18},{10... | collective-permute-start | bytes 73736 | tf_op jit(solution)/shard_map/ppermute | solution.py:172
  16.3 1.6 %collective-permute-start.6 = (f32[2,16,128]{2,1,0:T(8,128)S(1)}, f32[2,16,128]{2,1,0:T(8,128)S(1)}, u32[]{:S(2)}, u32[]{:S(2)}) collective-permute-start(f32[2,16,128]{2,1,0:T(8,128)S(1)} %shard_map.100), channel_id=1, source_target_pairs={{0,16},{8,24},{16,0},{24,8},{1,17},{9,25},{17,1},{25,9},{2,18},{10... | collective-permute-start | bytes 49160 | tf_op jit(solution)/shard_map/ppermute | solution.py:172
  17.9 0.0 collective-permute-done.7.ynear.near
  17.9 2.2 %collective-permute-done.6.slopes = f32[2,16,128]{2,1,0:T(8,128)S(1)} collective-permute-done((f32[2,16,128]{2,1,0:T(8,128)S(1)}, f32[2,16,128]{2,1,0:T(8,128)S(1)}, u32[]{:S(2)}, u32[]{:S(2)}) %collective-permute-start.6) | collective-permute-done | bytes 16416 | tf_op jit(solution)/shard_map/ppermute | solution.py:172
  20.1 0.0 collective-permute-done.9.rest_1_
  20.1 0.0 collective-permute-done.8.rest_0_
  20.1 0.0 collective-permute-done.5.near_ends
  20.1 0.5 %shard_map.101 = (f32[2,16,16,128]{3,2,1,0:T(8,128)S(1)}, f32[4,16,128]{2,1,0:T(8,128)S(1)}, f32[2,16,128]{2,1,0:T(8,128)S(1)}) custom-call(f32[2,16,16,128]{3,2,1,0:T(8,128)S(1)} %get-tuple-element.68.p, f32[2,16,16,128]{3,2,1,0:T(8,128)S(1)} %get-tuple-element.69.q, f32[2,16,16,128]{3,2,1,0:T(8,128)S(1)} %get-tuple-element.70.r, ...), custom_call_target="tpu_custom_call" | custom-call | flops 400000 | bytes 3096576 | tf_op jit(solution)/shard_map/pallas_call | solution.py:25
  20.6 0.4 %collective-permute-start.10 = (f32[4,16,128]{2,1,0:T(8,128)S(1)}, f32[4,16,128]{2,1,0:T(8,128)S(1)}, u32[]{:S(2)}, u32[]{:S(2)}) collective-permute-start(f32[4,16,128]{2,1,0:T(8,128)S(1)} %get-tuple-element.84.ends), channel_id=1, source_target_pairs={{0,2},{2,0},{4,6},{6,4},{1,3},{3,1},{5,7},{7,5},{8,10},{10,8},{12,... | collective-permute-start | bytes 98312 | tf_op jit(solution)/shard_map/ppermute | solution.py:172
  21.0 3.0 %collective-permute-start.11 = (f32[2,16,128]{2,1,0:T(8,128)S(1)}, f32[2,16,128]{2,1,0:T(8,128)S(1)}, u32[]{:S(2)}, u32[]{:S(2)}) collective-permute-start(f32[2,16,128]{2,1,0:T(8,128)S(1)} %shard_map.102), channel_id=1, source_target_pairs={{0,6},{2,4},{4,2},{6,0},{1,7},{3,5},{5,3},{7,1},{8,14},{10,12},{12... | collective-permute-start | bytes 49160 | tf_op jit(solution)/shard_map/ppermute | solution.py:172
  24.0 0.9 %collective-permute-start.13 = (f32[2,16,128]{2,1,0:T(8,128)S(1)}, f32[2,16,128]{2,1,0:T(8,128)S(1)}, u32[]{:S(2)}, u32[]{:S(2)}) collective-permute-start(f32[2,16,128]{2,1,0:T(8,128)S(1)} %get-tuple-element.85), channel_id=1, source_target_pairs={{0,6},{2,4},{4,2},{6,0},{1,7},{3,5},{5,3},{7,1},{8,14},{10,12},{12... | collective-permute-start | bytes 49160 | tf_op jit(solution)/shard_map/ppermute | solution.py:172
  24.9 0.0 collective-permute-start.12
  24.9 1.9 %collective-permute-done.11.slopes = f32[2,16,128]{2,1,0:T(8,128)S(1)} collective-permute-done((f32[2,16,128]{2,1,0:T(8,128)S(1)}, f32[2,16,128]{2,1,0:T(8,128)S(1)}, u32[]{:S(2)}, u32[]{:S(2)}) %collective-permute-start.11) | collective-permute-done | bytes 16416 | tf_op jit(solution)/shard_map/ppermute | solution.py:172
  26.8 2.7 %collective-permute-done.13.rest_1_ = f32[2,16,128]{2,1,0:T(8,128)S(1)} collective-permute-done((f32[2,16,128]{2,1,0:T(8,128)S(1)}, f32[2,16,128]{2,1,0:T(8,128)S(1)}, u32[]{:S(2)}, u32[]{:S(2)}) %collective-permute-start.13) | collective-permute-done | bytes 16416 | tf_op jit(solution)/shard_map/ppermute | solution.py:172
  29.5 0.3 %collective-permute-done.12.rest_0_ = f32[2,16,128]{2,1,0:T(8,128)S(1)} collective-permute-done((f32[2,16,128]{2,1,0:T(8,128)S(1)}, f32[2,16,128]{2,1,0:T(8,128)S(1)}, u32[]{:S(2)}, u32[]{:S(2)}) %collective-permute-start.12) | collective-permute-done | bytes 16416 | tf_op jit(solution)/shard_map/ppermute | solution.py:172
  29.9 0.0 collective-permute-done.10.near_ends
  29.9 0.8 %shard_map.103 = (f32[256,128]{1,0:T(8,128)}, f32[256,128]{1,0:T(8,128)}) custom-call(f32[2,16,16,128]{3,2,1,0:T(8,128)S(1)} %get-tuple-element.81.p, f32[2,16,16,128]{3,2,1,0:T(8,128)S(1)} %get-tuple-element.82.q, f32[2,16,16,128]{3,2,1,0:T(8,128)S(1)} %get-tuple-element.83.r, f32[4,16,128]{2,1,0:T(8,128)S(1)} %get-tuple-element.84.ends, ...), custom_call_target="tpu_custom_call" | custom-call | flops 400000 | bytes 1032192 | tf_op jit(solution)/shard_map/pallas_call | solution.py:25
  (5 shorter events, 0.1 us)
Async XLA Ops:
  2.3 4.8 %collective-permute-start = (f32[2,16,128]{2,1,0:T(8,128)S(1)}, f32[2,16,128]{2,1,0:T(8,128)S(1)}, u32[]{:S(2)}, u32[]{:S(2)}) collective-permute-start(f32[2,16,128]{2,1,0:T(8,128)S(1)} %get-tuple-element.51.mine), channel_id=1, source_target_pairs={{0,1},{1,0},{2,3},{3,2},{4,5},{5,4},{6,7},{7,6},{8,9},{9,8},{10,11... | collective-permute-start | bytes 49160 | tf_op jit(solution)/shard_map/ppermute | solution.py:172
  7.0 6.7 %collective-permute-start.1 = (f32[3,16,128]{2,1,0:T(8,128)S(1)}, f32[3,16,128]{2,1,0:T(8,128)S(1)}, u32[]{:S(2)}, u32[]{:S(2)}) collective-permute-start(f32[3,16,128]{2,1,0:T(8,128)S(1)} %get-tuple-element.88), channel_id=1, source_target_pairs={{0,2},{2,0},{4,6},{6,4},{8,10},{10,8},{12,14},{14,12},{16,18},{18,... | collective-permute-start | bytes 73736 | tf_op jit(solution)/shard_map/ppermute | solution.py:486
  9.1 4.6 %collective-permute-start.2 = (f32[3,16,128]{2,1,0:T(8,128)S(1)}, f32[3,16,128]{2,1,0:T(8,128)S(1)}, u32[]{:S(2)}, u32[]{:S(2)}) collective-permute-start(f32[3,16,128]{2,1,0:T(8,128)S(1)} %get-tuple-element.89), channel_id=1, source_target_pairs={{0,8},{2,4},{4,2},{6,14},{8,0},{10,12},{12,10},{14,6},{16,24},{18,... | collective-permute-start | bytes 73736 | tf_op jit(solution)/shard_map/ppermute | solution.py:486
  9.1 4.7 %collective-permute-start.3 = (f32[4,2,16,128]{3,2,1,0:T(8,128)S(1)}, f32[4,2,16,128]{3,2,1,0:T(8,128)S(1)}, u32[]{:S(2)}, u32[]{:S(2)}) collective-permute-start(f32[4,2,16,128]{3,2,1,0:T(8,128)S(1)} %get-tuple-element.66.own), channel_id=1, source_target_pairs={{0,8},{8,0},{16,24},{24,16},{1,9},{9,1},{17,25},{25,17},{2,10},{10... | collective-permute-start | bytes 196616 | tf_op jit(solution)/shard_map/ppermute | solution.py:172
  9.6 8.3 %collective-permute-start.7 = (f32[4,2,16,128]{3,2,1,0:T(8,128)S(1)}, f32[4,2,16,128]{3,2,1,0:T(8,128)S(1)}, u32[]{:S(2)}, u32[]{:S(2)}) collective-permute-start(f32[4,2,16,128]{3,2,1,0:T(8,128)S(1)} %get-tuple-element.79.yown.own), channel_id=1, source_target_pairs={{0,2},{2,0},{4,6},{6,4},{1,3},{3,1},{5,7},{7,5},{8,10},{10,8},{12,... | collective-permute-start | bytes 196616 | tf_op jit(solution)/shard_map/ppermute | solution.py:172
  12.5 1.3 %collective-permute-start.4 = (f32[4,16,128]{2,1,0:T(8,128)S(1)}, f32[4,16,128]{2,1,0:T(8,128)S(1)}, u32[]{:S(2)}, u32[]{:S(2)}) collective-permute-start(f32[4,16,128]{2,1,0:T(8,128)S(1)} %get-tuple-element.67.gown), channel_id=1, source_target_pairs={{0,8},{8,0},{16,24},{24,16},{1,9},{9,1},{17,25},{25,17},{2,10},{10... | collective-permute-start | bytes 98312 | tf_op jit(solution)/shard_map/ppermute | solution.py:172
  14.1 6.0 %collective-permute-start.5 = (f32[5,16,128]{2,1,0:T(8,128)S(1)}, f32[5,16,128]{2,1,0:T(8,128)S(1)}, u32[]{:S(2)}, u32[]{:S(2)}) collective-permute-start(f32[5,16,128]{2,1,0:T(8,128)S(1)} %get-tuple-element.74.ends), channel_id=1, source_target_pairs={{0,8},{8,0},{16,24},{24,16},{1,9},{9,1},{17,25},{25,17},{2,10},{10... | collective-permute-start | bytes 122888 | tf_op jit(solution)/shard_map/ppermute | solution.py:172
  14.4 5.7 %collective-permute-start.9 = (f32[3,16,128]{2,1,0:T(8,128)S(1)}, f32[3,16,128]{2,1,0:T(8,128)S(1)}, u32[]{:S(2)}, u32[]{:S(2)}) collective-permute-start(f32[3,16,128]{2,1,0:T(8,128)S(1)} %get-tuple-element.80), channel_id=1, source_target_pairs={{0,24},{8,16},{16,8},{24,0},{1,25},{9,17},{17,9},{25,1},{2,26},{10... | collective-permute-start | bytes 73736 | tf_op jit(solution)/shard_map/ppermute | solution.py:172
  15.8 4.3 %collective-permute-start.8 = (f32[3,16,128]{2,1,0:T(8,128)S(1)}, f32[3,16,128]{2,1,0:T(8,128)S(1)}, u32[]{:S(2)}, u32[]{:S(2)}) collective-permute-start(f32[3,16,128]{2,1,0:T(8,128)S(1)} %get-tuple-element.80), channel_id=1, source_target_pairs={{0,16},{8,24},{16,0},{24,8},{1,17},{9,25},{17,1},{25,9},{2,18},{10... | collective-permute-start | bytes 73736 | tf_op jit(solution)/shard_map/ppermute | solution.py:172
  16.3 3.8 %collective-permute-start.6 = (f32[2,16,128]{2,1,0:T(8,128)S(1)}, f32[2,16,128]{2,1,0:T(8,128)S(1)}, u32[]{:S(2)}, u32[]{:S(2)}) collective-permute-start(f32[2,16,128]{2,1,0:T(8,128)S(1)} %shard_map.100), channel_id=1, source_target_pairs={{0,16},{8,24},{16,0},{24,8},{1,17},{9,25},{17,1},{25,9},{2,18},{10... | collective-permute-start | bytes 49160 | tf_op jit(solution)/shard_map/ppermute | solution.py:172
  20.6 9.3 %collective-permute-start.10 = (f32[4,16,128]{2,1,0:T(8,128)S(1)}, f32[4,16,128]{2,1,0:T(8,128)S(1)}, u32[]{:S(2)}, u32[]{:S(2)}) collective-permute-start(f32[4,16,128]{2,1,0:T(8,128)S(1)} %get-tuple-element.84.ends), channel_id=1, source_target_pairs={{0,2},{2,0},{4,6},{6,4},{1,3},{3,1},{5,7},{7,5},{8,10},{10,8},{12,... | collective-permute-start | bytes 98312 | tf_op jit(solution)/shard_map/ppermute | solution.py:172
  21.0 5.8 %collective-permute-start.11 = (f32[2,16,128]{2,1,0:T(8,128)S(1)}, f32[2,16,128]{2,1,0:T(8,128)S(1)}, u32[]{:S(2)}, u32[]{:S(2)}) collective-permute-start(f32[2,16,128]{2,1,0:T(8,128)S(1)} %shard_map.102), channel_id=1, source_target_pairs={{0,6},{2,4},{4,2},{6,0},{1,7},{3,5},{5,3},{7,1},{8,14},{10,12},{12... | collective-permute-start | bytes 49160 | tf_op jit(solution)/shard_map/ppermute | solution.py:172
  24.0 5.6 %collective-permute-start.13 = (f32[2,16,128]{2,1,0:T(8,128)S(1)}, f32[2,16,128]{2,1,0:T(8,128)S(1)}, u32[]{:S(2)}, u32[]{:S(2)}) collective-permute-start(f32[2,16,128]{2,1,0:T(8,128)S(1)} %get-tuple-element.85), channel_id=1, source_target_pairs={{0,6},{2,4},{4,2},{6,0},{1,7},{3,5},{5,3},{7,1},{8,14},{10,12},{12... | collective-permute-start | bytes 49160 | tf_op jit(solution)/shard_map/ppermute | solution.py:172
  24.9 5.0 %collective-permute-start.12 = (f32[2,16,128]{2,1,0:T(8,128)S(1)}, f32[2,16,128]{2,1,0:T(8,128)S(1)}, u32[]{:S(2)}, u32[]{:S(2)}) collective-permute-start(f32[2,16,128]{2,1,0:T(8,128)S(1)} %get-tuple-element.85), channel_id=1, source_target_pairs={{0,4},{2,6},{4,0},{6,2},{1,5},{3,7},{5,1},{7,3},{8,12},{10,14},{12... | collective-permute-start | bytes 49160 | tf_op jit(solution)/shard_map/ppermute | solution.py:172

commit v5 on v4

--- a/solution.py
+++ b/solution.py
@@ -343,6 +343,7 @@
 ):
     odd = lax.axis_index("gy") % 2
     half = ny // 2
+    slopes = []
     for f in range(2):
         for k in range(nx):
             low = faces[1 - odd, f, pl.ds(k, half, stride=0), :]
@@ -354,7 +355,8 @@
         )
         ends[2 * f], ends[2 * f + 1] = mine
         if paired:
-            word[0][f] = pair_source("gx", mine, coefs_of(own, f), coefs_of(near, f))[0]
+            word[0][f], slope = pair_source("gx", mine, coefs_of(own, f), coefs_of(near, f))
+            slopes.append(slope)
     low_row = faces[1 - odd, 2, pl.ds(ny - 1, half, stride=0), :]
     high_row = faces[odd, 2, pl.ds(0, half, stride=0), :]
     first = lax.broadcasted_iota(jnp.int32, low_row.shape, 1) < low_row.shape[1] // 2
@@ -375,6 +377,7 @@
     ends[4] = packed(*mine)
     if paired:
         word[0][2] = packed(*pair_source("gx", mine, x_coefs(own, gown, 2), x_coefs(near, gnear, 2)))
+        word[0][3] = jnp.where(place("gx")[2] == 0, slopes[0], slopes[1])
 
 
 def packed(a, b):
@@ -398,7 +401,7 @@
 
 
 def second_kernel(
-    paired, nx, ny, nz, p, q, r, gp, gq, gr, ends, near_ends, own, near, gown, gnear, slopes,
+    paired, nx, ny, nz, p, q, r, gp, gq, gr, ends, near_ends, own, near, gown, gnear,
     d, load, up, cz, yi, ym, yu, yown, ynear, *rest,
 ):
     far, (py, *outs, s) = rest[: 1 + paired[0]], rest[1 + paired[0] :]
@@ -408,7 +411,7 @@
         if paired[0]:
             two, three = far
             if f < 2:
-                word = two[f] + three[f], slopes[f]
+                word = two[f] + three[f], jnp.where(place("gx")[2] == f, two[3], three[3])
             else:
                 word, more = unpacked(two[2]), unpacked(three[2])
                 word = word[0] + more[0], word[1]
@@ -513,11 +516,9 @@
         + ((4, 2) + block_x, (4, 2) + block_y, (2,) + block_y, (2,) + block_y),
         *(a.reshape(flat) for a in (thermal, vapour, lat, cx, cy)),
     )
-    xnear, ynear, xslopes, yslopes = xown, yown, xown[0], yown[0]
+    xnear, ynear, yslopes = xown, yown, yown[0]
     if paired[0]:
         xnear = swap(xown, "gx", 1)
-        (xslopes,) = call(functools.partial(slope_kernel, "gx"), ((2,) + block_x,), xown, xnear)
-        xslopes = swap(xslopes, "gx", 2)
     if paired[1]:
         ynear = swap(yown, "gy", 1)
         (yslopes,) = call(functools.partial(slope_kernel, "gy"), ((2,) + block_y,), yown, ynear)
@@ -536,7 +537,7 @@
     gnear = swap(gown, "gx", 1) if paired[0] else gown
     d, p, gp, ends, *word = call(
         functools.partial(first_kernel, paired[0], nx, ny),
-        (lines_x, lines_x, (nx,) + block_x, (5,) + block_x) + ((3,) + block_x,) * paired[0],
+        (lines_x, lines_x, (nx,) + block_x, (5,) + block_x) + ((4,) + block_x,) * paired[0],
         jnp.stack([one, two]), d, side, gd, gside, xi, xm, xu, gi, gm, gu, xown, xnear, gown, gnear,
     )
     if paired[0]:
@@ -547,7 +548,7 @@
     py, yends, *outs = call(
         functools.partial(second_kernel, paired, nx, ny, nz),
         (lines_y, (4,) + block_y) + (((2,) + block_y,) if paired[1] else ()),
-        p, xq, xr, gp, gq, gr, ends, near_ends, xown, xnear, gown, gnear, xslopes,
+        p, xq, xr, gp, gq, gr, ends, near_ends, xown, xnear, gown, gnear,
         d, load, up, cz, yi, ym, yu, yown, ynear, *far,
         scratch=[pltpu.VMEM((2,) + flat, F32)],
     )

time: 30.8 us -> 30.4 us (0.987)
  starting transfers between devices: 16.6 us -> 15 us
  waiting for transfers between devices: 8.52 us -> 9.71 us
    ppermute x12 -> x11, starting transfers between devices: 14.5 us -> 12.9 us  [swap(): lax.ppermute(value, axis, [(i, i ^ k) for i in range(lax.axis_size(axis))])]
    ppermute x12 -> x11, waiting for transfers between devices: 8.52 us -> 9.7 us  [swap(): lax.ppermute(value, axis, [(i, i ^ k) for i in range(lax.axis_size(axis))])]
    pallas_call x9 -> x8, Pallas kernels: 4.79 us -> 4.78 us  [run(): pl.pallas_call(kernel, out_shape=tuple((jax.ShapeDtypeStruct(s, F32) for...]
  transfers between devices with their start and end apart: 14 -> 13, of which waited for: 5 -> 6; matrix products, arithmetic and copies ran while one was open for 0% -> 0% of each run, Pallas kernels for 6% -> 6%
where the time goes in v5:
time: 30.4 us; the launch traced here: 30.2 us
  starting transfers between devices  15 us (49%)
  waiting for transfers between devices  9.71 us (32%)
  Pallas kernels  4.78 us (16%)
  between operations  0.7 us (2%)
    ppermute x11, starting transfers between devices, swap(): lax.ppermute(value, axis, [(i, i ^ k) for i in range(lax.axis_size(axis))])  12.9 us
    ppermute x11, waiting for transfers between devices, swap(): lax.ppermute(value, axis, [(i, i ^ k) for i in range(lax.axis_size(axis))])  9.7 us
    pallas_call x8, Pallas kernels, run(): pl.pallas_call(kernel, out_shape=tuple((jax.ShapeDtypeStruct(s, F32) for...  4.78 us
    ppermute x2, starting transfers between devices, swapped(): return lax.ppermute(value, ('gx', 'gy'), pairs)  2.11 us
  transfers between devices with their start and end apart: 13, of which 6 were waited for; matrix products, arithmetic and copies ran while one was open for 0% of the time, Pallas kernels for 6%

profile of v5, /device:TPU:0, one launch (start us, length us, event | category | flops | bytes accessed | tf_op | source)
XLA Modules:
  0.0 30.2 jit_solution(17126928906548000638)
XLA Ops:
  0.6 1.6 %shard_map.95 = (f32[16,16,128]{2,1,0:T(8,128)S(1)}, f32[16,16,128]{2,1,0:T(8,128)S(1)}, f32[16,16,128]{2,1,0:T(8,128)S(1)}, f32[16,16,128]{2,1,0:T(8,128)S(1)},...) custom-call(f32[16,16,128]{2,1,0:T(8,128)} %refs_0_.1, ...), custom_call_target="tpu_custom_call" | custom-call | flops 400000 | bytes 1048576 | tf_op jit(solution)/shard_map/pallas_call | solution.py:25
  2.3 3.0 %collective-permute-start = (f32[2,16,128]{2,1,0:T(8,128)S(1)}, f32[2,16,128]{2,1,0:T(8,128)S(1)}, u32[]{:S(2)}, u32[]{:S(2)}) collective-permute-start(f32[2,16,128]{2,1,0:T(8,128)S(1)} %get-tuple-element.51.mine), channel_id=1, source_target_pairs={{0,1},{1,0},{2,3},{3,2},{4,5},{5,4},{6,7},{7,6},{8,9},{9,8},{10,11... | collective-permute-start | bytes 49160 | tf_op jit(solution)/shard_map/ppermute | solution.py:172
  5.3 0.4 %shard_map.96 = (f32[2,16,16,128]{3,2,1,0:T(8,128)S(1)}, f32[2,16,16,128]{3,2,1,0:T(8,128)S(1)}, f32[2,16,16,128]{3,2,1,0:T(8,128)S(1)}, f32[2,16,16,128]{3,2,1,...) custom-call(f32[256,128]{1,0:T(8,128)S(1)} %bitcast.9, ...), custom_call_target="tpu_custom_call" | custom-call | flops 400000 | bytes 655360 | tf_op jit(solution)/shard_map/pallas_call | solution.py:25
  5.7 1.3 %collective-permute-done.tiles = f32[2,16,128]{2,1,0:T(8,128)S(1)} collective-permute-done((f32[2,16,128]{2,1,0:T(8,128)S(1)}, f32[2,16,128]{2,1,0:T(8,128)S(1)}, u32[]{:S(2)}, u32[]{:S(2)}) %collective-permute-start) | collective-permute-done | bytes 16416 | tf_op jit(solution)/shard_map/ppermute | solution.py:172
  7.0 2.1 %collective-permute-start.1 = (f32[3,16,128]{2,1,0:T(8,128)S(1)}, f32[3,16,128]{2,1,0:T(8,128)S(1)}, u32[]{:S(2)}, u32[]{:S(2)}) collective-permute-start(f32[3,16,128]{2,1,0:T(8,128)S(1)} %get-tuple-element.88), channel_id=1, source_target_pairs={{0,2},{2,0},{4,6},{6,4},{8,10},{10,8},{12,14},{14,12},{16,18},{18,... | collective-permute-start | bytes 73736 | tf_op jit(solution)/shard_map/ppermute | solution.py:489
  9.1 0.0 collective-permute-start.2
  9.1 0.5 %collective-permute-start.3 = (f32[4,2,16,128]{3,2,1,0:T(8,128)S(1)}, f32[4,2,16,128]{3,2,1,0:T(8,128)S(1)}, u32[]{:S(2)}, u32[]{:S(2)}) collective-permute-start(f32[4,2,16,128]{3,2,1,0:T(8,128)S(1)} %get-tuple-element.66.own), channel_id=1, source_target_pairs={{0,8},{8,0},{16,24},{24,16},{1,9},{9,1},{17,25},{25,17},{2,10},{10... | collective-permute-start | bytes 196616 | tf_op jit(solution)/shard_map/ppermute | solution.py:172
  9.6 2.6 %collective-permute-start.6 = (f32[4,2,16,128]{3,2,1,0:T(8,128)S(1)}, f32[4,2,16,128]{3,2,1,0:T(8,128)S(1)}, u32[]{:S(2)}, u32[]{:S(2)}) collective-permute-start(f32[4,2,16,128]{3,2,1,0:T(8,128)S(1)} %get-tuple-element.79.yown.own), channel_id=1, source_target_pairs={{0,2},{2,0},{4,6},{6,4},{1,3},{3,1},{5,7},{7,5},{8,10},{10,8},{12,... | collective-permute-start | bytes 196616 | tf_op jit(solution)/shard_map/ppermute | solution.py:172
  12.3 0.2 shard_map.98
  12.5 0.3 collective-permute-start.4
  12.8 0.9 %shard_map.97 = (f32[2,16,16,128]{3,2,1,0:T(8,128)S(1)}, f32[2,16,16,128]{3,2,1,0:T(8,128)S(1)}, f32[16,16,128]{2,1,0:T(8,128)S(1)}, f32[16,16,128]{2,1,0:T(8,128)S(1)}) custom-call(f32[16,16,128]{2,1,0:T(8,128)S(1)} %get-tuple-element.45.t, f32[16,16,128]{2,1,0:T(8,128)S(1)} %get-tuple-element.46.h, f32[16,16,128]{2,1,0:T(8,128)S(1)} %get-tuple-element.53.load, ...), custom_call_target="tpu_custom_call" | custom-call | flops 400000 | bytes 950272 | tf_op jit(solution)/shard_map/pallas_call | solution.py:25
  13.8 0.0 collective-permute-done.1
  13.8 0.0 collective-permute-done.2
  13.8 0.0 collective-permute-done.4.gnear
  13.8 0.0 collective-permute-done.3.near
  13.8 0.3 shard_map.99
  14.1 0.3 %collective-permute-start.5 = (f32[5,16,128]{2,1,0:T(8,128)S(1)}, f32[5,16,128]{2,1,0:T(8,128)S(1)}, u32[]{:S(2)}, u32[]{:S(2)}) collective-permute-start(f32[5,16,128]{2,1,0:T(8,128)S(1)} %get-tuple-element.74.ends), channel_id=1, source_target_pairs={{0,8},{8,0},{16,24},{24,16},{1,9},{9,1},{17,25},{25,17},{2,10},{10... | collective-permute-start | bytes 122888 | tf_op jit(solution)/shard_map/ppermute | solution.py:172
  14.5 1.4 %collective-permute-start.8 = (f32[4,16,128]{2,1,0:T(8,128)S(1)}, f32[4,16,128]{2,1,0:T(8,128)S(1)}, u32[]{:S(2)}, u32[]{:S(2)}) collective-permute-start(f32[4,16,128]{2,1,0:T(8,128)S(1)} %get-tuple-element.80), channel_id=1, source_target_pairs={{0,24},{8,16},{16,8},{24,0},{1,25},{9,17},{17,9},{25,1},{2,26},{10... | collective-permute-start | bytes 98312 | tf_op jit(solution)/shard_map/ppermute | solution.py:172
  15.8 0.5 %collective-permute-start.7 = (f32[4,16,128]{2,1,0:T(8,128)S(1)}, f32[4,16,128]{2,1,0:T(8,128)S(1)}, u32[]{:S(2)}, u32[]{:S(2)}) collective-permute-start(f32[4,16,128]{2,1,0:T(8,128)S(1)} %get-tuple-element.80), channel_id=1, source_target_pairs={{0,16},{8,24},{16,0},{24,8},{1,17},{9,25},{17,1},{25,9},{2,18},{10... | collective-permute-start | bytes 98312 | tf_op jit(solution)/shard_map/ppermute | solution.py:172
  16.3 0.0 collective-permute-done.6.ynear.near
  16.3 1.5 %collective-permute-done.8.rest_1_ = f32[4,16,128]{2,1,0:T(8,128)S(1)} collective-permute-done((f32[4,16,128]{2,1,0:T(8,128)S(1)}, f32[4,16,128]{2,1,0:T(8,128)S(1)}, u32[]{:S(2)}, u32[]{:S(2)}) %collective-permute-start.8) | collective-permute-done | bytes 32800 | tf_op jit(solution)/shard_map/ppermute | solution.py:172
  17.8 1.9 %collective-permute-done.7.rest_0_ = f32[4,16,128]{2,1,0:T(8,128)S(1)} collective-permute-done((f32[4,16,128]{2,1,0:T(8,128)S(1)}, f32[4,16,128]{2,1,0:T(8,128)S(1)}, u32[]{:S(2)}, u32[]{:S(2)}) %collective-permute-start.7) | collective-permute-done | bytes 32800 | tf_op jit(solution)/shard_map/ppermute | solution.py:172
  19.7 0.0 collective-permute-done.5.near_ends
  19.7 0.5 %shard_map.100 = (f32[2,16,16,128]{3,2,1,0:T(8,128)S(1)}, f32[4,16,128]{2,1,0:T(8,128)S(1)}, f32[2,16,128]{2,1,0:T(8,128)S(1)}) custom-call(f32[2,16,16,128]{3,2,1,0:T(8,128)S(1)} %get-tuple-element.68.p, f32[2,16,16,128]{3,2,1,0:T(8,128)S(1)} %get-tuple-element.69.q, f32[2,16,16,128]{3,2,1,0:T(8,128)S(1)} %get-tuple-element.70.r, ...), custom_call_target="tpu_custom_call" | custom-call | flops 400000 | bytes 3096576 | tf_op jit(solution)/shard_map/pallas_call | solution.py:25
  20.2 0.4 %collective-permute-start.9 = (f32[4,16,128]{2,1,0:T(8,128)S(1)}, f32[4,16,128]{2,1,0:T(8,128)S(1)}, u32[]{:S(2)}, u32[]{:S(2)}) collective-permute-start(f32[4,16,128]{2,1,0:T(8,128)S(1)} %get-tuple-element.84.ends), channel_id=1, source_target_pairs={{0,2},{2,0},{4,6},{6,4},{1,3},{3,1},{5,7},{7,5},{8,10},{10,8},{12,... | collective-permute-start | bytes 98312 | tf_op jit(solution)/shard_map/ppermute | solution.py:172
  20.6 3.0 %collective-permute-start.10 = (f32[2,16,128]{2,1,0:T(8,128)S(1)}, f32[2,16,128]{2,1,0:T(8,128)S(1)}, u32[]{:S(2)}, u32[]{:S(2)}) collective-permute-start(f32[2,16,128]{2,1,0:T(8,128)S(1)} %shard_map.101), channel_id=1, source_target_pairs={{0,6},{2,4},{4,2},{6,0},{1,7},{3,5},{5,3},{7,1},{8,14},{10,12},{12... | collective-permute-start | bytes 49160 | tf_op jit(solution)/shard_map/ppermute | solution.py:172
  23.6 0.9 %collective-permute-start.12 = (f32[2,16,128]{2,1,0:T(8,128)S(1)}, f32[2,16,128]{2,1,0:T(8,128)S(1)}, u32[]{:S(2)}, u32[]{:S(2)}) collective-permute-start(f32[2,16,128]{2,1,0:T(8,128)S(1)} %get-tuple-element.85), channel_id=1, source_target_pairs={{0,6},{2,4},{4,2},{6,0},{1,7},{3,5},{5,3},{7,1},{8,14},{10,12},{12... | collective-permute-start | bytes 49160 | tf_op jit(solution)/shard_map/ppermute | solution.py:172
  24.5 0.0 collective-permute-start.11
  24.5 1.8 %collective-permute-done.10.slopes = f32[2,16,128]{2,1,0:T(8,128)S(1)} collective-permute-done((f32[2,16,128]{2,1,0:T(8,128)S(1)}, f32[2,16,128]{2,1,0:T(8,128)S(1)}, u32[]{:S(2)}, u32[]{:S(2)}) %collective-permute-start.10) | collective-permute-done | bytes 16416 | tf_op jit(solution)/shard_map/ppermute | solution.py:172
  26.3 2.8 %collective-permute-done.12.rest_1_ = f32[2,16,128]{2,1,0:T(8,128)S(1)} collective-permute-done((f32[2,16,128]{2,1,0:T(8,128)S(1)}, f32[2,16,128]{2,1,0:T(8,128)S(1)}, u32[]{:S(2)}, u32[]{:S(2)}) %collective-permute-start.12) | collective-permute-done | bytes 16416 | tf_op jit(solution)/shard_map/ppermute | solution.py:172
  29.1 0.3 %collective-permute-done.11.rest_0_ = f32[2,16,128]{2,1,0:T(8,128)S(1)} collective-permute-done((f32[2,16,128]{2,1,0:T(8,128)S(1)}, f32[2,16,128]{2,1,0:T(8,128)S(1)}, u32[]{:S(2)}, u32[]{:S(2)}) %collective-permute-start.11) | collective-permute-done | bytes 16416 | tf_op jit(solution)/shard_map/ppermute | solution.py:172
  29.4 0.0 collective-permute-done.9.near_ends
  29.5 0.8 %shard_map.102 = (f32[256,128]{1,0:T(8,128)}, f32[256,128]{1,0:T(8,128)}) custom-call(f32[2,16,16,128]{3,2,1,0:T(8,128)S(1)} %get-tuple-element.81.p, f32[2,16,16,128]{3,2,1,0:T(8,128)S(1)} %get-tuple-element.82.q, f32[2,16,16,128]{3,2,1,0:T(8,128)S(1)} %get-tuple-element.83.r, f32[4,16,128]{2,1,0:T(8,128)S(1)} %get-tuple-element.84.ends, ...), custom_call_target="tpu_custom_call" | custom-call | flops 400000 | bytes 1032192 | tf_op jit(solution)/shard_map/pallas_call | solution.py:25
  (4 shorter events, 0.0 us)
Async XLA Ops:
  2.3 4.8 %collective-permute-start = (f32[2,16,128]{2,1,0:T(8,128)S(1)}, f32[2,16,128]{2,1,0:T(8,128)S(1)}, u32[]{:S(2)}, u32[]{:S(2)}) collective-permute-start(f32[2,16,128]{2,1,0:T(8,128)S(1)} %get-tuple-element.51.mine), channel_id=1, source_target_pairs={{0,1},{1,0},{2,3},{3,2},{4,5},{5,4},{6,7},{7,6},{8,9},{9,8},{10,11... | collective-permute-start | bytes 49160 | tf_op jit(solution)/shard_map/ppermute | solution.py:172
  7.0 6.7 %collective-permute-start.1 = (f32[3,16,128]{2,1,0:T(8,128)S(1)}, f32[3,16,128]{2,1,0:T(8,128)S(1)}, u32[]{:S(2)}, u32[]{:S(2)}) collective-permute-start(f32[3,16,128]{2,1,0:T(8,128)S(1)} %get-tuple-element.88), channel_id=1, source_target_pairs={{0,2},{2,0},{4,6},{6,4},{8,10},{10,8},{12,14},{14,12},{16,18},{18,... | collective-permute-start | bytes 73736 | tf_op jit(solution)/shard_map/ppermute | solution.py:489
  9.1 4.6 %collective-permute-start.2 = (f32[3,16,128]{2,1,0:T(8,128)S(1)}, f32[3,16,128]{2,1,0:T(8,128)S(1)}, u32[]{:S(2)}, u32[]{:S(2)}) collective-permute-start(f32[3,16,128]{2,1,0:T(8,128)S(1)} %get-tuple-element.89), channel_id=1, source_target_pairs={{0,8},{2,4},{4,2},{6,14},{8,0},{10,12},{12,10},{14,6},{16,24},{18,... | collective-permute-start | bytes 73736 | tf_op jit(solution)/shard_map/ppermute | solution.py:489
  9.1 4.7 %collective-permute-start.3 = (f32[4,2,16,128]{3,2,1,0:T(8,128)S(1)}, f32[4,2,16,128]{3,2,1,0:T(8,128)S(1)}, u32[]{:S(2)}, u32[]{:S(2)}) collective-permute-start(f32[4,2,16,128]{3,2,1,0:T(8,128)S(1)} %get-tuple-element.66.own), channel_id=1, source_target_pairs={{0,8},{8,0},{16,24},{24,16},{1,9},{9,1},{17,25},{25,17},{2,10},{10... | collective-permute-start | bytes 196616 | tf_op jit(solution)/shard_map/ppermute | solution.py:172
  9.6 6.7 %collective-permute-start.6 = (f32[4,2,16,128]{3,2,1,0:T(8,128)S(1)}, f32[4,2,16,128]{3,2,1,0:T(8,128)S(1)}, u32[]{:S(2)}, u32[]{:S(2)}) collective-permute-start(f32[4,2,16,128]{3,2,1,0:T(8,128)S(1)} %get-tuple-element.79.yown.own), channel_id=1, source_target_pairs={{0,2},{2,0},{4,6},{6,4},{1,3},{3,1},{5,7},{7,5},{8,10},{10,8},{12,... | collective-permute-start | bytes 196616 | tf_op jit(solution)/shard_map/ppermute | solution.py:172
  12.5 1.3 %collective-permute-start.4 = (f32[4,16,128]{2,1,0:T(8,128)S(1)}, f32[4,16,128]{2,1,0:T(8,128)S(1)}, u32[]{:S(2)}, u32[]{:S(2)}) collective-permute-start(f32[4,16,128]{2,1,0:T(8,128)S(1)} %get-tuple-element.67.gown), channel_id=1, source_target_pairs={{0,8},{8,0},{16,24},{24,16},{1,9},{9,1},{17,25},{25,17},{2,10},{10... | collective-permute-start | bytes 98312 | tf_op jit(solution)/shard_map/ppermute | solution.py:172
  14.1 5.6 %collective-permute-start.5 = (f32[5,16,128]{2,1,0:T(8,128)S(1)}, f32[5,16,128]{2,1,0:T(8,128)S(1)}, u32[]{:S(2)}, u32[]{:S(2)}) collective-permute-start(f32[5,16,128]{2,1,0:T(8,128)S(1)} %get-tuple-element.74.ends), channel_id=1, source_target_pairs={{0,8},{8,0},{16,24},{24,16},{1,9},{9,1},{17,25},{25,17},{2,10},{10... | collective-permute-start | bytes 122888 | tf_op jit(solution)/shard_map/ppermute | solution.py:172
  14.5 3.3 %collective-permute-start.8 = (f32[4,16,128]{2,1,0:T(8,128)S(1)}, f32[4,16,128]{2,1,0:T(8,128)S(1)}, u32[]{:S(2)}, u32[]{:S(2)}) collective-permute-start(f32[4,16,128]{2,1,0:T(8,128)S(1)} %get-tuple-element.80), channel_id=1, source_target_pairs={{0,24},{8,16},{16,8},{24,0},{1,25},{9,17},{17,9},{25,1},{2,26},{10... | collective-permute-start | bytes 98312 | tf_op jit(solution)/shard_map/ppermute | solution.py:172
  15.8 3.9 %collective-permute-start.7 = (f32[4,16,128]{2,1,0:T(8,128)S(1)}, f32[4,16,128]{2,1,0:T(8,128)S(1)}, u32[]{:S(2)}, u32[]{:S(2)}) collective-permute-start(f32[4,16,128]{2,1,0:T(8,128)S(1)} %get-tuple-element.80), channel_id=1, source_target_pairs={{0,16},{8,24},{16,0},{24,8},{1,17},{9,25},{17,1},{25,9},{2,18},{10... | collective-permute-start | bytes 98312 | tf_op jit(solution)/shard_map/ppermute | solution.py:172
  20.2 9.3 %collective-permute-start.9 = (f32[4,16,128]{2,1,0:T(8,128)S(1)}, f32[4,16,128]{2,1,0:T(8,128)S(1)}, u32[]{:S(2)}, u32[]{:S(2)}) collective-permute-start(f32[4,16,128]{2,1,0:T(8,128)S(1)} %get-tuple-element.84.ends), channel_id=1, source_target_pairs={{0,2},{2,0},{4,6},{6,4},{1,3},{3,1},{5,7},{7,5},{8,10},{10,8},{12,... | collective-permute-start | bytes 98312 | tf_op jit(solution)/shard_map/ppermute | solution.py:172
  20.6 5.7 %collective-permute-start.10 = (f32[2,16,128]{2,1,0:T(8,128)S(1)}, f32[2,16,128]{2,1,0:T(8,128)S(1)}, u32[]{:S(2)}, u32[]{:S(2)}) collective-permute-start(f32[2,16,128]{2,1,0:T(8,128)S(1)} %shard_map.101), channel_id=1, source_target_pairs={{0,6},{2,4},{4,2},{6,0},{1,7},{3,5},{5,3},{7,1},{8,14},{10,12},{12... | collective-permute-start | bytes 49160 | tf_op jit(solution)/shard_map/ppermute | solution.py:172
  23.6 5.6 %collective-permute-start.12 = (f32[2,16,128]{2,1,0:T(8,128)S(1)}, f32[2,16,128]{2,1,0:T(8,128)S(1)}, u32[]{:S(2)}, u32[]{:S(2)}) collective-permute-start(f32[2,16,128]{2,1,0:T(8,128)S(1)} %get-tuple-element.85), channel_id=1, source_target_pairs={{0,6},{2,4},{4,2},{6,0},{1,7},{3,5},{5,3},{7,1},{8,14},{10,12},{12... | collective-permute-start | bytes 49160 | tf_op jit(solution)/shard_map/ppermute | solution.py:172
  24.5 5.0 %collective-permute-start.11 = (f32[2,16,128]{2,1,0:T(8,128)S(1)}, f32[2,16,128]{2,1,0:T(8,128)S(1)}, u32[]{:S(2)}, u32[]{:S(2)}) collective-permute-start(f32[2,16,128]{2,1,0:T(8,128)S(1)} %get-tuple-element.85), channel_id=1, source_target_pairs={{0,4},{2,6},{4,0},{6,2},{1,5},{3,7},{5,1},{7,3},{8,12},{10,14},{12... | collective-permute-start | bytes 49160 | tf_op jit(solution)/shard_map/ppermute | solution.py:172

commit v6 on v5

--- a/solution.py
+++ b/solution.py
@@ -147,6 +147,26 @@
     return pick(second, (front, back), (back, front))
 
 
+def near_word(axis, ends, own, slope):
+    mine = oriented(axis, ends, own)
+    r1, r2 = mine[4:]
+    inner = mine[0] + r1 * slope / (1.0 - r2 * slope) * mine[1]
+    return jnp.where(place(axis)[1], mine[1], inner)
+
+
+def word_values(axis, ends, word, own, near, far):
+    second, outer, _ = place(axis)
+    zero = jnp.zeros_like(word)
+    source, slope = far
+    mine = oriented(axis, ends, own)
+    q1, q2, r1, r2 = oriented(axis, (zero, zero), near)[2:]
+    step = r1 * slope / (1.0 - r2 * slope)
+    ahead = pick(outer, (word + (r1 + step * r2) * source, q1 + step * q2), far)
+    behind = pick(outer, (zero, zero), (word, r2))
+    back, front = beside(mine, behind, ahead)
+    return pick(second, (front, back), (back, front))
+
+
 def scan_values(axis, mine, port_of):
     me, n = lax.axis_index(axis), lax.axis_size(axis)
     zero = jnp.zeros_like(mine[0])
@@ -450,17 +470,20 @@
             outs[1][f] = pair_source("gy", mine, coefs_of(yown, f), coefs_of(ynear, f))[0]
 
 
-def new_kernel(paired, nx, ny, p, q, r, ends, near_ends, own, near, slopes, *rest):
+def word_kernel(ends, own, slopes, out):
+    for f in range(2):
+        out[f] = near_word("gy", (ends[2 * f], ends[2 * f + 1]), coefs_of(own, f), slopes[f])
+
+
+def new_kernel(paired, nx, ny, p, q, r, ends, word, own, near, slopes, *rest):
     received, news = rest[:-2], rest[-2:]
     for f, ref in enumerate(news):
         mine = (ends[2 * f], ends[2 * f + 1])
         coefs = coefs_of(own, f)
         if paired:
-            other = (near_ends[2 * f], near_ends[2 * f + 1])
             two, three = received
-            low, high = pair_values(
-                "gy", mine, other, coefs, coefs_of(near, f), (two[f] + three[f], slopes[f])
-            )
+            far = two[f] + three[f], slopes[f]
+            low, high = word_values("gy", mine, word[f], coefs, coefs_of(near, f), far)
         else:
             (ports,) = received
 
@@ -554,13 +577,14 @@
     )
     if paired[1]:
         received = [swap(outs[0], "gy", k) for k in (2, 3)]
-        near_ends = swap(yends, "gy", 1)
+        (word,) = call(word_kernel, ((2,) + block_y,), yends, yown, yslopes)
+        word = swap(word, "gy", 1)
     else:
-        near_ends, received = yends, [everyones("gy", yends, yown)]
+        word, received = yends, [everyones("gy", yends, yown)]
     t_new, h_new = call(
         functools.partial(new_kernel, paired[1], nx, ny),
         (flat, flat),
-        py, yq, yr, yends, near_ends, yown, ynear, yslopes, *received,
+        py, yq, yr, yends, word, yown, ynear, yslopes, *received,
     )
     return t_new.reshape(thermal.shape), h_new.reshape(thermal.shape)
 

time: 30.4 us -> 29.1 us (0.957)
  waiting for transfers between devices: 9.71 us -> 7.62 us
  starting transfers between devices: 15 us -> 15.9 us
    ppermute x11, waiting for transfers between devices: 9.7 us -> 7.61 us  [swap(): lax.ppermute(value, axis, [(i, i ^ k) for i in range(lax.axis_size(axis))])]
    ppermute x11, starting transfers between devices: 12.9 us -> 13.8 us  [swap(): lax.ppermute(value, axis, [(i, i ^ k) for i in range(lax.axis_size(axis))])]
    pallas_call x8 -> x9, Pallas kernels: 4.78 us -> 4.79 us  [run(): pl.pallas_call(kernel, out_shape=tuple((jax.ShapeDtypeStruct(s, F32) for...]
  transfers between devices with their start and end apart: 13 -> 13, of which waited for: 6 -> 6; matrix products, arithmetic and copies ran while one was open for 0% -> 0% of each run, Pallas kernels for 6% -> 8%
where the time goes in v6:
time: 29.1 us; the launch traced here: 29 us
  starting transfers between devices  15.9 us (55%)
  waiting for transfers between devices  7.62 us (26%)
  Pallas kernels  4.79 us (16%)
  between operations  0.71 us (2%)
    ppermute x11, starting transfers between devices, swap(): lax.ppermute(value, axis, [(i, i ^ k) for i in range(lax.axis_size(axis))])  13.8 us
    ppermute x11, waiting for transfers between devices, swap(): lax.ppermute(value, axis, [(i, i ^ k) for i in range(lax.axis_size(axis))])  7.61 us
    pallas_call x9, Pallas kernels, run(): pl.pallas_call(kernel, out_shape=tuple((jax.ShapeDtypeStruct(s, F32) for...  4.79 us
    ppermute x2, starting transfers between devices, swapped(): return lax.ppermute(value, ('gx', 'gy'), pairs)  2.11 us
  transfers between devices with their start and end apart: 13, of which 6 were waited for; matrix products, arithmetic and copies ran while one was open for 0% of the time, Pallas kernels for 8%

profile of v6, /device:TPU:0, one launch (start us, length us, event | category | flops | bytes accessed | tf_op | source)
XLA Modules:
  0.0 29.0 jit_solution(7286119861907399393)
XLA Ops:
  0.6 1.6 %shard_map.95 = (f32[16,16,128]{2,1,0:T(8,128)S(1)}, f32[16,16,128]{2,1,0:T(8,128)S(1)}, f32[16,16,128]{2,1,0:T(8,128)S(1)}, f32[16,16,128]{2,1,0:T(8,128)S(1)},...) custom-call(f32[16,16,128]{2,1,0:T(8,128)} %refs_0_.1, ...), custom_call_target="tpu_custom_call" | custom-call | flops 400000 | bytes 1048576 | tf_op jit(solution)/shard_map/pallas_call | solution.py:25
  2.3 3.0 %collective-permute-start = (f32[2,16,128]{2,1,0:T(8,128)S(1)}, f32[2,16,128]{2,1,0:T(8,128)S(1)}, u32[]{:S(2)}, u32[]{:S(2)}) collective-permute-start(f32[2,16,128]{2,1,0:T(8,128)S(1)} %get-tuple-element.51.mine), channel_id=1, source_target_pairs={{0,1},{1,0},{2,3},{3,2},{4,5},{5,4},{6,7},{7,6},{8,9},{9,8},{10,11... | collective-permute-start | bytes 49160 | tf_op jit(solution)/shard_map/ppermute | solution.py:192
  5.3 0.4 %shard_map.96 = (f32[2,16,16,128]{3,2,1,0:T(8,128)S(1)}, f32[2,16,16,128]{3,2,1,0:T(8,128)S(1)}, f32[2,16,16,128]{3,2,1,0:T(8,128)S(1)}, f32[2,16,16,128]{3,2,1,...) custom-call(f32[256,128]{1,0:T(8,128)S(1)} %bitcast.9, ...), custom_call_target="tpu_custom_call" | custom-call | flops 400000 | bytes 655360 | tf_op jit(solution)/shard_map/pallas_call | solution.py:25
  5.7 1.3 %collective-permute-done.tiles = f32[2,16,128]{2,1,0:T(8,128)S(1)} collective-permute-done((f32[2,16,128]{2,1,0:T(8,128)S(1)}, f32[2,16,128]{2,1,0:T(8,128)S(1)}, u32[]{:S(2)}, u32[]{:S(2)}) %collective-permute-start) | collective-permute-done | bytes 16416 | tf_op jit(solution)/shard_map/ppermute | solution.py:192
  7.0 2.1 %collective-permute-start.1 = (f32[3,16,128]{2,1,0:T(8,128)S(1)}, f32[3,16,128]{2,1,0:T(8,128)S(1)}, u32[]{:S(2)}, u32[]{:S(2)}) collective-permute-start(f32[3,16,128]{2,1,0:T(8,128)S(1)} %get-tuple-element.88), channel_id=1, source_target_pairs={{0,2},{2,0},{4,6},{6,4},{8,10},{10,8},{12,14},{14,12},{16,18},{18,... | collective-permute-start | bytes 73736 | tf_op jit(solution)/shard_map/ppermute | solution.py:512
  9.1 0.0 collective-permute-start.2
  9.1 0.5 %collective-permute-start.3 = (f32[4,2,16,128]{3,2,1,0:T(8,128)S(1)}, f32[4,2,16,128]{3,2,1,0:T(8,128)S(1)}, u32[]{:S(2)}, u32[]{:S(2)}) collective-permute-start(f32[4,2,16,128]{3,2,1,0:T(8,128)S(1)} %get-tuple-element.66.own), channel_id=1, source_target_pairs={{0,8},{8,0},{16,24},{24,16},{1,9},{9,1},{17,25},{25,17},{2,10},{10... | collective-permute-start | bytes 196616 | tf_op jit(solution)/shard_map/ppermute | solution.py:192
  9.6 2.6 %collective-permute-start.6 = (f32[4,2,16,128]{3,2,1,0:T(8,128)S(1)}, f32[4,2,16,128]{3,2,1,0:T(8,128)S(1)}, u32[]{:S(2)}, u32[]{:S(2)}) collective-permute-start(f32[4,2,16,128]{3,2,1,0:T(8,128)S(1)} %get-tuple-element.79.yown.own), channel_id=1, source_target_pairs={{0,2},{2,0},{4,6},{6,4},{1,3},{3,1},{5,7},{7,5},{8,10},{10,8},{12,... | collective-permute-start | bytes 196616 | tf_op jit(solution)/shard_map/ppermute | solution.py:192
  12.3 0.2 shard_map.98
  12.5 0.3 %collective-permute-start.4 = (f32[4,16,128]{2,1,0:T(8,128)S(1)}, f32[4,16,128]{2,1,0:T(8,128)S(1)}, u32[]{:S(2)}, u32[]{:S(2)}) collective-permute-start(f32[4,16,128]{2,1,0:T(8,128)S(1)} %get-tuple-element.67.gown), channel_id=1, source_target_pairs={{0,8},{8,0},{16,24},{24,16},{1,9},{9,1},{17,25},{25,17},{2,10},{10... | collective-permute-start | bytes 98312 | tf_op jit(solution)/shard_map/ppermute | solution.py:192
  12.8 0.9 %shard_map.97 = (f32[2,16,16,128]{3,2,1,0:T(8,128)S(1)}, f32[2,16,16,128]{3,2,1,0:T(8,128)S(1)}, f32[16,16,128]{2,1,0:T(8,128)S(1)}, f32[16,16,128]{2,1,0:T(8,128)S(1)}) custom-call(f32[16,16,128]{2,1,0:T(8,128)S(1)} %get-tuple-element.45.t, f32[16,16,128]{2,1,0:T(8,128)S(1)} %get-tuple-element.46.h, f32[16,16,128]{2,1,0:T(8,128)S(1)} %get-tuple-element.53.load, ...), custom_call_target="tpu_custom_call" | custom-call | flops 400000 | bytes 950272 | tf_op jit(solution)/shard_map/pallas_call | solution.py:25
  13.8 0.0 collective-permute-done.1
  13.8 0.0 collective-permute-done.2
  13.8 0.0 collective-permute-done.4.gnear
  13.8 0.0 collective-permute-done.3.near
  13.8 0.3 shard_map.99
  14.1 0.3 %collective-permute-start.5 = (f32[5,16,128]{2,1,0:T(8,128)S(1)}, f32[5,16,128]{2,1,0:T(8,128)S(1)}, u32[]{:S(2)}, u32[]{:S(2)}) collective-permute-start(f32[5,16,128]{2,1,0:T(8,128)S(1)} %get-tuple-element.74.ends), channel_id=1, source_target_pairs={{0,8},{8,0},{16,24},{24,16},{1,9},{9,1},{17,25},{25,17},{2,10},{10... | collective-permute-start | bytes 122888 | tf_op jit(solution)/shard_map/ppermute | solution.py:192
  14.5 1.4 %collective-permute-start.8 = (f32[4,16,128]{2,1,0:T(8,128)S(1)}, f32[4,16,128]{2,1,0:T(8,128)S(1)}, u32[]{:S(2)}, u32[]{:S(2)}) collective-permute-start(f32[4,16,128]{2,1,0:T(8,128)S(1)} %get-tuple-element.80), channel_id=1, source_target_pairs={{0,24},{8,16},{16,8},{24,0},{1,25},{9,17},{17,9},{25,1},{2,26},{10... | collective-permute-start | bytes 98312 | tf_op jit(solution)/shard_map/ppermute | solution.py:192
  15.8 0.5 %collective-permute-start.7 = (f32[4,16,128]{2,1,0:T(8,128)S(1)}, f32[4,16,128]{2,1,0:T(8,128)S(1)}, u32[]{:S(2)}, u32[]{:S(2)}) collective-permute-start(f32[4,16,128]{2,1,0:T(8,128)S(1)} %get-tuple-element.80), channel_id=1, source_target_pairs={{0,16},{8,24},{16,0},{24,8},{1,17},{9,25},{17,1},{25,9},{2,18},{10... | collective-permute-start | bytes 98312 | tf_op jit(solution)/shard_map/ppermute | solution.py:192
  16.3 0.0 collective-permute-done.6.ynear.near
  16.3 1.5 %collective-permute-start.9 = (f32[2,16,128]{2,1,0:T(8,128)S(1)}, f32[2,16,128]{2,1,0:T(8,128)S(1)}, u32[]{:S(2)}, u32[]{:S(2)}) collective-permute-start(f32[2,16,128]{2,1,0:T(8,128)S(1)} %shard_map.101), channel_id=1, source_target_pairs={{0,6},{2,4},{4,2},{6,0},{1,7},{3,5},{5,3},{7,1},{8,14},{10,12},{12... | collective-permute-start | bytes 49160 | tf_op jit(solution)/shard_map/ppermute | solution.py:192
  17.9 0.0 collective-permute-done.8.rest_1_
  17.9 1.8 %collective-permute-done.7.rest_0_ = f32[4,16,128]{2,1,0:T(8,128)S(1)} collective-permute-done((f32[4,16,128]{2,1,0:T(8,128)S(1)}, f32[4,16,128]{2,1,0:T(8,128)S(1)}, u32[]{:S(2)}, u32[]{:S(2)}) %collective-permute-start.7) | collective-permute-done | bytes 32800 | tf_op jit(solution)/shard_map/ppermute | solution.py:192
  19.7 0.0 collective-permute-done.5.near_ends
  19.7 0.5 %shard_map.100 = (f32[2,16,16,128]{3,2,1,0:T(8,128)S(1)}, f32[4,16,128]{2,1,0:T(8,128)S(1)}, f32[2,16,128]{2,1,0:T(8,128)S(1)}) custom-call(f32[2,16,16,128]{3,2,1,0:T(8,128)S(1)} %get-tuple-element.68.p, f32[2,16,16,128]{3,2,1,0:T(8,128)S(1)} %get-tuple-element.69.q, f32[2,16,16,128]{3,2,1,0:T(8,128)S(1)} %get-tuple-element.70.r, ...), custom_call_target="tpu_custom_call" | custom-call | flops 400000 | bytes 3096576 | tf_op jit(solution)/shard_map/pallas_call | solution.py:25
  20.2 1.8 %collective-permute-done.9.slopes = f32[2,16,128]{2,1,0:T(8,128)S(1)} collective-permute-done((f32[2,16,128]{2,1,0:T(8,128)S(1)}, f32[2,16,128]{2,1,0:T(8,128)S(1)}, u32[]{:S(2)}, u32[]{:S(2)}) %collective-permute-start.9) | collective-permute-done | bytes 16416 | tf_op jit(solution)/shard_map/ppermute | solution.py:192
  22.0 0.1 collective-permute-start.10
  22.0 1.5 %collective-permute-start.12 = (f32[2,16,128]{2,1,0:T(8,128)S(1)}, f32[2,16,128]{2,1,0:T(8,128)S(1)}, u32[]{:S(2)}, u32[]{:S(2)}) collective-permute-start(f32[2,16,128]{2,1,0:T(8,128)S(1)} %get-tuple-element.85), channel_id=1, source_target_pairs={{0,6},{2,4},{4,2},{6,0},{1,7},{3,5},{5,3},{7,1},{8,14},{10,12},{12... | collective-permute-start | bytes 49160 | tf_op jit(solution)/shard_map/ppermute | solution.py:192
  23.6 1.9 %collective-permute-start.11 = (f32[2,16,128]{2,1,0:T(8,128)S(1)}, f32[2,16,128]{2,1,0:T(8,128)S(1)}, u32[]{:S(2)}, u32[]{:S(2)}) collective-permute-start(f32[2,16,128]{2,1,0:T(8,128)S(1)} %get-tuple-element.85), channel_id=1, source_target_pairs={{0,4},{2,6},{4,0},{6,2},{1,5},{3,7},{5,1},{7,3},{8,12},{10,14},{12... | collective-permute-start | bytes 49160 | tf_op jit(solution)/shard_map/ppermute | solution.py:192
  25.5 0.3 %collective-permute-done.10.word = f32[2,16,128]{2,1,0:T(8,128)S(1)} collective-permute-done((f32[2,16,128]{2,1,0:T(8,128)S(1)}, f32[2,16,128]{2,1,0:T(8,128)S(1)}, u32[]{:S(2)}, u32[]{:S(2)}) %collective-permute-start.10) | collective-permute-done | bytes 16416 | tf_op jit(solution)/shard_map/ppermute | solution.py:192
  25.8 1.8 %collective-permute-done.12.rest_1_ = f32[2,16,128]{2,1,0:T(8,128)S(1)} collective-permute-done((f32[2,16,128]{2,1,0:T(8,128)S(1)}, f32[2,16,128]{2,1,0:T(8,128)S(1)}, u32[]{:S(2)}, u32[]{:S(2)}) %collective-permute-start.12) | collective-permute-done | bytes 16416 | tf_op jit(solution)/shard_map/ppermute | solution.py:192
  27.6 0.6 %collective-permute-done.11.rest_0_ = f32[2,16,128]{2,1,0:T(8,128)S(1)} collective-permute-done((f32[2,16,128]{2,1,0:T(8,128)S(1)}, f32[2,16,128]{2,1,0:T(8,128)S(1)}, u32[]{:S(2)}, u32[]{:S(2)}) %collective-permute-start.11) | collective-permute-done | bytes 16416 | tf_op jit(solution)/shard_map/ppermute | solution.py:192
  28.2 0.8 %shard_map.103 = (f32[256,128]{1,0:T(8,128)}, f32[256,128]{1,0:T(8,128)}) custom-call(f32[2,16,16,128]{3,2,1,0:T(8,128)S(1)} %get-tuple-element.81.p, f32[2,16,16,128]{3,2,1,0:T(8,128)S(1)} %get-tuple-element.82.q, f32[2,16,16,128]{3,2,1,0:T(8,128)S(1)} %get-tuple-element.83.r, f32[4,16,128]{2,1,0:T(8,128)S(1)} %get-tuple-element.84.ends, ...), custom_call_target="tpu_custom_call" | custom-call | flops 400000 | bytes 1015808 | tf_op jit(solution)/shard_map/pallas_call | solution.py:25
  (5 shorter events, 0.1 us)
Async XLA Ops:
  2.3 4.8 %collective-permute-start = (f32[2,16,128]{2,1,0:T(8,128)S(1)}, f32[2,16,128]{2,1,0:T(8,128)S(1)}, u32[]{:S(2)}, u32[]{:S(2)}) collective-permute-start(f32[2,16,128]{2,1,0:T(8,128)S(1)} %get-tuple-element.51.mine), channel_id=1, source_target_pairs={{0,1},{1,0},{2,3},{3,2},{4,5},{5,4},{6,7},{7,6},{8,9},{9,8},{10,11... | collective-permute-start | bytes 49160 | tf_op jit(solution)/shard_map/ppermute | solution.py:192
  7.0 6.7 %collective-permute-start.1 = (f32[3,16,128]{2,1,0:T(8,128)S(1)}, f32[3,16,128]{2,1,0:T(8,128)S(1)}, u32[]{:S(2)}, u32[]{:S(2)}) collective-permute-start(f32[3,16,128]{2,1,0:T(8,128)S(1)} %get-tuple-element.88), channel_id=1, source_target_pairs={{0,2},{2,0},{4,6},{6,4},{8,10},{10,8},{12,14},{14,12},{16,18},{18,... | collective-permute-start | bytes 73736 | tf_op jit(solution)/shard_map/ppermute | solution.py:512
  9.1 4.6 %collective-permute-start.2 = (f32[3,16,128]{2,1,0:T(8,128)S(1)}, f32[3,16,128]{2,1,0:T(8,128)S(1)}, u32[]{:S(2)}, u32[]{:S(2)}) collective-permute-start(f32[3,16,128]{2,1,0:T(8,128)S(1)} %get-tuple-element.89), channel_id=1, source_target_pairs={{0,8},{2,4},{4,2},{6,14},{8,0},{10,12},{12,10},{14,6},{16,24},{18,... | collective-permute-start | bytes 73736 | tf_op jit(solution)/shard_map/ppermute | solution.py:512
  9.1 4.7 %collective-permute-start.3 = (f32[4,2,16,128]{3,2,1,0:T(8,128)S(1)}, f32[4,2,16,128]{3,2,1,0:T(8,128)S(1)}, u32[]{:S(2)}, u32[]{:S(2)}) collective-permute-start(f32[4,2,16,128]{3,2,1,0:T(8,128)S(1)} %get-tuple-element.66.own), channel_id=1, source_target_pairs={{0,8},{8,0},{16,24},{24,16},{1,9},{9,1},{17,25},{25,17},{2,10},{10... | collective-permute-start | bytes 196616 | tf_op jit(solution)/shard_map/ppermute | solution.py:192
  9.6 6.7 %collective-permute-start.6 = (f32[4,2,16,128]{3,2,1,0:T(8,128)S(1)}, f32[4,2,16,128]{3,2,1,0:T(8,128)S(1)}, u32[]{:S(2)}, u32[]{:S(2)}) collective-permute-start(f32[4,2,16,128]{3,2,1,0:T(8,128)S(1)} %get-tuple-element.79.yown.own), channel_id=1, source_target_pairs={{0,2},{2,0},{4,6},{6,4},{1,3},{3,1},{5,7},{7,5},{8,10},{10,8},{12,... | collective-permute-start | bytes 196616 | tf_op jit(solution)/shard_map/ppermute | solution.py:192
  12.5 1.3 %collective-permute-start.4 = (f32[4,16,128]{2,1,0:T(8,128)S(1)}, f32[4,16,128]{2,1,0:T(8,128)S(1)}, u32[]{:S(2)}, u32[]{:S(2)}) collective-permute-start(f32[4,16,128]{2,1,0:T(8,128)S(1)} %get-tuple-element.67.gown), channel_id=1, source_target_pairs={{0,8},{8,0},{16,24},{24,16},{1,9},{9,1},{17,25},{25,17},{2,10},{10... | collective-permute-start | bytes 98312 | tf_op jit(solution)/shard_map/ppermute | solution.py:192
  14.1 5.6 %collective-permute-start.5 = (f32[5,16,128]{2,1,0:T(8,128)S(1)}, f32[5,16,128]{2,1,0:T(8,128)S(1)}, u32[]{:S(2)}, u32[]{:S(2)}) collective-permute-start(f32[5,16,128]{2,1,0:T(8,128)S(1)} %get-tuple-element.74.ends), channel_id=1, source_target_pairs={{0,8},{8,0},{16,24},{24,16},{1,9},{9,1},{17,25},{25,17},{2,10},{10... | collective-permute-start | bytes 122888 | tf_op jit(solution)/shard_map/ppermute | solution.py:192
  14.5 3.4 %collective-permute-start.8 = (f32[4,16,128]{2,1,0:T(8,128)S(1)}, f32[4,16,128]{2,1,0:T(8,128)S(1)}, u32[]{:S(2)}, u32[]{:S(2)}) collective-permute-start(f32[4,16,128]{2,1,0:T(8,128)S(1)} %get-tuple-element.80), channel_id=1, source_target_pairs={{0,24},{8,16},{16,8},{24,0},{1,25},{9,17},{17,9},{25,1},{2,26},{10... | collective-permute-start | bytes 98312 | tf_op jit(solution)/shard_map/ppermute | solution.py:192
  15.8 3.9 %collective-permute-start.7 = (f32[4,16,128]{2,1,0:T(8,128)S(1)}, f32[4,16,128]{2,1,0:T(8,128)S(1)}, u32[]{:S(2)}, u32[]{:S(2)}) collective-permute-start(f32[4,16,128]{2,1,0:T(8,128)S(1)} %get-tuple-element.80), channel_id=1, source_target_pairs={{0,16},{8,24},{16,0},{24,8},{1,17},{9,25},{17,1},{25,9},{2,18},{10... | collective-permute-start | bytes 98312 | tf_op jit(solution)/shard_map/ppermute | solution.py:192
  16.3 5.6 %collective-permute-start.9 = (f32[2,16,128]{2,1,0:T(8,128)S(1)}, f32[2,16,128]{2,1,0:T(8,128)S(1)}, u32[]{:S(2)}, u32[]{:S(2)}) collective-permute-start(f32[2,16,128]{2,1,0:T(8,128)S(1)} %shard_map.101), channel_id=1, source_target_pairs={{0,6},{2,4},{4,2},{6,0},{1,7},{3,5},{5,3},{7,1},{8,14},{10,12},{12... | collective-permute-start | bytes 49160 | tf_op jit(solution)/shard_map/ppermute | solution.py:192
  22.0 3.9 %collective-permute-start.10 = (f32[2,16,128]{2,1,0:T(8,128)S(1)}, f32[2,16,128]{2,1,0:T(8,128)S(1)}, u32[]{:S(2)}, u32[]{:S(2)}) collective-permute-start(f32[2,16,128]{2,1,0:T(8,128)S(1)} %shard_map.102), channel_id=1, source_target_pairs={{0,2},{2,0},{4,6},{6,4},{1,3},{3,1},{5,7},{7,5},{8,10},{10,8},{12,... | collective-permute-start | bytes 49160 | tf_op jit(solution)/shard_map/ppermute | solution.py:192
  22.0 5.6 %collective-permute-start.12 = (f32[2,16,128]{2,1,0:T(8,128)S(1)}, f32[2,16,128]{2,1,0:T(8,128)S(1)}, u32[]{:S(2)}, u32[]{:S(2)}) collective-permute-start(f32[2,16,128]{2,1,0:T(8,128)S(1)} %get-tuple-element.85), channel_id=1, source_target_pairs={{0,6},{2,4},{4,2},{6,0},{1,7},{3,5},{5,3},{7,1},{8,14},{10,12},{12... | collective-permute-start | bytes 49160 | tf_op jit(solution)/shard_map/ppermute | solution.py:192
  23.6 4.6 %collective-permute-start.11 = (f32[2,16,128]{2,1,0:T(8,128)S(1)}, f32[2,16,128]{2,1,0:T(8,128)S(1)}, u32[]{:S(2)}, u32[]{:S(2)}) collective-permute-start(f32[2,16,128]{2,1,0:T(8,128)S(1)} %get-tuple-element.85), channel_id=1, source_target_pairs={{0,4},{2,6},{4,0},{6,2},{1,5},{3,7},{5,1},{7,3},{8,12},{10,14},{12... | collective-permute-start | bytes 49160 | tf_op jit(solution)/shard_map/ppermute | solution.py:192

commit v7 on v6

--- a/solution.py
+++ b/solution.py
@@ -446,14 +446,14 @@
         return scan_values("gx", tuple(mine) + coefs, port_of)
 
     ghost_low, ghost_high = values(2)
+    beyond = [gp[k] + gq[k] * ghost_low + gr[k] * ghost_high for k in range(nx)]
     for f, ratio in enumerate(RATIOS):
         low, high = values(f)
         for k in range(nx):
             v = p[f, k] + q[f, k] * low + r[f, k] * high
-            beyond = gp[k] + gq[k] * ghost_low + gr[k] * ghost_high
             at = f * nz // 2
             out = 2.0 * v - d[f, k]
-            out = out + vertical_step(nz, v, beyond[:, at : at + 1], ratio * up[k], 0.5 * cz[k])
+            out = out + vertical_step(nz, v, beyond[k][:, at : at + 1], ratio * up[k], 0.5 * cz[k])
             if f == 0:
                 out = out + load[k]
             s[f, pl.ds(k * ny, ny), :] = out
@@ -545,7 +545,7 @@
     if paired[1]:
         ynear = swap(yown, "gy", 1)
         (yslopes,) = call(functools.partial(slope_kernel, "gy"), ((2,) + block_y,), yown, ynear)
-        yslopes = swap(yslopes, "gy", 3)
+        yslopes = swap(yslopes, "gy", 2)
     one, two = neighbours(
         jnp.concatenate([one, tiles[:1]]), jnp.concatenate([two, tiles[:1]])
     )

time: 29.1 us -> 29.9 us (1.027)
  waiting for transfers between devices: 7.62 us -> 8.11 us
  starting transfers between devices: 15.9 us -> 16.2 us
    ppermute x11, waiting for transfers between devices: 7.61 us -> 8.1 us  [swap(): lax.ppermute(value, axis, [(i, i ^ k) for i in range(lax.axis_size(axis))])]
where the time goes in v7:
time: 29.9 us; the launch traced here: 29.8 us
  starting transfers between devices  16.2 us (54%)
  waiting for transfers between devices  8.11 us (27%)
  Pallas kernels  4.79 us (16%)
  between operations  0.7 us (2%)
    ppermute x11, starting transfers between devices, swap(): lax.ppermute(value, axis, [(i, i ^ k) for i in range(lax.axis_size(axis))])  14.1 us
    ppermute x11, waiting for transfers between devices, swap(): lax.ppermute(value, axis, [(i, i ^ k) for i in range(lax.axis_size(axis))])  8.1 us
    pallas_call x9, Pallas kernels, run(): pl.pallas_call(kernel, out_shape=tuple((jax.ShapeDtypeStruct(s, F32) for...  4.79 us
    ppermute x2, starting transfers between devices, swapped(): return lax.ppermute(value, ('gx', 'gy'), pairs)  2.11 us
  transfers between devices with their start and end apart: 13, of which 6 were waited for; matrix products, arithmetic and copies ran while one was open for 0% of the time, Pallas kernels for 8%

profile of v7, /device:TPU:0, one launch (start us, length us, event | category | flops | bytes accessed | tf_op | source)
XLA Modules:
  0.0 29.8 jit_solution(2772940596676273882)
XLA Ops:
  0.6 1.6 %shard_map.95 = (f32[16,16,128]{2,1,0:T(8,128)S(1)}, f32[16,16,128]{2,1,0:T(8,128)S(1)}, f32[16,16,128]{2,1,0:T(8,128)S(1)}, f32[16,16,128]{2,1,0:T(8,128)S(1)},...) custom-call(f32[16,16,128]{2,1,0:T(8,128)} %refs_0_.1, ...), custom_call_target="tpu_custom_call" | custom-call | flops 400000 | bytes 1048576 | tf_op jit(solution)/shard_map/pallas_call | solution.py:25
  2.3 3.0 %collective-permute-start = (f32[2,16,128]{2,1,0:T(8,128)S(1)}, f32[2,16,128]{2,1,0:T(8,128)S(1)}, u32[]{:S(2)}, u32[]{:S(2)}) collective-permute-start(f32[2,16,128]{2,1,0:T(8,128)S(1)} %get-tuple-element.51.mine), channel_id=1, source_target_pairs={{0,1},{1,0},{2,3},{3,2},{4,5},{5,4},{6,7},{7,6},{8,9},{9,8},{10,11... | collective-permute-start | bytes 49160 | tf_op jit(solution)/shard_map/ppermute | solution.py:192
  5.3 0.4 %shard_map.96 = (f32[2,16,16,128]{3,2,1,0:T(8,128)S(1)}, f32[2,16,16,128]{3,2,1,0:T(8,128)S(1)}, f32[2,16,16,128]{3,2,1,0:T(8,128)S(1)}, f32[2,16,16,128]{3,2,1,...) custom-call(f32[256,128]{1,0:T(8,128)S(1)} %bitcast.9, ...), custom_call_target="tpu_custom_call" | custom-call | flops 400000 | bytes 655360 | tf_op jit(solution)/shard_map/pallas_call | solution.py:25
  5.7 1.3 %collective-permute-done.tiles = f32[2,16,128]{2,1,0:T(8,128)S(1)} collective-permute-done((f32[2,16,128]{2,1,0:T(8,128)S(1)}, f32[2,16,128]{2,1,0:T(8,128)S(1)}, u32[]{:S(2)}, u32[]{:S(2)}) %collective-permute-start) | collective-permute-done | bytes 16416 | tf_op jit(solution)/shard_map/ppermute | solution.py:192
  7.0 2.1 %collective-permute-start.1 = (f32[3,16,128]{2,1,0:T(8,128)S(1)}, f32[3,16,128]{2,1,0:T(8,128)S(1)}, u32[]{:S(2)}, u32[]{:S(2)}) collective-permute-start(f32[3,16,128]{2,1,0:T(8,128)S(1)} %get-tuple-element.88), channel_id=1, source_target_pairs={{0,2},{2,0},{4,6},{6,4},{8,10},{10,8},{12,14},{14,12},{16,18},{18,... | collective-permute-start | bytes 73736 | tf_op jit(solution)/shard_map/ppermute | solution.py:512
  9.1 0.0 collective-permute-start.2
  9.1 0.5 %collective-permute-start.3 = (f32[4,2,16,128]{3,2,1,0:T(8,128)S(1)}, f32[4,2,16,128]{3,2,1,0:T(8,128)S(1)}, u32[]{:S(2)}, u32[]{:S(2)}) collective-permute-start(f32[4,2,16,128]{3,2,1,0:T(8,128)S(1)} %get-tuple-element.66.own), channel_id=1, source_target_pairs={{0,8},{8,0},{16,24},{24,16},{1,9},{9,1},{17,25},{25,17},{2,10},{10... | collective-permute-start | bytes 196616 | tf_op jit(solution)/shard_map/ppermute | solution.py:192
  9.6 2.6 %collective-permute-start.6 = (f32[4,2,16,128]{3,2,1,0:T(8,128)S(1)}, f32[4,2,16,128]{3,2,1,0:T(8,128)S(1)}, u32[]{:S(2)}, u32[]{:S(2)}) collective-permute-start(f32[4,2,16,128]{3,2,1,0:T(8,128)S(1)} %get-tuple-element.79.yown.own), channel_id=1, source_target_pairs={{0,2},{2,0},{4,6},{6,4},{1,3},{3,1},{5,7},{7,5},{8,10},{10,8},{12,... | collective-permute-start | bytes 196616 | tf_op jit(solution)/shard_map/ppermute | solution.py:192
  12.3 0.2 shard_map.98
  12.5 0.3 collective-permute-start.4
  12.8 0.9 %shard_map.97 = (f32[2,16,16,128]{3,2,1,0:T(8,128)S(1)}, f32[2,16,16,128]{3,2,1,0:T(8,128)S(1)}, f32[16,16,128]{2,1,0:T(8,128)S(1)}, f32[16,16,128]{2,1,0:T(8,128)S(1)}) custom-call(f32[16,16,128]{2,1,0:T(8,128)S(1)} %get-tuple-element.45.t, f32[16,16,128]{2,1,0:T(8,128)S(1)} %get-tuple-element.46.h, f32[16,16,128]{2,1,0:T(8,128)S(1)} %get-tuple-element.53.load, ...), custom_call_target="tpu_custom_call" | custom-call | flops 400000 | bytes 950272 | tf_op jit(solution)/shard_map/pallas_call | solution.py:25
  13.8 0.0 collective-permute-done.1
  13.8 0.0 collective-permute-done.2
  13.8 0.0 collective-permute-done.4.gnear
  13.8 0.0 collective-permute-done.3.near
  13.8 0.3 shard_map.99
  14.1 0.3 %collective-permute-start.5 = (f32[5,16,128]{2,1,0:T(8,128)S(1)}, f32[5,16,128]{2,1,0:T(8,128)S(1)}, u32[]{:S(2)}, u32[]{:S(2)}) collective-permute-start(f32[5,16,128]{2,1,0:T(8,128)S(1)} %get-tuple-element.74.ends), channel_id=1, source_target_pairs={{0,8},{8,0},{16,24},{24,16},{1,9},{9,1},{17,25},{25,17},{2,10},{10... | collective-permute-start | bytes 122888 | tf_op jit(solution)/shard_map/ppermute | solution.py:192
  14.5 1.4 %collective-permute-start.8 = (f32[4,16,128]{2,1,0:T(8,128)S(1)}, f32[4,16,128]{2,1,0:T(8,128)S(1)}, u32[]{:S(2)}, u32[]{:S(2)}) collective-permute-start(f32[4,16,128]{2,1,0:T(8,128)S(1)} %get-tuple-element.80), channel_id=1, source_target_pairs={{0,24},{8,16},{16,8},{24,0},{1,25},{9,17},{17,9},{25,1},{2,26},{10... | collective-permute-start | bytes 98312 | tf_op jit(solution)/shard_map/ppermute | solution.py:192
  15.8 0.5 %collective-permute-start.7 = (f32[4,16,128]{2,1,0:T(8,128)S(1)}, f32[4,16,128]{2,1,0:T(8,128)S(1)}, u32[]{:S(2)}, u32[]{:S(2)}) collective-permute-start(f32[4,16,128]{2,1,0:T(8,128)S(1)} %get-tuple-element.80), channel_id=1, source_target_pairs={{0,16},{8,24},{16,0},{24,8},{1,17},{9,25},{17,1},{25,9},{2,18},{10... | collective-permute-start | bytes 98312 | tf_op jit(solution)/shard_map/ppermute | solution.py:192
  16.3 0.0 collective-permute-done.6.ynear.near
  16.3 1.8 %collective-permute-start.9 = (f32[2,16,128]{2,1,0:T(8,128)S(1)}, f32[2,16,128]{2,1,0:T(8,128)S(1)}, u32[]{:S(2)}, u32[]{:S(2)}) collective-permute-start(f32[2,16,128]{2,1,0:T(8,128)S(1)} %shard_map.101), channel_id=1, source_target_pairs={{0,4},{2,6},{4,0},{6,2},{1,5},{3,7},{5,1},{7,3},{8,12},{10,14},{12... | collective-permute-start | bytes 49160 | tf_op jit(solution)/shard_map/ppermute | solution.py:192
  18.2 0.0 collective-permute-done.8.rest_1_
  18.2 1.6 %collective-permute-done.7.rest_0_ = f32[4,16,128]{2,1,0:T(8,128)S(1)} collective-permute-done((f32[4,16,128]{2,1,0:T(8,128)S(1)}, f32[4,16,128]{2,1,0:T(8,128)S(1)}, u32[]{:S(2)}, u32[]{:S(2)}) %collective-permute-start.7) | collective-permute-done | bytes 32800 | tf_op jit(solution)/shard_map/ppermute | solution.py:192
  19.7 0.0 collective-permute-done.5.near_ends
  19.7 0.5 %shard_map.100 = (f32[2,16,16,128]{3,2,1,0:T(8,128)S(1)}, f32[4,16,128]{2,1,0:T(8,128)S(1)}, f32[2,16,128]{2,1,0:T(8,128)S(1)}) custom-call(f32[2,16,16,128]{3,2,1,0:T(8,128)S(1)} %get-tuple-element.68.p, f32[2,16,16,128]{3,2,1,0:T(8,128)S(1)} %get-tuple-element.69.q, f32[2,16,16,128]{3,2,1,0:T(8,128)S(1)} %get-tuple-element.70.r, ...), custom_call_target="tpu_custom_call" | custom-call | flops 400000 | bytes 3096576 | tf_op jit(solution)/shard_map/pallas_call | solution.py:25
  20.2 1.0 %collective-permute-done.9.slopes = f32[2,16,128]{2,1,0:T(8,128)S(1)} collective-permute-done((f32[2,16,128]{2,1,0:T(8,128)S(1)}, f32[2,16,128]{2,1,0:T(8,128)S(1)}, u32[]{:S(2)}, u32[]{:S(2)}) %collective-permute-start.9) | collective-permute-done | bytes 16416 | tf_op jit(solution)/shard_map/ppermute | solution.py:192
  21.2 0.5 %collective-permute-start.10 = (f32[2,16,128]{2,1,0:T(8,128)S(1)}, f32[2,16,128]{2,1,0:T(8,128)S(1)}, u32[]{:S(2)}, u32[]{:S(2)}) collective-permute-start(f32[2,16,128]{2,1,0:T(8,128)S(1)} %shard_map.102), channel_id=1, source_target_pairs={{0,2},{2,0},{4,6},{6,4},{1,3},{3,1},{5,7},{7,5},{8,10},{10,8},{12,... | collective-permute-start | bytes 49160 | tf_op jit(solution)/shard_map/ppermute | solution.py:192
  21.6 2.7 %collective-permute-start.12 = (f32[2,16,128]{2,1,0:T(8,128)S(1)}, f32[2,16,128]{2,1,0:T(8,128)S(1)}, u32[]{:S(2)}, u32[]{:S(2)}) collective-permute-start(f32[2,16,128]{2,1,0:T(8,128)S(1)} %get-tuple-element.85), channel_id=1, source_target_pairs={{0,6},{2,4},{4,2},{6,0},{1,7},{3,5},{5,3},{7,1},{8,14},{10,12},{12... | collective-permute-start | bytes 49160 | tf_op jit(solution)/shard_map/ppermute | solution.py:192
  24.4 0.4 %collective-permute-start.11 = (f32[2,16,128]{2,1,0:T(8,128)S(1)}, f32[2,16,128]{2,1,0:T(8,128)S(1)}, u32[]{:S(2)}, u32[]{:S(2)}) collective-permute-start(f32[2,16,128]{2,1,0:T(8,128)S(1)} %get-tuple-element.85), channel_id=1, source_target_pairs={{0,4},{2,6},{4,0},{6,2},{1,5},{3,7},{5,1},{7,3},{8,12},{10,14},{12... | collective-permute-start | bytes 49160 | tf_op jit(solution)/shard_map/ppermute | solution.py:192
  24.7 0.2 collective-permute-done.10.word
  25.0 2.2 %collective-permute-done.12.rest_1_ = f32[2,16,128]{2,1,0:T(8,128)S(1)} collective-permute-done((f32[2,16,128]{2,1,0:T(8,128)S(1)}, f32[2,16,128]{2,1,0:T(8,128)S(1)}, u32[]{:S(2)}, u32[]{:S(2)}) %collective-permute-start.12) | collective-permute-done | bytes 16416 | tf_op jit(solution)/shard_map/ppermute | solution.py:192
  27.2 1.8 %collective-permute-done.11.rest_0_ = f32[2,16,128]{2,1,0:T(8,128)S(1)} collective-permute-done((f32[2,16,128]{2,1,0:T(8,128)S(1)}, f32[2,16,128]{2,1,0:T(8,128)S(1)}, u32[]{:S(2)}, u32[]{:S(2)}) %collective-permute-start.11) | collective-permute-done | bytes 16416 | tf_op jit(solution)/shard_map/ppermute | solution.py:192
  29.0 0.8 %shard_map.103 = (f32[256,128]{1,0:T(8,128)}, f32[256,128]{1,0:T(8,128)}) custom-call(f32[2,16,16,128]{3,2,1,0:T(8,128)S(1)} %get-tuple-element.81.p, f32[2,16,16,128]{3,2,1,0:T(8,128)S(1)} %get-tuple-element.82.q, f32[2,16,16,128]{3,2,1,0:T(8,128)S(1)} %get-tuple-element.83.r, f32[4,16,128]{2,1,0:T(8,128)S(1)} %get-tuple-element.84.ends, ...), custom_call_target="tpu_custom_call" | custom-call | flops 400000 | bytes 1015808 | tf_op jit(solution)/shard_map/pallas_call | solution.py:25
  (5 shorter events, 0.1 us)
Async XLA Ops:
  2.3 4.8 %collective-permute-start = (f32[2,16,128]{2,1,0:T(8,128)S(1)}, f32[2,16,128]{2,1,0:T(8,128)S(1)}, u32[]{:S(2)}, u32[]{:S(2)}) collective-permute-start(f32[2,16,128]{2,1,0:T(8,128)S(1)} %get-tuple-element.51.mine), channel_id=1, source_target_pairs={{0,1},{1,0},{2,3},{3,2},{4,5},{5,4},{6,7},{7,6},{8,9},{9,8},{10,11... | collective-permute-start | bytes 49160 | tf_op jit(solution)/shard_map/ppermute | solution.py:192
  7.0 6.7 %collective-permute-start.1 = (f32[3,16,128]{2,1,0:T(8,128)S(1)}, f32[3,16,128]{2,1,0:T(8,128)S(1)}, u32[]{:S(2)}, u32[]{:S(2)}) collective-permute-start(f32[3,16,128]{2,1,0:T(8,128)S(1)} %get-tuple-element.88), channel_id=1, source_target_pairs={{0,2},{2,0},{4,6},{6,4},{8,10},{10,8},{12,14},{14,12},{16,18},{18,... | collective-permute-start | bytes 73736 | tf_op jit(solution)/shard_map/ppermute | solution.py:512
  9.1 4.6 %collective-permute-start.2 = (f32[3,16,128]{2,1,0:T(8,128)S(1)}, f32[3,16,128]{2,1,0:T(8,128)S(1)}, u32[]{:S(2)}, u32[]{:S(2)}) collective-permute-start(f32[3,16,128]{2,1,0:T(8,128)S(1)} %get-tuple-element.89), channel_id=1, source_target_pairs={{0,8},{2,4},{4,2},{6,14},{8,0},{10,12},{12,10},{14,6},{16,24},{18,... | collective-permute-start | bytes 73736 | tf_op jit(solution)/shard_map/ppermute | solution.py:512
  9.1 4.7 %collective-permute-start.3 = (f32[4,2,16,128]{3,2,1,0:T(8,128)S(1)}, f32[4,2,16,128]{3,2,1,0:T(8,128)S(1)}, u32[]{:S(2)}, u32[]{:S(2)}) collective-permute-start(f32[4,2,16,128]{3,2,1,0:T(8,128)S(1)} %get-tuple-element.66.own), channel_id=1, source_target_pairs={{0,8},{8,0},{16,24},{24,16},{1,9},{9,1},{17,25},{25,17},{2,10},{10... | collective-permute-start | bytes 196616 | tf_op jit(solution)/shard_map/ppermute | solution.py:192
  9.6 6.7 %collective-permute-start.6 = (f32[4,2,16,128]{3,2,1,0:T(8,128)S(1)}, f32[4,2,16,128]{3,2,1,0:T(8,128)S(1)}, u32[]{:S(2)}, u32[]{:S(2)}) collective-permute-start(f32[4,2,16,128]{3,2,1,0:T(8,128)S(1)} %get-tuple-element.79.yown.own), channel_id=1, source_target_pairs={{0,2},{2,0},{4,6},{6,4},{1,3},{3,1},{5,7},{7,5},{8,10},{10,8},{12,... | collective-permute-start | bytes 196616 | tf_op jit(solution)/shard_map/ppermute | solution.py:192
  12.5 1.3 %collective-permute-start.4 = (f32[4,16,128]{2,1,0:T(8,128)S(1)}, f32[4,16,128]{2,1,0:T(8,128)S(1)}, u32[]{:S(2)}, u32[]{:S(2)}) collective-permute-start(f32[4,16,128]{2,1,0:T(8,128)S(1)} %get-tuple-element.67.gown), channel_id=1, source_target_pairs={{0,8},{8,0},{16,24},{24,16},{1,9},{9,1},{17,25},{25,17},{2,10},{10... | collective-permute-start | bytes 98312 | tf_op jit(solution)/shard_map/ppermute | solution.py:192
  14.1 5.6 %collective-permute-start.5 = (f32[5,16,128]{2,1,0:T(8,128)S(1)}, f32[5,16,128]{2,1,0:T(8,128)S(1)}, u32[]{:S(2)}, u32[]{:S(2)}) collective-permute-start(f32[5,16,128]{2,1,0:T(8,128)S(1)} %get-tuple-element.74.ends), channel_id=1, source_target_pairs={{0,8},{8,0},{16,24},{24,16},{1,9},{9,1},{17,25},{25,17},{2,10},{10... | collective-permute-start | bytes 122888 | tf_op jit(solution)/shard_map/ppermute | solution.py:192
  14.5 3.7 %collective-permute-start.8 = (f32[4,16,128]{2,1,0:T(8,128)S(1)}, f32[4,16,128]{2,1,0:T(8,128)S(1)}, u32[]{:S(2)}, u32[]{:S(2)}) collective-permute-start(f32[4,16,128]{2,1,0:T(8,128)S(1)} %get-tuple-element.80), channel_id=1, source_target_pairs={{0,24},{8,16},{16,8},{24,0},{1,25},{9,17},{17,9},{25,1},{2,26},{10... | collective-permute-start | bytes 98312 | tf_op jit(solution)/shard_map/ppermute | solution.py:192
  15.8 3.9 %collective-permute-start.7 = (f32[4,16,128]{2,1,0:T(8,128)S(1)}, f32[4,16,128]{2,1,0:T(8,128)S(1)}, u32[]{:S(2)}, u32[]{:S(2)}) collective-permute-start(f32[4,16,128]{2,1,0:T(8,128)S(1)} %get-tuple-element.80), channel_id=1, source_target_pairs={{0,16},{8,24},{16,0},{24,8},{1,17},{9,25},{17,1},{25,9},{2,18},{10... | collective-permute-start | bytes 98312 | tf_op jit(solution)/shard_map/ppermute | solution.py:192
  16.3 4.8 %collective-permute-start.9 = (f32[2,16,128]{2,1,0:T(8,128)S(1)}, f32[2,16,128]{2,1,0:T(8,128)S(1)}, u32[]{:S(2)}, u32[]{:S(2)}) collective-permute-start(f32[2,16,128]{2,1,0:T(8,128)S(1)} %shard_map.101), channel_id=1, source_target_pairs={{0,4},{2,6},{4,0},{6,2},{1,5},{3,7},{5,1},{7,3},{8,12},{10,14},{12... | collective-permute-start | bytes 49160 | tf_op jit(solution)/shard_map/ppermute | solution.py:192
  21.2 3.8 %collective-permute-start.10 = (f32[2,16,128]{2,1,0:T(8,128)S(1)}, f32[2,16,128]{2,1,0:T(8,128)S(1)}, u32[]{:S(2)}, u32[]{:S(2)}) collective-permute-start(f32[2,16,128]{2,1,0:T(8,128)S(1)} %shard_map.102), channel_id=1, source_target_pairs={{0,2},{2,0},{4,6},{6,4},{1,3},{3,1},{5,7},{7,5},{8,10},{10,8},{12,... | collective-permute-start | bytes 49160 | tf_op jit(solution)/shard_map/ppermute | solution.py:192
  21.6 5.5 %collective-permute-start.12 = (f32[2,16,128]{2,1,0:T(8,128)S(1)}, f32[2,16,128]{2,1,0:T(8,128)S(1)}, u32[]{:S(2)}, u32[]{:S(2)}) collective-permute-start(f32[2,16,128]{2,1,0:T(8,128)S(1)} %get-tuple-element.85), channel_id=1, source_target_pairs={{0,6},{2,4},{4,2},{6,0},{1,7},{3,5},{5,3},{7,1},{8,14},{10,12},{12... | collective-permute-start | bytes 49160 | tf_op jit(solution)/shard_map/ppermute | solution.py:192
  24.4 4.6 %collective-permute-start.11 = (f32[2,16,128]{2,1,0:T(8,128)S(1)}, f32[2,16,128]{2,1,0:T(8,128)S(1)}, u32[]{:S(2)}, u32[]{:S(2)}) collective-permute-start(f32[2,16,128]{2,1,0:T(8,128)S(1)} %get-tuple-element.85), channel_id=1, source_target_pairs={{0,4},{2,6},{4,0},{6,2},{1,5},{3,7},{5,1},{7,3},{8,12},{10,14},{12... | collective-permute-start | bytes 49160 | tf_op jit(solution)/shard_map/ppermute | solution.py:192
